TPU v7x, 256 devices: a whole 4x4x8 slice. The times are simulated.
256 devices in a mesh: req: 2 (over core), row: 32 (over x, z), col: 4 (over y).
Axes of the slice: x: 4, y: 4, z: 8, core: 2. Of those that a mesh axis runs over, the one named last changes fastest.
Arguments:
- hidden: bfloat16 [2, 3072, 3072], P('req', 'row'), may hold values from -6 to 6
- text_hidden: bfloat16 [2, 128, 3072], P('req', 'row'), may hold values from -6 to 6
- text_len: int32 [2], replicated, may hold values from 32 to 128, as said below
- grid: int32 [2, 2], replicated, may hold values from 8 to 32, as said below
- timestep: int32 [2], replicated, may hold values from 250 to 999
- modulation: float32 [2, 8, 3072], P('req'), may hold values from -4 to 4
- q_gain: float32 [64], replicated, may hold values from 1 to 3
- k_gain: float32 [64], replicated, may hold values from 1 to 3
- w_qkv: bfloat16 [3, 3072, 3072], P(None, 'row', 'col'), may hold values from -0.109375 to 0.109375
- w_out: bfloat16 [3072, 3072], P('col'), may hold values from -0.109375 to 0.109375
- w_up: bfloat16 [3072, 12288], P(None, 'row'), may hold values from -0.109375 to 0.109375
- w_down: bfloat16 [12288, 3072], P('row'), may hold values from -0.0546875 to 0.0546875
- w_proj: bfloat16 [3072, 64], replicated, may hold values from -0.109375 to 0.109375
- latent: float32 [2, 3072, 64], P('req', ('row', 'col')), may hold values from -6 to 6
- conv_w: bfloat16 [3, 3, 16, 512], replicated, may hold values from -0.5 to 0.5
Outputs:
- hidden_out: bfloat16 [2, 3072, 3072], P('req', ('row', 'col'))
- new_latent: float32 [2, 3072, 64], P('req', ('row', 'col'))
- decoded: bfloat16 [2, 6, 64, 32, 512], P('req', None, 'row', 'col')
Inputs may be any that keep to these rules, and one draw needn't show every extreme that they name: Each request's live token rows and columns; one of the two requests, drawn, fills its whole grid of 32 rows and 16 columns, the other keeps at least half of each. `text_len`: one of the two requests, drawn, has all 128 text tokens live. The previous timestep of the sampling step is timestep - 250.
All inputs are finite; a program needn't handle non-finite values.
Results may differ from a plain program's by a relative error of at most 0.014.
Values may be sent and summed in bfloat16 or wider, within the bound.
A program may use at most 128 MiB of HBM per device.

v0:
```python
import jax
import jax.numpy as jnp
from jax import lax
from jax.sharding import PartitionSpec as P

CH = 16
FR = 6
TR = 1
TC = 4
TRAIN_STEPS = 1000
STRIDE = 250


latent_scale = 0.7


def extended(cells, sides, width):
    for axis, dim in sides:
        count = lax.axis_size(axis)
        ends = count - 1
        head = lax.slice_in_dim(cells, 0, width, axis=dim)
        tail = lax.slice_in_dim(cells, cells.shape[dim] - width, cells.shape[dim], axis=dim)
        cells = jnp.concatenate(
            [
                lax.ppermute(tail, axis, [(i, (i + 1) % count) for i in range(ends)]),
                cells,
                lax.ppermute(head, axis, [((i + 1) % count, i) for i in range(ends)]),
            ],
            axis=dim,
        )
    return cells


def layer_norm(tensor, epsilon):
    average = jnp.mean(tensor, axis=-1, keepdims=True)
    centered = tensor - average
    spread = jnp.mean(centered * centered, axis=-1, keepdims=True)
    return centered * lax.rsqrt(spread + epsilon)


def modulate(tensor, offset, factor):
    return (layer_norm(tensor, 1e-05) * (1.0 + factor) + offset).astype(jnp.bfloat16)


def head_norm(tensor, scaling):
    return (layer_norm(tensor, 1e-06) * scaling).astype(jnp.bfloat16)


def pick_entry(entries, position):
    slot_ids = jnp.arange(entries.shape[0], dtype=jnp.int32)
    return jnp.sum(jnp.where(slot_ids == position, entries, jnp.zeros_like(entries)))


def solver_weights(step_index):
    plan = jnp.linspace(0.00085**0.5, 0.012**0.5, TRAIN_STEPS, dtype=jnp.float32) ** 2
    cumulative = jnp.cumprod(1.0 - plan)
    alpha_now = pick_entry(cumulative, step_index)
    alpha_prev = pick_entry(cumulative, step_index - STRIDE)
    root_now = jnp.sqrt(alpha_now)
    rest_now = jnp.sqrt(1.0 - alpha_now)
    root_prev = jnp.sqrt(alpha_prev)
    rest_prev = jnp.sqrt(1.0 - alpha_prev)
    return (
        root_prev * root_now + rest_prev * rest_now,
        rest_prev * root_now - root_prev * rest_now,
    )


def key_mask(count, owners, grid, text_len, span, block_tokens, tile, text_rows):
    positions = jnp.arange(count, dtype=jnp.int32)
    owner_row = positions // span
    within = positions % span
    is_video = within < block_tokens
    owner_col = within // tile
    local_ids = within % tile
    token_row = owner_row * TR + local_ids // TC % TR
    token_col = owner_col * TC + local_ids % TC
    text_index = owner_row * text_rows + within - block_tokens
    matches = jnp.arange(grid.shape[0], dtype=jnp.int32)[None, :] == owners[:, None]
    rows_live = jnp.sum(jnp.where(matches, grid[None, :, 0], 0), axis=1)
    cols_live = jnp.sum(jnp.where(matches, grid[None, :, 1], 0), axis=1)
    text_lens = jnp.sum(jnp.where(matches, text_len[None, :], 0), axis=1)
    video_live = (token_row[None, :] < rows_live[:, None]) & (
        token_col[None, :] < cols_live[:, None]
    )
    text_live = text_index[None, :] < text_lens[:, None]
    return jnp.where(is_video[None, :], video_live, text_live).astype(jnp.float32)


def projector(stacked, piece):
    return jnp.einsum("gld,cde->cgle", stacked, piece, preferred_element_type=jnp.float32)


def attention_step(queries, owners, grid, text_len, span, block_tokens, tile, text_rows):
    score_scale = queries.shape[3] ** (-0.5)

    def attend(carry, pieces, start):
        key_piece, value_piece = pieces
        live_keys = key_mask(
            key_piece.shape[1], owners, grid, text_len, span, block_tokens, tile, text_rows
        )
        scores = (
            jnp.einsum("gqhd,gkhd->gqhk", queries, key_piece, preferred_element_type=jnp.float32)
            * score_scale
        )
        raw_weights = jnp.exp(scores) * live_keys[:, None, None, :]
        weighted = jnp.einsum(
            "gqhk,gkhd->gqhd",
            raw_weights.astype(jnp.bfloat16),
            value_piece,
            preferred_element_type=jnp.float32,
        )
        return (weighted, jnp.sum(raw_weights, axis=3))

    return attend


def shards(
    hidden,
    text_hidden,
    text_len,
    grid,
    timestep,
    modulation,
    q_gain,
    k_gain,
    w_qkv,
    w_out,
    w_up,
    w_down,
    w_proj,
    latent,
    conv_w,
):
    col_count = lax.axis_size("col")
    request_id = lax.axis_index("req")
    row_id = lax.axis_index("row")
    col_id = lax.axis_index("col")
    block_tokens = hidden.shape[1]
    tile = block_tokens // col_count
    text_rows = text_hidden.shape[1]
    head_dim = q_gain.shape[0]
    adaptive = modulation[0]
    source = hidden[0].astype(jnp.float32)
    joined = jnp.concatenate(
        [
            modulate(source, adaptive[0], adaptive[1]),
            modulate(text_hidden[0].astype(jnp.float32), adaptive[0], adaptive[1]),
        ],
        axis=0,
    )
    span = joined.shape[0]
    stacked = joined[None]
    owners = jnp.reshape(request_id, (1,))
    qkv = projector(stacked, lax.all_gather(w_qkv, "row", axis=1, tiled=True))
    groups = stacked.shape[0]
    heads_here = qkv.shape[3] // head_dim
    shaped = qkv.reshape(3, groups, span, heads_here, head_dim)
    queries = head_norm(shaped[0, :, :block_tokens], q_gain)
    key_block = head_norm(shaped[1], k_gain)
    value_block = shaped[2].astype(jnp.bfloat16)
    attend = attention_step(queries, owners, grid, text_len, span, block_tokens, tile, text_rows)
    empty_state = (jnp.zeros(queries.shape, jnp.float32), jnp.zeros(queries.shape[:3], jnp.float32))
    weighted, totals = attend(
        empty_state,
        (
            lax.all_gather(key_block, "row", axis=1, tiled=True),
            lax.all_gather(value_block, "row", axis=1, tiled=True),
        ),
        jnp.int32(0),
    )
    attended = (
        (weighted / totals[..., None])
        .astype(jnp.bfloat16)
        .reshape(groups * block_tokens, heads_here * head_dim)
    )
    partial_out = jnp.dot(attended, w_out, preferred_element_type=jnp.float32)
    projected = lax.psum_scatter(partial_out, "col", scatter_dimension=0, tiled=True)
    own_rows = lax.dynamic_slice_in_dim(source, col_id * tile, tile, 0)
    mixed = lax.optimization_barrier(
        (own_rows + adaptive[2] * projected).astype(jnp.bfloat16)
    ).astype(jnp.float32)
    second_norm = modulate(mixed, adaptive[3], adaptive[4])
    hidden_units = jax.nn.gelu(
        jnp.dot(
            lax.all_gather(second_norm, "row", axis=0, tiled=True),
            w_up,
            preferred_element_type=jnp.float32,
        ),
        approximate=True,
    ).astype(jnp.bfloat16)
    feed_terms = jnp.dot(hidden_units, w_down, preferred_element_type=jnp.float32)
    feed_out = lax.psum_scatter(
        feed_terms.astype(jnp.bfloat16), "row", scatter_dimension=0, tiled=True
    ).astype(jnp.float32)
    out_hidden = (mixed + adaptive[5] * feed_out).astype(jnp.bfloat16)
    final_norm = modulate(out_hidden.astype(jnp.float32), adaptive[6], adaptive[7])
    velocity = jnp.dot(final_norm, w_proj, preferred_element_type=jnp.float32)
    local_ids = jnp.arange(tile, dtype=jnp.int32)
    token_row = row_id * TR + local_ids // TC % TR
    token_col = col_id * TC + local_ids % TC
    rows_live = pick_entry(grid[:, 0], request_id)
    cols_live = pick_entry(grid[:, 1], request_id)
    live_tokens = ((token_row < rows_live) & (token_col < cols_live)).astype(jnp.float32)
    keep_part, velocity_part = solver_weights(pick_entry(timestep, request_id))
    updated = (keep_part * latent[0] + velocity_part * velocity) * live_tokens[:, None]
    pixels = (
        updated.reshape(FR, TR, TC, CH, 2, 2)
        .transpose(0, 1, 4, 2, 5, 3)
        .reshape(FR, 2 * TR, 2 * TC, CH)
    )
    scaled = (pixels / latent_scale).astype(jnp.bfloat16)
    padded = extended(scaled, (("row", 1), ("col", 2)), 1)
    running = jnp.zeros((FR, 2 * TR, 2 * TC, conv_w.shape[3]), jnp.float32)
    for row_tap in range(3):
        for col_tap in range(3):
            window = padded[:, row_tap : row_tap + 2 * TR, col_tap : col_tap + 2 * TC, :]
            running = running + jnp.einsum(
                "fyxc,cd->fyxd",
                window,
                conv_w[row_tap, col_tap],
                preferred_element_type=jnp.float32,
            )
    return (out_hidden[None], updated[None], running.astype(jnp.bfloat16)[None])


def solution(mesh):
    placed = (
        P("req", "row", None),
        P("req", "row", None),
        P(),
        P(),
        P(),
        P("req", None, None),
        P(),
        P(),
        P(None, "row", "col"),
        P("col", None),
        P(None, "row"),
        P("row", None),
        P(),
        P("req", ("row", "col"), None),
        P(),
    )
    return jax.shard_map(
        shards,
        mesh=mesh,
        in_specs=placed,
        out_specs=(
            P("req", ("row", "col"), None),
            P("req", ("row", "col"), None),
            P("req", None, "row", "col", None),
        ),
        check_vma=False,
    )
```

profile of v0, /device:TPU:2, one launch (start us, length us, event | category | flops | bytes accessed | tf_op | source)
XLA Modules:
  0.0 793.3 jit_solution(17732168062341165365)
XLA Ops:
  7.2 0.7 all-gather.5.cloned.1.call-update
  8.0 1.0 convert_reduce_fusion.3
  8.9 0.9 fusion.79
  9.9 1.2 convert_reduce_fusion
  11.1 1.4 multiply_reduce_fusion
  12.6 2.2 slice_add_fusion
  14.8 1.4 fusion.82
  16.2 0.3 add_convert_fusion
  16.5 123.0 %all-gather.5.cloned.1.call-done = bf16[3,3072,768]{2,1,0:T(8,128)(2,1)} async-done(((bf16[3,96,768]{2,1,0:T(8,128)(2,1)}), bf16[3,3072,768]{2,1,0:T(8,128)(2,1)}) %all-gather.5.cloned.1.call-update) | async-done | bytes 14155792 | tf_op jit(solution)/shard_map/all_gather | solution.py:155
  139.5 7.3 convolution_bitcast_fusion
  146.8 1.0 copy-done.2
  147.8 0.7 slice.173
  148.5 1.2 copy.31
  149.8 0.8 multiply_convert_fusion
  150.6 1.1 copy.33
  151.8 1.0 slice.227
  152.8 0.2 copy.28
  153.0 1.1 copy.29
  154.1 0.2 reduce-scatter.3.cloned.1.call-start
  154.3 1.3 select_reduce_fusion.5
  155.6 0.2 slice_reduce_fusion.3
  155.8 0.7 fusion.165
  156.5 2.0 fusion.160
  158.6 2.6 copy.35
  161.2 1.1 slice_reduce_fusion
  162.2 1.1 fusion.49
  163.4 107.8 %all-gather.9.cloned.1.call-done = bf16[1,3200,12,64]{3,2,0,1:T(8,128)(2,1)} async-done(((bf16[1,100,12,64]{3,2,0,1:T(8,128)(2,1)}), bf16[1,3200,12,64]{3,2,0,1:T(8,128)(2,1)}) %all-gather.9.cloned.1.call-update) | async-done | bytes 4915216 | tf_op jit(solution)/shard_map/all_gather | solution.py:167
  271.2 14.5 %copy.34 = bf16[1,3200,12,64]{1,3,2,0:T(8,128)(2,1)} copy(bf16[1,3200,12,64]{3,2,0,1:T(8,128)(2,1)} %all-gather.9.cloned.1.call-done) | data formatting | bytes 9830400 | tf_op jit(solution)/shard_map/all_gather | solution.py:167
  285.7 10.5 %bitcast_reduce_fusion = (f32[96,12]{0,1:T(8,128)S(1)}, f32[12,3200,96]{1,2,0:T(8,128)}) fusion(f32[3200]{0:T(1024)S(1)} %fusion.160, f32[3,1,100,12,64]{2,4,3,0,1:T(8,128)} %bitcast.217, f32[64]{0:T(128)S(1)} %copy-done.11, f32[96,12]{0,1:T(8,128)S(1)} %add_rsqrt_fusion, f32[96,12]{0,1:T(8,128)S(1)} %broadcast_multiply_fusion, bf16[1,3200,12,64]{1,3,2,0:T(8,128)(2,1)} %copy.34), kind=kOutput, calls=%fused_computation | convolution fusion | flops 483212160 | bytes 20080896 | tf_op jit(solution)/shard_map/gqhd,gkhd->gqhk/dot_general | solution.py:103
  296.2 96.9 %all-gather.7.cloned.1.call-done = bf16[1,3200,12,64]{3,2,0,1:T(8,128)(2,1)} async-done(((bf16[1,100,12,64]{3,2,0,1:T(8,128)(2,1)}), bf16[1,3200,12,64]{3,2,0,1:T(8,128)(2,1)}) %all-gather.7.cloned.1.call-update) | async-done | bytes 4915216 | tf_op jit(solution)/shard_map/all_gather | solution.py:168
  393.1 14.5 %copy.30 = bf16[1,3200,12,64]{1,3,2,0:T(8,128)(2,1)} copy(bf16[1,3200,12,64]{3,2,0,1:T(8,128)(2,1)} %all-gather.7.cloned.1.call-done) | data formatting | bytes 9830400 | tf_op jit(solution)/shard_map/all_gather | solution.py:168
  407.6 9.8 %fusion.36 = bf16[1,96,12,64]{1,3,2,0:T(8,128)(2,1)S(1)} fusion(f32[12,3200,96]{1,2,0:T(8,128)} %get-tuple-element.22, f32[3200]{0:T(1024)S(1)} %fusion.160, bf16[1,3200,12,64]{1,3,2,0:T(8,128)(2,1)} %copy.30, f32[96,12]{0,1:T(8,128)S(1)} %get-tuple-element.21), kind=kOutput, calls=%fused_computation.39 | convolution fusion | flops 483065856 | bytes 19825664 | tf_op jit(solution)/shard_map/gqhk,gkhd->gqhd/dot_general | solution.py:107
  417.4 4.3 fusion.186
  421.8 1.1 convert_element_type.114
  422.9 24.1 %reduce-scatter.3.cloned.1.call-done = f32[24,3072]{1,0:T(8,128)} async-done(((f32[96,3072]{1,0:T(8,128)}), f32[24,3072]{1,0:T(8,128)}) %reduce-scatter.3.cloned.1.call-update) | async-done | bytes 294928 | tf_op jit(solution)/shard_map/reduce_scatter | solution.py:178
  447.0 1.1 fusion.66
  448.2 0.2 fusion.57
  448.5 0.8 fusion.60
  449.3 0.3 reduce-scatter.5.cloned.1.call-start
  449.6 82.6 %all-gather.11.cloned.1.call-done = bf16[768,3072]{1,0:T(8,128)(2,1)} async-done(((bf16[24,3072]{1,0:T(8,128)(2,1)}), bf16[768,3072]{1,0:T(8,128)(2,1)}) %all-gather.11.cloned.1.call-update) | async-done | bytes 4718608 | tf_op jit(solution)/shard_map/all_gather | solution.py:186
  532.2 10.4 %convolution_convert_fusion = bf16[768,3072]{1,0:T(8,128)(2,1)} fusion(bf16[384,3072]{1,0:T(8,128)(2,1)S(1)} %copy-done, bf16[768,3072]{1,0:T(8,128)(2,1)} %all-gather.11.cloned.1.call-done, bf16[3072,384]{1,0:T(8,128)(2,1)} %param.25), kind=kOutput, calls=%fused_computation.7 | convolution fusion | flops 3628892160 | bytes 14155776 | tf_op jit(solution)/shard_map/dot_general | solution.py:192
  542.7 0.3 reduce-window.9
  543.2 0.6 select_reduce_fusion.3
  544.7 1.3 select_reduce_fusion
  549.3 0.6 select_reduce_fusion.2
  549.9 0.7 and_convert_fusion
  550.6 213.1 %reduce-scatter.5.cloned.1.call-done = bf16[24,3072]{1,0:T(8,128)(2,1)} async-done(((bf16[768,3072]{1,0:T(8,128)(2,1)}), bf16[24,3072]{1,0:T(8,128)(2,1)}) %reduce-scatter.5.cloned.1.call-update) | async-done | bytes 147472 | tf_op jit(solution)/shard_map/reduce_scatter | solution.py:193
  763.7 1.1 convert_reduce_fusion.2
  764.8 0.2 fusion.61
  765.1 0.9 multiply_convert_fusion.1
  766.2 0.3 copy.37
  766.5 2.8 collective-permute-start
  769.2 5.2 collective-permute-start.1
  774.6 1.2 collective-permute-done.1
  775.8 3.4 collective-permute-start.2
  779.2 1.3 collective-permute-start.3
  780.7 0.1 fusion.83
  780.8 4.0 collective-permute-done.3
  784.8 0.1 fusion.110
  785.0 0.2 fusion.91
  785.1 0.1 fusion.102
  785.3 0.2 fusion.93
  785.4 0.2 fusion.26
  785.6 0.8 fusion.28
  (68 shorter events, 1.7 us)
Async XLA Ops:
  7.2 525.0 %copy-start = (bf16[384,3072]{1,0:T(8,128)(2,1)S(1)}, bf16[384,3072]{1,0:T(8,128)(2,1)}, u32[]{:S(2)}) copy-start(bf16[384,3072]{1,0:T(8,128)(2,1)} %param.26) | copy-start | bytes 7077892
  7.2 9.0 %copy-start.1 = (bf16[1,96,3072]{2,1,0:T(8,128)(2,1)S(1)}, bf16[1,96,3072]{2,1,0:T(8,128)(2,1)}, u32[]{:S(2)}) copy-start(bf16[1,96,3072]{2,1,0:T(8,128)(2,1)} %param.15) | copy-start | bytes 1769476
  7.2 132.3 %all-gather.5.cloned.1.call-start = ((), (), s32[]{:S(2)}) async-start(), calls=%async_computation.2 | async-start | bytes 14598144 | tf_op jit(solution)/shard_map/all_gather | solution.py:155
  7.9 263.3 %all-gather.9.cloned.1.call-start = ((), (), s32[]{:S(2)}) async-start(), calls=%async_computation.4 | async-start | bytes 13516800 | tf_op jit(solution)/shard_map/all_gather | solution.py:167
  146.8 1.0 copy-start.2
  148.5 7.1 copy-start.10
  151.8 241.4 %all-gather.7.cloned.1.call-start = ((), (), s32[]{:S(2)}) async-start(), calls=%async_computation.3 | async-start | bytes 13516800 | tf_op jit(solution)/shard_map/all_gather | solution.py:168
  154.1 292.9 %reduce-scatter.3.cloned.1.call-start = ((), (), s32[]{:S(2)}) async-start(), calls=%async_computation.5 | async-start | bytes 1474560 | tf_op jit(solution)/shard_map/reduce_scatter | solution.py:178
  163.4 122.4 %copy-start.11 = (f32[64]{0:T(128)S(1)}, f32[64]{0:T(128)}, u32[]{:S(2)}) copy-start(f32[64]{0:T(128)} %param.21) | copy-start | bytes 772
  421.7 25.2 %copy-start.7 = (f32[1,1,3072]{2,1,0:T(1,128)S(1)}, f32[1,1,3072]{2,1,0:T(1,128)}, u32[]{:S(2)}) copy-start(f32[1,1,3072]{2,1,0:T(1,128)} %get-tuple-element.15) | copy-start | bytes 36868
  421.8 26.7 %copy-start.5 = (f32[1,1,3072]{2,1,0:T(1,128)S(1)}, f32[1,1,3072]{2,1,0:T(1,128)}, u32[]{:S(2)}) copy-start(f32[1,1,3072]{2,1,0:T(1,128)} %get-tuple-element.11) | copy-start | bytes 36868
  421.8 110.4 %all-gather.11.cloned.1.call-start = ((), (), s32[]{:S(2)}) async-start(), calls=%async_computation.6 | async-start | bytes 4866048 | tf_op jit(solution)/shard_map/all_gather | solution.py:186
  449.3 314.4 %reduce-scatter.5.cloned.1.call-start = ((), (), s32[]{:S(2)}) async-start(), calls=%async_computation.7 | async-start | bytes 4866048 | tf_op jit(solution)/shard_map/reduce_scatter | solution.py:193
  542.5 0.7 copy-start.12
  542.5 221.2 %copy-start.6 = (f32[1,1,3072]{2,1,0:T(1,128)S(1)}, f32[1,1,3072]{2,1,0:T(1,128)}, u32[]{:S(2)}) copy-start(f32[1,1,3072]{2,1,0:T(1,128)} %get-tuple-element.12) | copy-start | bytes 36868
  542.5 222.5 %copy-start.8 = (f32[1,1,3072]{2,1,0:T(1,128)S(1)}, f32[1,1,3072]{2,1,0:T(1,128)}, u32[]{:S(2)}) copy-start(f32[1,1,3072]{2,1,0:T(1,128)} %get-tuple-element.9) | copy-start | bytes 36868
  542.5 222.5 %copy-start.9 = (f32[1,1,3072]{2,1,0:T(1,128)S(1)}, f32[1,1,3072]{2,1,0:T(1,128)}, u32[]{:S(2)}) copy-start(f32[1,1,3072]{2,1,0:T(1,128)} %get-tuple-element.16) | copy-start | bytes 36868
  542.6 222.5 %copy-start.13 = (bf16[3072,64]{0,1:T(8,128)(2,1)S(1)}, bf16[3072,64]{0,1:T(8,128)(2,1)}, u32[]{:S(2)}) copy-start(bf16[3072,64]{0,1:T(8,128)(2,1)} %param.27) | copy-start | bytes 1179652
  542.6 222.5 %copy-start.14 = (f32[1,24,64]{2,1,0:T(8,128)S(1)}, f32[1,24,64]{2,1,0:T(8,128)}, u32[]{:S(2)}) copy-start(f32[1,24,64]{2,1,0:T(8,128)} %param.28) | copy-start | bytes 18436
  542.6 231.8 %copy-start.4 = (bf16[3,3,16,512]{3,2,1,0:T(8,128)(2,1)S(1)}, bf16[3,3,16,512]{3,2,1,0:T(8,128)(2,1)}, u32[]{:S(2)}) copy-start(bf16[3,3,16,512]{3,2,1,0:T(8,128)(2,1)} %param.29) | copy-start | bytes 442372
  764.8 21.6 %copy-start.3 = (bf16[24,3072]{1,0:T(8,128)(2,1)}, bf16[24,3072]{1,0:T(8,128)(2,1)S(1)}, u32[]{:S(2)}) copy-start(bf16[24,3072]{1,0:T(8,128)(2,1)S(1)} %get-tuple-element.8) | copy-start | bytes 442372
  766.5 8.1 %collective-permute-start = (bf16[6,1,8,16]{3,2,1,0:T(8,128)(2,1)S(1)}, bf16[6,1,8,16]{3,2,1,0:T(8,128)(2,1)S(1)}, u32[]{:S(2)}, u32[]{:S(2)}) collective-permute-start(bf16[6,1,8,16]{3,2,1,0:T(8,128)(2,1)S(1)} %get-tuple-element.19), channel_id=1, source_target_pairs={{0,4},{4,8},{8,12},{12,16},{16,20},{20,24},{24,28},{28,32},{32,36}... | collective-permute-start | bytes 4616 | tf_op jit(solution)/shard_map/ppermute | solution.py:25
  769.2 6.6 collective-permute-start.1
  775.8 9.3 %collective-permute-start.2 = (bf16[6,4,1,16]{3,2,1,0:T(2,128)(2,1)S(1)}, bf16[6,4,1,16]{3,2,1,0:T(2,128)(2,1)S(1)}, u32[]{:S(2)}, u32[]{:S(2)}) collective-permute-start(bf16[6,4,1,16]{3,2,1,0:T(2,128)(2,1)S(1)} %get-tuple-element.17), channel_id=1, source_target_pairs={{0,1},{1,2},{2,3},{4,5},{5,6},{6,7},{8,9},{9,10},{10,11},{12,13},{... | collective-permute-start | bytes 2312 | tf_op jit(solution)/shard_map/ppermute | solution.py:25
  779.2 5.6 collective-permute-start.3
Sparse Core Ops, SparseCore 0:
  10.6 128.8 all-gather.4
  151.9 119.2 all-gather.8
  273.8 119.2 all-gather.6
  421.9 25.0 reduce-scatter.2
  450.0 82.1 all-gather.10
  542.7 220.9 reduce-scatter.4
where the time goes:
time: 795 us; the launch traced here: 793 us
  waiting for transfers between devices  654 us (82%)
  matrix products  45.2 us (6%)
  local copies, waits for them, and re-layouts  38.9 us (5%)
  other arithmetic  23.9 us (3%)
  between operations  18.4 us (2%)
  starting transfers between devices  13.3 us (2%)
    reduce_scatter x1, waiting for transfers between devices, shards(): lax.psum_scatter(feed_terms.astype(jnp.bfloat16), 'row', scatter_dimensio...  213 us
    all_gather x1, waiting for transfers between devices, shards(): qkv = projector(stacked, lax.all_gather(w_qkv, 'row', axis=1, tiled=True))  123 us
    all_gather x1, waiting for transfers between devices, shards(): lax.all_gather(key_block, 'row', axis=1, tiled=True)  108 us
    all_gather x1, waiting for transfers between devices, shards(): lax.all_gather(value_block, 'row', axis=1, tiled=True)  96.9 us
    all_gather x1, waiting for transfers between devices, shards(): lax.all_gather(second_norm, 'row', axis=0, tiled=True)  82.6 us
    reduce_scatter x1, waiting for transfers between devices, shards(): lax.psum_scatter(partial_out, 'col', scatter_dimension=0, tiled=True)  24.1 us
  transfers between devices with their start and end apart: 10, of which 8 were waited for; matrix products, arithmetic and copies ran while one was open for 6% of the time, Pallas kernels for 0%

commit v1 on v0

--- a/solution.py
+++ b/solution.py
@@ -152,7 +152,10 @@
     span = joined.shape[0]
     stacked = joined[None]
     owners = jnp.reshape(request_id, (1,))
-    qkv = projector(stacked, lax.all_gather(w_qkv, "row", axis=1, tiled=True))
+    half_cols = w_qkv.shape[2] // 2
+    own_half = lax.dynamic_slice_in_dim(w_qkv, request_id * half_cols, half_cols, 2)
+    gathered_half = lax.all_gather(own_half, "row", axis=1, tiled=True)
+    qkv = projector(stacked, lax.all_gather(gathered_half, "req", axis=2, tiled=True))
     groups = stacked.shape[0]
     heads_here = qkv.shape[3] // head_dim
     shaped = qkv.reshape(3, groups, span, heads_here, head_dim)
@@ -161,12 +164,12 @@
     value_block = shaped[2].astype(jnp.bfloat16)
     attend = attention_step(queries, owners, grid, text_len, span, block_tokens, tile, text_rows)
     empty_state = (jnp.zeros(queries.shape, jnp.float32), jnp.zeros(queries.shape[:3], jnp.float32))
+    both = jnp.stack([key_block[0], value_block[0]], axis=0)[None]
+    both = lax.all_gather(both, "row", axis=0, tiled=True)
+    both = jnp.swapaxes(both, 0, 1).reshape(2, 1, -1, heads_here, head_dim)
     weighted, totals = attend(
         empty_state,
-        (
-            lax.all_gather(key_block, "row", axis=1, tiled=True),
-            lax.all_gather(value_block, "row", axis=1, tiled=True),
-        ),
+        (both[0], both[1]),
         jnp.int32(0),
     )
     attended = (

time: 795 us -> 707 us (0.89)
  waiting for transfers between devices: 654 us -> 564 us
  local copies, waits for them, and re-layouts: 38.9 us -> 50.3 us
    all_gather x3, waiting for transfers between devices: 328 us -> 237 us  [the longest x1 113 us: shards(): both = lax.all_gather(both, 'row', axis=0, tiled=True)]
    another operation x2 -> x4, local copies, waits for them, and re-layouts: 0.12 us -> 26 us
    all_gather x2 -> x1, local copies, waits for them, and re-layouts: 29 us -> 11.9 us  [shards(): both = lax.all_gather(both, 'row', axis=0, tiled=True)]
  transfers between devices with their start and end apart: 10 -> 10, of which waited for: 8 -> 8; matrix products, arithmetic and copies ran while one was open for 6% -> 2% of each run, Pallas kernels for 0% -> 0%
where the time goes in v1:
time: 707 us; the launch traced here: 705 us
  waiting for transfers between devices  564 us (80%)
  local copies, waits for them, and re-layouts  50.3 us (7%)
  matrix products  43.7 us (6%)
  between operations  18.5 us (3%)
  other arithmetic  16 us (2%)
  starting transfers between devices  12.7 us (2%)
    reduce_scatter x1, waiting for transfers between devices, shards(): lax.psum_scatter(feed_terms.astype(jnp.bfloat16), 'row', scatter_dimensio...  213 us
    all_gather x1, waiting for transfers between devices, shards(): both = lax.all_gather(both, 'row', axis=0, tiled=True)  113 us
    all_gather x1, waiting for transfers between devices, shards(): gathered_half = lax.all_gather(own_half, 'row', axis=1, tiled=True)  95.3 us
    all_gather x1, waiting for transfers between devices, shards(): lax.all_gather(second_norm, 'row', axis=0, tiled=True)  82.8 us
    all_gather x1, waiting for transfers between devices, shards(): lax.all_gather(gathered_half, 'req', axis=2, tiled=True)  28.7 us
    another operation x4, local copies, waits for them, and re-layouts  26 us
    reduce_scatter x1, waiting for transfers between devices, shards(): lax.psum_scatter(partial_out, 'col', scatter_dimension=0, tiled=True)  24 us
  transfers between devices with their start and end apart: 10, of which 8 were waited for; matrix products, arithmetic and copies ran while one was open for 2% of the time, Pallas kernels for 0%

profile of v1, /device:TPU:2, one launch (start us, length us, event | category | flops | bytes accessed | tf_op | source)
XLA Modules:
  0.0 705.3 jit_solution(1297304816965305826)
XLA Ops:
  7.2 1.8 constant_dynamic-slice_fusion
  9.1 95.3 %all-gather.6.cloned.1.call-done = bf16[3,3072,384]{2,1,0:T(8,128)(2,1)} async-done(((bf16[3,96,384]{2,1,0:T(8,128)(2,1)}), bf16[3,3072,384]{2,1,0:T(8,128)(2,1)}) %all-gather.6.cloned.1.call-update) | async-done | bytes 7077904 | tf_op jit(solution)/shard_map/all_gather | solution.py:157
  104.4 0.7 copy-done.6
  105.1 0.1 convert_reduce_fusion.3
  105.2 0.2 fusion.71
  105.4 0.2 convert_reduce_fusion
  105.6 0.3 multiply_reduce_fusion
  106.0 0.7 slice_add_fusion
  106.7 0.7 fusion.74
  107.4 0.3 add_convert_fusion
  107.7 28.7 %all-gather.8.cloned.1.call-done = bf16[3,3072,768]{2,1,0:T(8,128)(2,1)} async-done(((bf16[3,3072,384]{2,1,0:T(8,128)(2,1)}), bf16[3,3072,768]{2,1,0:T(8,128)(2,1)}) %all-gather.8.cloned.1.call-update) | async-done | bytes 14155792 | tf_op jit(solution)/shard_map/all_gather | solution.py:158
  136.4 7.0 convolution_bitcast_fusion
  143.5 0.9 copy-done.4
  144.4 0.2 copy.30
  144.6 0.2 copy.28
  145.1 0.8 pad_maximum_fusion
  146.0 0.6 select_reduce_fusion.5
  146.6 0.2 slice_reduce_fusion.3
  146.8 0.7 fusion.157
  147.5 2.0 fusion.152
  149.5 1.6 copy.32
  151.2 0.7 copy-done.9
  152.0 0.6 add_rsqrt_fusion
  152.6 113.2 %all-gather.12.cloned.1.call-done = bf16[64,100,12,64]{1,3,2,0:T(8,128)(2,1)} async-done(((bf16[2,100,12,64]{1,3,2,0:T(8,128)(2,1)}), bf16[64,100,12,64]{1,3,2,0:T(8,128)(2,1)}) %all-gather.12.cloned.1.call-update) | async-done | bytes 9830416 | tf_op jit(solution)/shard_map/all_gather | solution.py:168
  265.8 11.9 %copy.45 = bf16[32,2,100,12,64]{2,0,4,3,1:T(8,128)(2,1)S(1)} copy(bf16[32,2,100,12,64]{2,4,3,1,0:T(8,128)(2,1)} %bitcast.213) | data formatting | bytes 19660800 | tf_op jit(solution)/shard_map/all_gather | solution.py:168
  277.6 5.5 fusion.175
  283.1 12.9 %reshape.413 = bf16[3200,12,64]{0,2,1:T(8,128)(2,1)} reshape(bf16[1,32,100,12,64]{2,1,4,3,0:T(8,128)(2,1)} %get-tuple-element.10) | data formatting | bytes 9830400 | tf_op jit(solution)/shard_map/reshape.45
  296.0 13.0 %reshape.414 = bf16[3200,12,64]{0,2,1:T(8,128)(2,1)} reshape(bf16[1,32,100,12,64]{2,1,4,3,0:T(8,128)(2,1)} %get-tuple-element.9) | data formatting | bytes 9830400 | tf_op jit(solution)/shard_map/reshape.37
  309.0 10.7 %bitcast_reduce_fusion = (f32[96,12]{0,1:T(8,128)S(1)}, f32[12,3200,96]{1,2,0:T(8,128)}) fusion(f32[3200]{0:T(1024)S(1)} %fusion.152, bf16[3200,12,64]{0,2,1:T(8,128)(2,1)} %reshape.414, f32[3,1,100,12,64]{2,4,3,0,1:T(8,128)} %bitcast.219, f32[64]{0:T(128)S(1)} %copy-done.23, f32[96,12]{0,1:T(8,128)S(1)} %copy-done.15, f32[96,12]{0,1:T(8,128)S(1)} %copy-done.10), kind=kOutput, calls=%fused_computation | convolution fusion | flops 483212160 | bytes 20080896 | tf_op jit(solution)/shard_map/gqhd,gkhd->gqhk/dot_general | solution.py:103
  319.7 8.3 %fusion.29 = bf16[1,96,12,64]{1,3,2,0:T(8,128)(2,1)S(1)} fusion(bf16[3200,12,64]{0,2,1:T(8,128)(2,1)S(1)} %bitcast.212, f32[12,3200,96]{1,2,0:T(8,128)} %get-tuple-element.24, f32[3200]{0:T(1024)S(1)} %fusion.152, f32[96,12]{0,1:T(8,128)S(1)} %get-tuple-element.23), kind=kOutput, calls=%fused_computation.37 | convolution fusion | flops 483065856 | bytes 19825664 | tf_op jit(solution)/shard_map/gqhk,gkhd->gqhd/dot_general | solution.py:107
  328.0 4.4 fusion.179
  332.5 1.1 convert_element_type.114
  333.6 24.0 %reduce-scatter.3.cloned.1.call-done = f32[24,3072]{1,0:T(8,128)} async-done(((f32[96,3072]{1,0:T(8,128)}), f32[24,3072]{1,0:T(8,128)}) %reduce-scatter.3.cloned.1.call-update) | async-done | bytes 294928 | tf_op jit(solution)/shard_map/reduce_scatter | solution.py:181
  357.6 1.1 fusion.57
  358.8 0.2 fusion.48
  359.1 0.8 fusion.51
  359.9 0.3 reduce-scatter.5.cloned.1.call-start
  360.2 82.8 %all-gather.10.cloned.1.call-done = bf16[768,3072]{1,0:T(8,128)(2,1)} async-done(((bf16[24,3072]{1,0:T(8,128)(2,1)}), bf16[768,3072]{1,0:T(8,128)(2,1)}) %all-gather.10.cloned.1.call-update) | async-done | bytes 4718608 | tf_op jit(solution)/shard_map/all_gather | solution.py:189
  442.9 10.4 %convolution_convert_fusion = bf16[768,3072]{1,0:T(8,128)(2,1)} fusion(bf16[384,3072]{1,0:T(8,128)(2,1)S(1)} %copy-done, bf16[768,3072]{1,0:T(8,128)(2,1)} %all-gather.10.cloned.1.call-done, bf16[3072,384]{1,0:T(8,128)(2,1)} %param.25), kind=kOutput, calls=%fused_computation.8 | convolution fusion | flops 3628892160 | bytes 14155776 | tf_op jit(solution)/shard_map/dot_general | solution.py:195
  453.5 0.3 reduce-window.9
  454.0 0.6 select_reduce_fusion.3
  455.5 1.3 select_reduce_fusion
  460.0 0.6 select_reduce_fusion.2
  460.6 0.7 and_convert_fusion
  461.2 213.4 %reduce-scatter.5.cloned.1.call-done = bf16[24,3072]{1,0:T(8,128)(2,1)} async-done(((bf16[768,3072]{1,0:T(8,128)(2,1)}), bf16[24,3072]{1,0:T(8,128)(2,1)}) %reduce-scatter.5.cloned.1.call-update) | async-done | bytes 147472 | tf_op jit(solution)/shard_map/reduce_scatter | solution.py:196
  674.6 1.1 convert_reduce_fusion.2
  675.7 0.2 fusion.52
  676.0 0.9 multiply_convert_fusion.1
  677.1 0.3 copy.34
  677.4 4.5 collective-permute-start.1
  681.9 1.9 collective-permute-start
  683.8 0.1 fusion.126
  684.0 5.6 collective-permute-done
  689.6 1.3 collective-permute-start.3
  690.9 4.5 collective-permute-start.2
  695.4 0.1 fusion.79
  695.6 0.2 fusion.75
  695.7 1.1 collective-permute-done.2
  696.8 0.1 fusion.85
  697.0 0.2 fusion.94
  697.1 0.1 fusion.83
  697.3 0.2 fusion.102
  697.4 0.2 fusion.21
  697.6 0.8 fusion.23
  (103 shorter events, 1.7 us)
Async XLA Ops:
  7.2 435.8 %copy-start = (bf16[384,3072]{1,0:T(8,128)(2,1)S(1)}, bf16[384,3072]{1,0:T(8,128)(2,1)}, u32[]{:S(2)}) copy-start(bf16[384,3072]{1,0:T(8,128)(2,1)} %param.26) | copy-start | bytes 7077892
  7.2 97.2 %all-gather.6.cloned.1.call-start = ((), (), s32[]{:S(2)}) async-start(), calls=%async_computation.2 | async-start | bytes 7299072 | tf_op jit(solution)/shard_map/all_gather | solution.py:157
  9.0 127.3 %all-gather.8.cloned.1.call-start = ((), (), s32[]{:S(2)}) async-start(), calls=%async_computation.3 | async-start | bytes 21233664 | tf_op jit(solution)/shard_map/all_gather | solution.py:158
  104.4 0.7 copy-start.6
  104.4 1.1 copy-start.1
  104.4 1.6 copy-start.8
  104.4 161.4 %all-gather.12.cloned.1.call-start = ((), (), s32[]{:S(2)}) async-start(), calls=%async_computation.7 | async-start | bytes 12976128 | tf_op jit(solution)/shard_map/all_gather | solution.py:168
  143.4 1.0 copy-start.4
  143.4 1.5 copy-start.25
  143.4 2.6 copy-start.28
  143.4 3.2 copy-start.20
  145.9 211.7 %reduce-scatter.3.cloned.1.call-start = ((), (), s32[]{:S(2)}) async-start(), calls=%async_computation.4 | async-start | bytes 1474560 | tf_op jit(solution)/shard_map/reduce_scatter | solution.py:181
  146.8 0.7 copy-start.18
  146.8 0.7 copy-start.21
  151.1 126.5 %copy-start.3 = (f32[3,1,100,768]{2,3,0,1:T(8,128)}, f32[3,1,100,768]{2,3,0,1:T(8,128)S(1)}, u32[]{:S(2)}) copy-start(f32[3,1,100,768]{2,3,0,1:T(8,128)S(1)} %copy.32) | copy-start | bytes 2764804
  151.2 0.7 copy-start.9
  296.0 13.0 %copy-start.10 = (f32[96,12]{0,1:T(8,128)S(1)}, f32[96,12]{0,1:T(8,128)}, u32[]{:S(2)}) copy-start(f32[96,12]{0,1:T(8,128)} %copy-done.9) | copy-start | bytes 13828
  296.0 13.0 %copy-start.15 = (f32[96,12]{0,1:T(8,128)S(1)}, f32[96,12]{0,1:T(8,128)}, u32[]{:S(2)}) copy-start(f32[96,12]{0,1:T(8,128)} %add_rsqrt_fusion) | copy-start | bytes 13828
  296.0 13.0 %copy-start.23 = (f32[64]{0:T(128)S(1)}, f32[64]{0:T(128)}, u32[]{:S(2)}) copy-start(f32[64]{0:T(128)} %param.21) | copy-start | bytes 772
  296.0 23.6 %slice-start = ((s8[4915200]{0:T(1024)(128)(4,1)}), s8[720896]{0:T(1024)(128)(4,1)S(1)}, s32[]{:S(2)}) async-start(s8[4915200]{0:T(1024)(128)(4,1)} %bitcast.211), calls=%async_computation.8 | async-start | bytes 1441792
  309.0 10.7 %slice-start.1 = ((s8[4915200]{0:T(1024)(128)(4,1)}), s8[4194304]{0:T(1024)(128)(4,1)S(1)}, s32[]{:S(2)}) async-start(s8[4915200]{0:T(1024)(128)(4,1)} %bitcast.211), calls=%async_computation.9 | async-start | bytes 8388608
  328.0 4.5 copy-start.2
  332.4 25.2 %copy-start.14 = (f32[1,1,3072]{2,1,0:T(1,128)S(1)}, f32[1,1,3072]{2,1,0:T(1,128)}, u32[]{:S(2)}) copy-start(f32[1,1,3072]{2,1,0:T(1,128)} %get-tuple-element.17) | copy-start | bytes 36868
  332.4 26.7 %copy-start.11 = (f32[1,1,3072]{2,1,0:T(1,128)S(1)}, f32[1,1,3072]{2,1,0:T(1,128)}, u32[]{:S(2)}) copy-start(f32[1,1,3072]{2,1,0:T(1,128)} %get-tuple-element.12) | copy-start | bytes 36868
  332.4 26.7 %copy-start.12 = (f32[1,1,3072]{2,1,0:T(1,128)S(1)}, f32[1,1,3072]{2,1,0:T(1,128)}, u32[]{:S(2)}) copy-start(f32[1,1,3072]{2,1,0:T(1,128)} %get-tuple-element.13) | copy-start | bytes 36868
  332.4 110.5 %all-gather.10.cloned.1.call-start = ((), (), s32[]{:S(2)}) async-start(), calls=%async_computation.5 | async-start | bytes 4866048 | tf_op jit(solution)/shard_map/all_gather | solution.py:189
  359.9 314.7 %reduce-scatter.5.cloned.1.call-start = ((), (), s32[]{:S(2)}) async-start(), calls=%async_computation.6 | async-start | bytes 4866048 | tf_op jit(solution)/shard_map/reduce_scatter | solution.py:196
  453.3 0.7 copy-start.19
  453.3 0.7 copy-start.24
  453.3 6.6 copy-start.22
  453.3 221.3 %copy-start.13 = (f32[1,1,3072]{2,1,0:T(1,128)S(1)}, f32[1,1,3072]{2,1,0:T(1,128)}, u32[]{:S(2)}) copy-start(f32[1,1,3072]{2,1,0:T(1,128)} %get-tuple-element.14) | copy-start | bytes 36868
  453.3 222.6 %copy-start.16 = (f32[1,1,3072]{2,1,0:T(1,128)S(1)}, f32[1,1,3072]{2,1,0:T(1,128)}, u32[]{:S(2)}) copy-start(f32[1,1,3072]{2,1,0:T(1,128)} %get-tuple-element.11) | copy-start | bytes 36868
  453.3 222.6 %copy-start.17 = (f32[1,1,3072]{2,1,0:T(1,128)S(1)}, f32[1,1,3072]{2,1,0:T(1,128)}, u32[]{:S(2)}) copy-start(f32[1,1,3072]{2,1,0:T(1,128)} %get-tuple-element.18) | copy-start | bytes 36868
  453.3 222.6 %copy-start.26 = (bf16[3072,64]{0,1:T(8,128)(2,1)S(1)}, bf16[3072,64]{0,1:T(8,128)(2,1)}, u32[]{:S(2)}) copy-start(bf16[3072,64]{0,1:T(8,128)(2,1)} %param.27) | copy-start | bytes 1179652
  453.4 222.6 %copy-start.27 = (f32[1,24,64]{2,1,0:T(8,128)S(1)}, f32[1,24,64]{2,1,0:T(8,128)}, u32[]{:S(2)}) copy-start(f32[1,24,64]{2,1,0:T(8,128)} %param.28) | copy-start | bytes 18436
  453.4 230.4 %copy-start.7 = (bf16[3,3,16,512]{3,2,1,0:T(8,128)(2,1)S(1)}, bf16[3,3,16,512]{3,2,1,0:T(8,128)(2,1)}, u32[]{:S(2)}) copy-start(bf16[3,3,16,512]{3,2,1,0:T(8,128)(2,1)} %param.29) | copy-start | bytes 442372
  675.7 22.7 %copy-start.5 = (bf16[24,3072]{1,0:T(8,128)(2,1)}, bf16[24,3072]{1,0:T(8,128)(2,1)S(1)}, u32[]{:S(2)}) copy-start(bf16[24,3072]{1,0:T(8,128)(2,1)S(1)} %get-tuple-element.8) | copy-start | bytes 442372
  677.4 6.6 collective-permute-start.1
  681.9 7.7 %collective-permute-start = (bf16[6,1,8,16]{3,2,1,0:T(8,128)(2,1)S(1)}, bf16[6,1,8,16]{3,2,1,0:T(8,128)(2,1)S(1)}, u32[]{:S(2)}, u32[]{:S(2)}) collective-permute-start(bf16[6,1,8,16]{3,2,1,0:T(8,128)(2,1)S(1)} %get-tuple-element.21), channel_id=1, source_target_pairs={{0,4},{4,8},{8,12},{12,16},{16,20},{20,24},{24,28},{28,32},{32,36}... | collective-permute-start | bytes 4616 | tf_op jit(solution)/shard_map/ppermute | solution.py:25
  689.6 7.5 %collective-permute-start.3 = (bf16[6,4,1,16]{3,2,1,0:T(2,128)(2,1)S(1)}, bf16[6,4,1,16]{3,2,1,0:T(2,128)(2,1)S(1)}, u32[]{:S(2)}, u32[]{:S(2)}) collective-permute-start(bf16[6,4,1,16]{3,2,1,0:T(2,128)(2,1)S(1)} %get-tuple-element.20), channel_id=1, source_target_pairs={{1,0},{2,1},{3,2},{5,4},{6,5},{7,6},{9,8},{10,9},{11,10},{13,12},{... | collective-permute-start | bytes 2312 | tf_op jit(solution)/shard_map/ppermute | solution.py:27
  690.9 5.9 collective-permute-start.2
Sparse Core Ops, SparseCore 0:
  10.6 93.6 all-gather.5
  106.2 30.1 all-gather.7
  146.0 119.6 all-gather.11
  332.6 24.9 reduce-scatter.2
  360.6 82.2 all-gather.9
  453.5 221.0 reduce-scatter.4

commit v2 on v1

--- a/solution.py
+++ b/solution.py
@@ -1,7 +1,13 @@
+import functools
+
 import jax
 import jax.numpy as jnp
 from jax import lax
 from jax.sharding import PartitionSpec as P
+from jax.experimental import pallas as pl
+from jax.experimental.pallas import tpu as pltpu
+
+MESH_IDS = pl.DeviceIdType.MESH
 
 CH = 16
 FR = 6
@@ -29,6 +35,70 @@
             axis=dim,
         )
     return cells
+
+
+def scatter_sum_kernel(count, rows, part_ref, out_ref, landed, send_sems, recv_sems, own_sem):
+    me = lax.axis_index("row")
+    req = lax.axis_index("req")
+    col = lax.axis_index("col")
+    barrier = pltpu.get_barrier_semaphore()
+    for step in range(1, count):
+        peer = lax.rem(me + step, count)
+        pl.semaphore_signal(barrier, inc=1, device_id=(req, peer, col), device_id_type=MESH_IDS)
+    pl.semaphore_wait(barrier, count - 1)
+    own = pltpu.make_async_copy(part_ref.at[pl.ds(me * rows, rows)], landed.at[me], own_sem)
+    own.start()
+    sends = []
+    for step in range(1, count):
+        peer = lax.rem(me + step, count)
+        copy = pltpu.make_async_remote_copy(
+            src_ref=part_ref.at[pl.ds(peer * rows, rows)],
+            dst_ref=landed.at[me],
+            send_sem=send_sems.at[step],
+            recv_sem=recv_sems.at[step],
+            device_id=(req, peer, col),
+            device_id_type=MESH_IDS,
+        )
+        copy.start()
+        sends.append(copy)
+    own.wait()
+    for step in range(1, count):
+        source = lax.rem(me + count - step, count)
+        pltpu.make_async_remote_copy(
+            src_ref=part_ref.at[pl.ds(me * rows, rows)],
+            dst_ref=landed.at[source],
+            send_sem=send_sems.at[step],
+            recv_sem=recv_sems.at[step],
+            device_id=(req, source, col),
+            device_id_type=MESH_IDS,
+        ).wait_recv()
+    for copy in sends:
+        copy.wait_send()
+    total = landed[0].astype(jnp.float32)
+    for slot in range(1, count):
+        total = total + landed[slot].astype(jnp.float32)
+    out_ref[...] = total
+
+
+def row_scatter_sum(part):
+    count = lax.axis_size("row")
+    rows = part.shape[0] // count
+    width = part.shape[1]
+    return pl.pallas_call(
+        functools.partial(scatter_sum_kernel, count, rows),
+        out_shape=jax.ShapeDtypeStruct((rows, width), jnp.float32),
+        in_specs=[pl.BlockSpec(memory_space=pl.ANY)],
+        out_specs=pl.BlockSpec(memory_space=pltpu.VMEM),
+        scratch_shapes=[
+            pltpu.VMEM((count, rows, width), part.dtype),
+            pltpu.SemaphoreType.DMA((count,)),
+            pltpu.SemaphoreType.DMA((count,)),
+            pltpu.SemaphoreType.DMA(()),
+        ],
+        compiler_params=pltpu.CompilerParams(
+            collective_id=0, has_side_effects=True, vmem_limit_bytes=48 * 1024 * 1024
+        ),
+    )(part)
 
 
 def layer_norm(tensor, epsilon):
@@ -193,9 +263,7 @@
         approximate=True,
     ).astype(jnp.bfloat16)
     feed_terms = jnp.dot(hidden_units, w_down, preferred_element_type=jnp.float32)
-    feed_out = lax.psum_scatter(
-        feed_terms.astype(jnp.bfloat16), "row", scatter_dimension=0, tiled=True
-    ).astype(jnp.float32)
+    feed_out = row_scatter_sum(feed_terms.astype(jnp.bfloat16))
     out_hidden = (mixed + adaptive[5] * feed_out).astype(jnp.bfloat16)
     final_norm = modulate(out_hidden.astype(jnp.float32), adaptive[6], adaptive[7])
     velocity = jnp.dot(final_norm, w_proj, preferred_element_type=jnp.float32)

time: 707 us -> 594 us (0.84)
  waiting for transfers between devices: 564 us -> 343 us
  Pallas kernels: 0 us -> 108 us
    reduce_scatter x1 -> x0, waiting for transfers between devices: 213 us -> none  [shards(): lax.psum_scatter(feed_terms.astype(jnp.bfloat16), 'row', scatter_dimensio...]
    pallas_call x0 -> x1, Pallas kernels: none -> 108 us  [row_scatter_sum(): pl.pallas_call(functools.partial(scatter_sum_kernel, count, rows), out_sh...]
    all_gather x1, waiting for transfers between devices: 82.8 us -> 75.7 us  [shards(): lax.all_gather(second_norm, 'row', axis=0, tiled=True)]
  transfers between devices with their start and end apart: 10 -> 9, of which waited for: 8 -> 7; matrix products, arithmetic and copies ran while one was open for 2% -> 2% of each run, Pallas kernels for 0% -> 0%
where the time goes in v2:
time: 594 us; the launch traced here: 592 us
  waiting for transfers between devices  343 us (58%)
  Pallas kernels  108 us (18%)
  local copies, waits for them, and re-layouts  52.5 us (9%)
  matrix products  43.7 us (7%)
  between operations  18.3 us (3%)
  other arithmetic  14.5 us (2%)
  starting transfers between devices  12.1 us (2%)
    all_gather x1, waiting for transfers between devices, shards(): both = lax.all_gather(both, 'row', axis=0, tiled=True)  113 us
    pallas_call x1, Pallas kernels, row_scatter_sum(): pl.pallas_call(functools.partial(scatter_sum_kernel, count, rows), out_sh...  108 us
    all_gather x1, waiting for transfers between devices, shards(): gathered_half = lax.all_gather(own_half, 'row', axis=1, tiled=True)  95.3 us
    all_gather x1, waiting for transfers between devices, shards(): lax.all_gather(second_norm, 'row', axis=0, tiled=True)  75.7 us
    all_gather x1, waiting for transfers between devices, shards(): lax.all_gather(gathered_half, 'req', axis=2, tiled=True)  28.7 us
    another operation x4, local copies, waits for them, and re-layouts  26 us
    reduce_scatter x1, waiting for transfers between devices, shards(): lax.psum_scatter(partial_out, 'col', scatter_dimension=0, tiled=True)  23.8 us
  transfers between devices with their start and end apart: 9, of which 7 were waited for; matrix products, arithmetic and copies ran while one was open for 2% of the time, Pallas kernels for 0%

profile of v2, /device:TPU:2, one launch (start us, length us, event | category | flops | bytes accessed | tf_op | source)
XLA Modules:
  0.0 592.1 jit_solution(15148180402457044612)
XLA Ops:
  7.2 1.8 constant_dynamic-slice_fusion
  9.1 95.3 %all-gather.6.cloned.1.call-done = bf16[3,3072,384]{2,1,0:T(8,128)(2,1)} async-done(((bf16[3,96,384]{2,1,0:T(8,128)(2,1)}), bf16[3,3072,384]{2,1,0:T(8,128)(2,1)}) %all-gather.6.cloned.1.call-update) | async-done | bytes 7077904 | tf_op jit(solution)/shard_map/all_gather | solution.py:227
  104.4 0.7 copy-done.7
  105.1 0.1 convert_reduce_fusion.3
  105.2 0.2 fusion.71
  105.4 0.2 convert_reduce_fusion
  105.6 0.3 multiply_reduce_fusion
  106.0 0.7 slice_add_fusion
  106.7 0.7 fusion.74
  107.4 0.3 add_convert_fusion
  107.7 28.7 %all-gather.8.cloned.1.call-done = bf16[3,3072,768]{2,1,0:T(8,128)(2,1)} async-done(((bf16[3,3072,384]{2,1,0:T(8,128)(2,1)}), bf16[3,3072,768]{2,1,0:T(8,128)(2,1)}) %all-gather.8.cloned.1.call-update) | async-done | bytes 14155792 | tf_op jit(solution)/shard_map/all_gather | solution.py:228
  136.4 7.0 %convolution_bitcast_fusion = f32[3,1,100,768]{3,2,0,1:T(8,128)S(1)} fusion(bf16[3,3072,768]{2,1,0:T(8,128)(2,1)} %all-gather.8.cloned.1.call-done, bf16[4,3072]{1,0:T(4,128)(2,1)} %fusion.74, bf16[96,3072]{1,0:T(8,128)(2,1)S(1)} %add_convert_fusion), kind=kOutput, calls=%fused_computation.10 | convolution fusion | flops 1416806400 | bytes 15691776 | tf_op jit(solution)/shard_map/gld,cde->cgle/dot_general | solution.py:161
  143.5 0.9 copy-done.5
  144.4 0.2 copy.30
  144.6 0.2 copy.28
  145.1 0.8 pad_maximum_fusion
  146.0 0.2 slice_reduce_fusion.3
  146.2 0.7 select_reduce_fusion.4
  146.9 0.7 fusion.157
  147.6 2.0 fusion.152
  149.6 1.6 copy.32
  151.3 0.7 copy-done.10
  152.1 0.6 add_rsqrt_fusion
  152.7 113.1 %all-gather.12.cloned.1.call-done = bf16[64,100,12,64]{1,3,2,0:T(8,128)(2,1)} async-done(((bf16[2,100,12,64]{1,3,2,0:T(8,128)(2,1)}), bf16[64,100,12,64]{1,3,2,0:T(8,128)(2,1)}) %all-gather.12.cloned.1.call-update) | async-done | bytes 9830416 | tf_op jit(solution)/shard_map/all_gather | solution.py:238
  265.8 11.9 %copy.45 = bf16[32,2,100,12,64]{2,0,4,3,1:T(8,128)(2,1)S(1)} copy(bf16[32,2,100,12,64]{2,4,3,1,0:T(8,128)(2,1)} %bitcast.213) | data formatting | bytes 19660800 | tf_op jit(solution)/shard_map/all_gather | solution.py:238
  277.6 5.5 fusion.175
  283.1 12.9 %reshape.413 = bf16[3200,12,64]{0,2,1:T(8,128)(2,1)} reshape(bf16[1,32,100,12,64]{2,1,4,3,0:T(8,128)(2,1)} %get-tuple-element.10) | data formatting | bytes 9830400 | tf_op jit(solution)/shard_map/reshape.45
  296.0 13.0 %reshape.414 = bf16[3200,12,64]{0,2,1:T(8,128)(2,1)} reshape(bf16[1,32,100,12,64]{2,1,4,3,0:T(8,128)(2,1)} %get-tuple-element.9) | data formatting | bytes 9830400 | tf_op jit(solution)/shard_map/reshape.37
  309.0 10.7 %bitcast_reduce_fusion = (f32[96,12]{0,1:T(8,128)S(1)}, f32[12,3200,96]{1,2,0:T(8,128)}) fusion(f32[3200]{0:T(1024)S(1)} %fusion.152, bf16[3200,12,64]{0,2,1:T(8,128)(2,1)} %reshape.414, f32[3,1,100,12,64]{2,4,3,0,1:T(8,128)} %bitcast.219, f32[64]{0:T(128)S(1)} %copy-done.24, f32[96,12]{0,1:T(8,128)S(1)} %copy-done.16, f32[96,12]{0,1:T(8,128)S(1)} %copy-done.11), kind=kOutput, calls=%fused_computation | convolution fusion | flops 483212160 | bytes 20080896 | tf_op jit(solution)/shard_map/gqhd,gkhd->gqhk/dot_general | solution.py:173
  319.7 8.3 %fusion.29 = bf16[1,96,12,64]{1,3,2,0:T(8,128)(2,1)S(1)} fusion(bf16[3200,12,64]{0,2,1:T(8,128)(2,1)S(1)} %bitcast.212, f32[12,3200,96]{1,2,0:T(8,128)} %get-tuple-element.24, f32[3200]{0:T(1024)S(1)} %fusion.152, f32[96,12]{0,1:T(8,128)S(1)} %get-tuple-element.23), kind=kOutput, calls=%fused_computation.37 | convolution fusion | flops 483065856 | bytes 19825664 | tf_op jit(solution)/shard_map/gqhk,gkhd->gqhd/dot_general | solution.py:177
  328.0 4.4 fusion.179
  332.5 0.3 all-gather.10.cloned.1.call-start
  332.7 1.1 convert_element_type.111
  333.8 23.8 %reduce-scatter.2.cloned.1.call-done = f32[24,3072]{1,0:T(8,128)} async-done(((f32[96,3072]{1,0:T(8,128)}), f32[24,3072]{1,0:T(8,128)}) %reduce-scatter.2.cloned.1.call-update) | async-done | bytes 294928 | tf_op jit(solution)/shard_map/reduce_scatter | solution.py:251
  357.6 1.1 fusion.57
  358.9 0.2 fusion.48
  359.1 0.8 fusion.51
  360.0 0.3 reduce-window.9
  361.2 1.3 select_reduce_fusion
  365.3 0.6 select_reduce_fusion.2
  366.4 0.7 and_convert_fusion
  367.1 75.7 %all-gather.10.cloned.1.call-done = bf16[768,3072]{1,0:T(8,128)(2,1)} async-done(((bf16[24,3072]{1,0:T(8,128)(2,1)}), bf16[768,3072]{1,0:T(8,128)(2,1)}) %all-gather.10.cloned.1.call-update) | async-done | bytes 4718608 | tf_op jit(solution)/shard_map/all_gather | solution.py:259
  442.8 10.4 %convolution_convert_fusion.part_ref = bf16[768,3072]{1,0:T(8,128)(2,1)} fusion(bf16[384,3072]{1,0:T(8,128)(2,1)S(1)} %copy-done, bf16[768,3072]{1,0:T(8,128)(2,1)} %all-gather.10.cloned.1.call-done, bf16[3072,384]{1,0:T(8,128)(2,1)} %param.25), kind=kOutput, calls=%fused_computation.8 | convolution fusion | flops 3628892160 | bytes 14155776 | tf_op jit(solution)/shard_map/dot_general | solution.py:265
  453.2 2.3 copy-done.1
  455.6 107.7 %shard_map.166 = f32[24,3072]{1,0:T(8,128)S(1)} custom-call(bf16[768,3072]{1,0:T(8,128)(2,1)S(1)} %copy-done.1), custom_call_target="tpu_custom_call" | custom-call | tf_op jit(solution)/shard_map/pallas_call | solution.py:87
  563.3 0.2 convert_reduce_fusion.2
  563.5 0.2 fusion.52
  563.7 0.9 multiply_convert_fusion.1
  564.9 0.3 copy.34
  565.1 3.9 collective-permute-start.1
  569.0 1.9 collective-permute-start
  571.0 0.1 fusion.126
  571.2 5.6 collective-permute-done
  576.8 1.3 collective-permute-start.3
  578.1 4.5 collective-permute-start.2
  582.6 0.1 fusion.79
  582.8 0.2 fusion.75
  582.9 1.1 collective-permute-done.2
  584.0 0.1 fusion.85
  584.2 0.2 fusion.94
  584.3 0.1 fusion.83
  584.5 0.2 fusion.102
  584.6 0.2 fusion.21
  584.8 0.8 fusion.23
  (102 shorter events, 1.6 us)
Async XLA Ops:
  7.2 435.6 %copy-start = (bf16[384,3072]{1,0:T(8,128)(2,1)S(1)}, bf16[384,3072]{1,0:T(8,128)(2,1)}, u32[]{:S(2)}) copy-start(bf16[384,3072]{1,0:T(8,128)(2,1)} %param.26) | copy-start | bytes 7077892
  7.2 97.2 %all-gather.6.cloned.1.call-start = ((), (), s32[]{:S(2)}) async-start(), calls=%async_computation.1 | async-start | bytes 7299072 | tf_op jit(solution)/shard_map/all_gather | solution.py:227
  9.0 127.3 %all-gather.8.cloned.1.call-start = ((), (), s32[]{:S(2)}) async-start(), calls=%async_computation.2 | async-start | bytes 21233664 | tf_op jit(solution)/shard_map/all_gather | solution.py:228
  104.4 0.7 copy-start.7
  104.4 1.1 copy-start.2
  104.4 1.6 copy-start.9
  104.4 161.4 %all-gather.12.cloned.1.call-start = ((), (), s32[]{:S(2)}) async-start(), calls=%async_computation.5 | async-start | bytes 12976128 | tf_op jit(solution)/shard_map/all_gather | solution.py:238
  143.4 1.0 copy-start.5
  143.4 1.5 copy-start.27
  143.4 2.6 copy-start.23
  143.4 2.7 copy-start.25
  143.4 2.7 copy-start.26
  145.9 211.7 %reduce-scatter.2.cloned.1.call-start = ((), (), s32[]{:S(2)}) async-start(), calls=%async_computation.3 | async-start | bytes 1474560 | tf_op jit(solution)/shard_map/reduce_scatter | solution.py:251
  146.2 1.4 copy-start.19
  146.2 1.4 copy-start.21
  151.2 126.4 %copy-start.4 = (f32[3,1,100,768]{2,3,0,1:T(8,128)}, f32[3,1,100,768]{2,3,0,1:T(8,128)S(1)}, u32[]{:S(2)}) copy-start(f32[3,1,100,768]{2,3,0,1:T(8,128)S(1)} %copy.32) | copy-start | bytes 2764804
  151.3 0.7 copy-start.10
  296.0 13.0 %copy-start.11 = (f32[96,12]{0,1:T(8,128)S(1)}, f32[96,12]{0,1:T(8,128)}, u32[]{:S(2)}) copy-start(f32[96,12]{0,1:T(8,128)} %copy-done.10) | copy-start | bytes 13828
  296.0 13.0 %copy-start.16 = (f32[96,12]{0,1:T(8,128)S(1)}, f32[96,12]{0,1:T(8,128)}, u32[]{:S(2)}) copy-start(f32[96,12]{0,1:T(8,128)} %add_rsqrt_fusion) | copy-start | bytes 13828
  296.0 13.0 %copy-start.24 = (f32[64]{0:T(128)S(1)}, f32[64]{0:T(128)}, u32[]{:S(2)}) copy-start(f32[64]{0:T(128)} %param.21) | copy-start | bytes 772
  296.0 23.6 %slice-start = ((s8[4915200]{0:T(1024)(128)(4,1)}), s8[720896]{0:T(1024)(128)(4,1)S(1)}, s32[]{:S(2)}) async-start(s8[4915200]{0:T(1024)(128)(4,1)} %bitcast.211), calls=%async_computation.6 | async-start | bytes 1441792
  309.0 10.7 %slice-start.1 = ((s8[4915200]{0:T(1024)(128)(4,1)}), s8[4194304]{0:T(1024)(128)(4,1)S(1)}, s32[]{:S(2)}) async-start(s8[4915200]{0:T(1024)(128)(4,1)} %bitcast.211), calls=%async_computation.7 | async-start | bytes 8388608
  328.0 4.7 copy-start.3
  332.4 25.2 %copy-start.15 = (f32[1,1,3072]{2,1,0:T(1,128)S(1)}, f32[1,1,3072]{2,1,0:T(1,128)}, u32[]{:S(2)}) copy-start(f32[1,1,3072]{2,1,0:T(1,128)} %get-tuple-element.17) | copy-start | bytes 36868
  332.4 26.7 %copy-start.12 = (f32[1,1,3072]{2,1,0:T(1,128)S(1)}, f32[1,1,3072]{2,1,0:T(1,128)}, u32[]{:S(2)}) copy-start(f32[1,1,3072]{2,1,0:T(1,128)} %get-tuple-element.12) | copy-start | bytes 36868
  332.4 26.7 %copy-start.13 = (f32[1,1,3072]{2,1,0:T(1,128)S(1)}, f32[1,1,3072]{2,1,0:T(1,128)}, u32[]{:S(2)}) copy-start(f32[1,1,3072]{2,1,0:T(1,128)} %get-tuple-element.13) | copy-start | bytes 36868
  332.4 32.8 %copy-start.20 = (s32[2]{0:T(128)S(1)}, s32[2]{0:T(128)}, u32[]{:S(2)}) copy-start(s32[2]{0:T(128)} %copy-done.19) | copy-start | bytes 28
  332.4 32.8 %copy-start.22 = (s32[2]{0:T(128)S(1)}, s32[2]{0:T(128)}, u32[]{:S(2)}) copy-start(s32[2]{0:T(128)} %copy-done.21) | copy-start | bytes 28
  332.5 110.3 %all-gather.10.cloned.1.call-start = ((), (), s32[]{:S(2)}) async-start(), calls=%async_computation.4 | async-start | bytes 4866048 | tf_op jit(solution)/shard_map/all_gather | solution.py:259
  453.2 2.3 copy-start.1
  455.5 107.8 %copy-start.14 = (f32[1,1,3072]{2,1,0:T(1,128)S(1)}, f32[1,1,3072]{2,1,0:T(1,128)}, u32[]{:S(2)}) copy-start(f32[1,1,3072]{2,1,0:T(1,128)} %get-tuple-element.14) | copy-start | bytes 36868
  455.5 108.2 %copy-start.17 = (f32[1,1,3072]{2,1,0:T(1,128)S(1)}, f32[1,1,3072]{2,1,0:T(1,128)}, u32[]{:S(2)}) copy-start(f32[1,1,3072]{2,1,0:T(1,128)} %get-tuple-element.11) | copy-start | bytes 36868
  455.5 108.2 %copy-start.18 = (f32[1,1,3072]{2,1,0:T(1,128)S(1)}, f32[1,1,3072]{2,1,0:T(1,128)}, u32[]{:S(2)}) copy-start(f32[1,1,3072]{2,1,0:T(1,128)} %get-tuple-element.18) | copy-start | bytes 36868
  455.5 108.2 %copy-start.28 = (bf16[3072,64]{0,1:T(8,128)(2,1)S(1)}, bf16[3072,64]{0,1:T(8,128)(2,1)}, u32[]{:S(2)}) copy-start(bf16[3072,64]{0,1:T(8,128)(2,1)} %param.27) | copy-start | bytes 1179652
  455.5 108.2 %copy-start.29 = (f32[1,24,64]{2,1,0:T(8,128)S(1)}, f32[1,24,64]{2,1,0:T(8,128)}, u32[]{:S(2)}) copy-start(f32[1,24,64]{2,1,0:T(8,128)} %param.28) | copy-start | bytes 18436
  455.5 115.4 %copy-start.8 = (bf16[3,3,16,512]{3,2,1,0:T(8,128)(2,1)S(1)}, bf16[3,3,16,512]{3,2,1,0:T(8,128)(2,1)}, u32[]{:S(2)}) copy-start(bf16[3,3,16,512]{3,2,1,0:T(8,128)(2,1)} %param.29) | copy-start | bytes 442372
  563.5 22.2 %copy-start.6 = (bf16[24,3072]{1,0:T(8,128)(2,1)}, bf16[24,3072]{1,0:T(8,128)(2,1)S(1)}, u32[]{:S(2)}) copy-start(bf16[24,3072]{1,0:T(8,128)(2,1)S(1)} %get-tuple-element.8) | copy-start | bytes 442372
  565.1 6.0 %collective-permute-start.1 = (bf16[6,1,8,16]{3,2,1,0:T(8,128)(2,1)S(1)}, bf16[6,1,8,16]{3,2,1,0:T(8,128)(2,1)S(1)}, u32[]{:S(2)}, u32[]{:S(2)}) collective-permute-start(bf16[6,1,8,16]{3,2,1,0:T(8,128)(2,1)S(1)} %get-tuple-element.22), channel_id=1, source_target_pairs={{4,0},{8,4},{12,8},{16,12},{20,16},{24,20},{28,24},{32,28},{36,32}... | collective-permute-start | bytes 4616 | tf_op jit(solution)/shard_map/ppermute | solution.py:33
  569.0 7.7 %collective-permute-start = (bf16[6,1,8,16]{3,2,1,0:T(8,128)(2,1)S(1)}, bf16[6,1,8,16]{3,2,1,0:T(8,128)(2,1)S(1)}, u32[]{:S(2)}, u32[]{:S(2)}) collective-permute-start(bf16[6,1,8,16]{3,2,1,0:T(8,128)(2,1)S(1)} %get-tuple-element.21), channel_id=1, source_target_pairs={{0,4},{4,8},{8,12},{12,16},{16,20},{20,24},{24,28},{28,32},{32,36}... | collective-permute-start | bytes 4616 | tf_op jit(solution)/shard_map/ppermute | solution.py:31
  576.8 7.5 %collective-permute-start.3 = (bf16[6,4,1,16]{3,2,1,0:T(2,128)(2,1)S(1)}, bf16[6,4,1,16]{3,2,1,0:T(2,128)(2,1)S(1)}, u32[]{:S(2)}, u32[]{:S(2)}) collective-permute-start(bf16[6,4,1,16]{3,2,1,0:T(2,128)(2,1)S(1)} %get-tuple-element.20), channel_id=1, source_target_pairs={{1,0},{2,1},{3,2},{5,4},{6,5},{7,6},{9,8},{10,9},{11,10},{13,12},{... | collective-permute-start | bytes 2312 | tf_op jit(solution)/shard_map/ppermute | solution.py:33
  578.1 5.9 %collective-permute-start.2 = (bf16[6,4,1,16]{3,2,1,0:T(2,128)(2,1)S(1)}, bf16[6,4,1,16]{3,2,1,0:T(2,128)(2,1)S(1)}, u32[]{:S(2)}, u32[]{:S(2)}) collective-permute-start(bf16[6,4,1,16]{3,2,1,0:T(2,128)(2,1)S(1)} %get-tuple-element.19), channel_id=1, source_target_pairs={{0,1},{1,2},{2,3},{4,5},{5,6},{6,7},{8,9},{9,10},{10,11},{12,13},{... | collective-permute-start | bytes 2312 | tf_op jit(solution)/shard_map/ppermute | solution.py:31
Sparse Core Ops, SparseCore 0:
  10.6 93.6 all-gather.5
  106.2 30.1 all-gather.7
  146.0 119.6 all-gather.11
  332.6 24.9 reduce-scatter.1
  360.6 82.1 all-gather.9

commit v3 on v2

--- a/solution.py
+++ b/solution.py
@@ -37,14 +37,16 @@
     return cells
 
 
-def scatter_sum_kernel(count, rows, part_ref, out_ref, landed, send_sems, recv_sems, own_sem):
-    me = lax.axis_index("row")
-    req = lax.axis_index("req")
-    col = lax.axis_index("col")
+def peer_on(axis, peer):
+    return tuple(peer if name == axis else lax.axis_index(name) for name in ("req", "row", "col"))
+
+
+def scatter_sum_kernel(axis, count, rows, part_ref, out_ref, landed, send_sems, recv_sems, own_sem):
+    me = lax.axis_index(axis)
     barrier = pltpu.get_barrier_semaphore()
     for step in range(1, count):
         peer = lax.rem(me + step, count)
-        pl.semaphore_signal(barrier, inc=1, device_id=(req, peer, col), device_id_type=MESH_IDS)
+        pl.semaphore_signal(barrier, inc=1, device_id=peer_on(axis, peer), device_id_type=MESH_IDS)
     pl.semaphore_wait(barrier, count - 1)
     own = pltpu.make_async_copy(part_ref.at[pl.ds(me * rows, rows)], landed.at[me], own_sem)
     own.start()
@@ -56,7 +58,7 @@
             dst_ref=landed.at[me],
             send_sem=send_sems.at[step],
             recv_sem=recv_sems.at[step],
-            device_id=(req, peer, col),
+            device_id=peer_on(axis, peer),
             device_id_type=MESH_IDS,
         )
         copy.start()
@@ -69,7 +71,7 @@
             dst_ref=landed.at[source],
             send_sem=send_sems.at[step],
             recv_sem=recv_sems.at[step],
-            device_id=(req, source, col),
+            device_id=peer_on(axis, source),
             device_id_type=MESH_IDS,
         ).wait_recv()
     for copy in sends:
@@ -80,12 +82,12 @@
     out_ref[...] = total
 
 
-def row_scatter_sum(part):
-    count = lax.axis_size("row")
+def scatter_sum(part, axis, kernel_id):
+    count = lax.axis_size(axis)
     rows = part.shape[0] // count
     width = part.shape[1]
     return pl.pallas_call(
-        functools.partial(scatter_sum_kernel, count, rows),
+        functools.partial(scatter_sum_kernel, axis, count, rows),
         out_shape=jax.ShapeDtypeStruct((rows, width), jnp.float32),
         in_specs=[pl.BlockSpec(memory_space=pl.ANY)],
         out_specs=pl.BlockSpec(memory_space=pltpu.VMEM),
@@ -96,9 +98,42 @@
             pltpu.SemaphoreType.DMA(()),
         ],
         compiler_params=pltpu.CompilerParams(
-            collective_id=0, has_side_effects=True, vmem_limit_bytes=48 * 1024 * 1024
+            collective_id=kernel_id, has_side_effects=True, vmem_limit_bytes=48 * 1024 * 1024
         ),
     )(part)
+
+
+def attention_kernel(scale, q_ref, kv_ref, live_ref, out_ref):
+    sources, _, block, width = kv_ref.shape
+    lane = lax.broadcasted_iota(jnp.int32, (1, 128), 1)
+    first = lane < 64
+    live = live_ref[...]
+    for pair in range(width // 128):
+        cols = slice(pair * 128, (pair + 1) * 128)
+        query = q_ref[:, cols]
+        keys = kv_ref[:, 0, :, cols].reshape(sources * block, 128)
+        values = kv_ref[:, 1, :, cols].reshape(sources * block, 128)
+        results = []
+        for half in (first, jnp.logical_not(first)):
+            picked = jnp.where(half, query, jnp.zeros_like(query))
+            scores = lax.dot_general(
+                picked, keys, (((1,), (1,)), ((), ())), preferred_element_type=jnp.float32
+            ) * scale
+            weights = jnp.exp(scores) * live
+            totals = jnp.sum(weights, axis=1, keepdims=True)
+            summed = jnp.dot(weights.astype(jnp.bfloat16), values, preferred_element_type=jnp.float32)
+            results.append(summed / totals)
+        out_ref[:, cols] = jnp.where(first, results[0], results[1]).astype(out_ref.dtype)
+
+
+def attention(queries, gathered, live, scale):
+    return pl.pallas_call(
+        functools.partial(attention_kernel, scale),
+        out_shape=jax.ShapeDtypeStruct(queries.shape, jnp.bfloat16),
+        in_specs=[pl.BlockSpec(memory_space=pltpu.VMEM)] * 3,
+        out_specs=pl.BlockSpec(memory_space=pltpu.VMEM),
+        compiler_params=pltpu.CompilerParams(vmem_limit_bytes=56 * 1024 * 1024),
+    )(queries, gathered, live)
 
 
 def layer_norm(tensor, epsilon):
@@ -153,7 +188,7 @@
     video_live = (token_row[None, :] < rows_live[:, None]) & (
         token_col[None, :] < cols_live[:, None]
     )
-    text_live = text_index[None, :] < text_lens[:, None]
+    text_live = (text_index[None, :] < text_lens[:, None]) & (within < block_tokens + text_rows)[None, :]
     return jnp.where(is_video[None, :], video_live, text_live).astype(jnp.float32)
 
 
@@ -234,21 +269,21 @@
     value_block = shaped[2].astype(jnp.bfloat16)
     attend = attention_step(queries, owners, grid, text_len, span, block_tokens, tile, text_rows)
     empty_state = (jnp.zeros(queries.shape, jnp.float32), jnp.zeros(queries.shape[:3], jnp.float32))
-    both = jnp.stack([key_block[0], value_block[0]], axis=0)[None]
-    both = lax.all_gather(both, "row", axis=0, tiled=True)
-    both = jnp.swapaxes(both, 0, 1).reshape(2, 1, -1, heads_here, head_dim)
-    weighted, totals = attend(
-        empty_state,
-        (both[0], both[1]),
-        jnp.int32(0),
-    )
-    attended = (
-        (weighted / totals[..., None])
-        .astype(jnp.bfloat16)
-        .reshape(groups * block_tokens, heads_here * head_dim)
+    padded_span = 128 * pl.cdiv(span, 128)
+    both = jnp.stack([key_block[0], value_block[0]], axis=0).reshape(2, span, heads_here * head_dim)
+    both = jnp.pad(both, ((0, 0), (0, padded_span - span), (0, 0)))[None]
+    gathered = lax.all_gather(both, "row", axis=0, tiled=True)
+    live = key_mask(
+        gathered.shape[0] * padded_span, owners, grid, text_len, padded_span, block_tokens, tile, text_rows
+    )
+    attended = attention(
+        queries[0].reshape(block_tokens, heads_here * head_dim),
+        gathered,
+        live,
+        head_dim ** (-0.5),
     )
     partial_out = jnp.dot(attended, w_out, preferred_element_type=jnp.float32)
-    projected = lax.psum_scatter(partial_out, "col", scatter_dimension=0, tiled=True)
+    projected = scatter_sum(partial_out, "col", 1)
     own_rows = lax.dynamic_slice_in_dim(source, col_id * tile, tile, 0)
     mixed = lax.optimization_barrier(
         (own_rows + adaptive[2] * projected).astype(jnp.bfloat16)
@@ -263,7 +298,7 @@
         approximate=True,
     ).astype(jnp.bfloat16)
     feed_terms = jnp.dot(hidden_units, w_down, preferred_element_type=jnp.float32)
-    feed_out = row_scatter_sum(feed_terms.astype(jnp.bfloat16))
+    feed_out = scatter_sum(feed_terms.astype(jnp.bfloat16), "row", 0)
     out_hidden = (mixed + adaptive[5] * feed_out).astype(jnp.bfloat16)
     final_norm = modulate(out_hidden.astype(jnp.float32), adaptive[6], adaptive[7])
     velocity = jnp.dot(final_norm, w_proj, preferred_element_type=jnp.float32)

time: 594 us -> 534 us (0.90)
  local copies, waits for them, and re-layouts: 52.5 us -> 15 us
  waiting for transfers between devices: 343 us -> 306 us
  Pallas kernels: 108 us -> 138 us
  matrix products: 43.7 us -> 22.1 us
    pallas_call x1 -> x3, Pallas kernels: 108 us -> 138 us  [the longest x2 125 us: scatter_sum(): pl.pallas_call(functools.partial(scatter_sum_kernel, axis, count, rows),...]
    another operation x4 -> x2, local copies, waits for them, and re-layouts: 26 us -> 0.12 us
    reduce_scatter x1 -> x0, waiting for transfers between devices: 23.8 us -> none  [shards(): lax.psum_scatter(partial_out, 'col', scatter_dimension=0, tiled=True)]
    dot_general x2 -> x0, matrix products: 19 us -> none  [the longest x1 10.7 us: attend(): jnp.einsum('gqhd,gkhd->gqhk', queries, key_piece, preferred_element_type=...]
    all_gather x1 -> x0, local copies, waits for them, and re-layouts: 11.9 us -> none  [shards(): both = lax.all_gather(both, 'row', axis=0, tiled=True)]
  transfers between devices with their start and end apart: 9 -> 8, of which waited for: 7 -> 6; matrix products, arithmetic and copies ran while one was open for 2% -> 4% of each run, Pallas kernels for 0% -> 0%
where the time goes in v3:
time: 534 us; the launch traced here: 532 us
  waiting for transfers between devices  306 us (57%)
  Pallas kernels  138 us (26%)
  matrix products  22.1 us (4%)
  other arithmetic  19 us (4%)
  between operations  18.2 us (3%)
  local copies, waits for them, and re-layouts  15 us (3%)
  starting transfers between devices  14.1 us (3%)
    pallas_call x2, Pallas kernels, scatter_sum(): pl.pallas_call(functools.partial(scatter_sum_kernel, axis, count, rows),...  125 us
    all_gather x1, waiting for transfers between devices, shards(): gathered = lax.all_gather(both, 'row', axis=0, tiled=True)  108 us
    all_gather x1, waiting for transfers between devices, shards(): gathered_half = lax.all_gather(own_half, 'row', axis=1, tiled=True)  95.3 us
    all_gather x1, waiting for transfers between devices, shards(): lax.all_gather(second_norm, 'row', axis=0, tiled=True)  72.1 us
    all_gather x1, waiting for transfers between devices, shards(): lax.all_gather(gathered_half, 'req', axis=2, tiled=True)  28.7 us
    pallas_call x1, Pallas kernels, attention(): pl.pallas_call(functools.partial(attention_kernel, scale), out_shape=jax....  12.8 us
  transfers between devices with their start and end apart: 8, of which 6 were waited for; matrix products, arithmetic and copies ran while one was open for 4% of the time, Pallas kernels for 0%

profile of v3, /device:TPU:2, one launch (start us, length us, event | category | flops | bytes accessed | tf_op | source)
XLA Modules:
  0.0 532.4 jit_solution(8474808766969291200)
XLA Ops:
  7.2 1.8 constant_dynamic-slice_fusion
  9.1 95.3 %all-gather.6.cloned.1.call-done = bf16[3,3072,384]{2,1,0:T(8,128)(2,1)} async-done(((bf16[3,96,384]{2,1,0:T(8,128)(2,1)}), bf16[3,3072,384]{2,1,0:T(8,128)(2,1)}) %all-gather.6.cloned.1.call-update) | async-done | bytes 7077904 | tf_op jit(solution)/shard_map/all_gather | solution.py:262
  104.4 0.6 copy-done.18
  105.3 0.2 fusion.57
  105.5 0.2 convert_reduce_fusion
  105.6 0.3 multiply_reduce_fusion
  106.0 0.7 slice_add_fusion
  106.7 0.7 fusion.60
  107.4 0.3 add_convert_fusion
  107.7 28.7 %all-gather.8.cloned.1.call-done = bf16[3,3072,768]{2,1,0:T(8,128)(2,1)} async-done(((bf16[3,3072,384]{2,1,0:T(8,128)(2,1)}), bf16[3,3072,768]{2,1,0:T(8,128)(2,1)}) %all-gather.8.cloned.1.call-update) | async-done | bytes 14155792 | tf_op jit(solution)/shard_map/all_gather | solution.py:263
  136.4 7.0 %fusion.20 = f32[3,768,100]{1,2,0:T(8,128)S(1)} fusion(bf16[3,3072,768]{2,1,0:T(8,128)(2,1)} %all-gather.8.cloned.1.call-done, bf16[4,3072]{1,0:T(4,128)(2,1)} %fusion.60, bf16[96,3072]{1,0:T(8,128)(2,1)S(1)} %add_convert_fusion), kind=kOutput, calls=%fused_computation.31 | convolution fusion | flops 1416806400 | bytes 15691776 | tf_op jit(solution)/shard_map/gld,cde->cgle/dot_general | solution.py:196
  143.4 0.9 copy-done.3
  144.3 0.7 slice.173
  145.1 1.1 copy.37
  146.4 0.9 copy.40
  147.3 0.9 copy.38
  148.2 1.0 fusion.48
  149.2 1.2 fusion.37
  150.4 0.8 fusion.28
  151.2 0.2 all-gather.10.cloned.1.call-start
  151.5 1.2 convert_element_type.103
  152.7 0.6 select_reduce_fusion.5
  153.4 0.2 slice_reduce_fusion.2
  153.6 0.7 fusion.128
  154.3 2.8 select_convert_fusion.live_ref
  157.1 1.6 copy.32
  158.6 0.8 fusion.145
  159.6 0.2 copy.35
  159.8 0.9 copy.34
  160.6 0.9 copy.33
  161.5 1.8 multiply_convert_fusion.q_ref
  163.3 107.8 %all-gather.12.cloned.1.call-done = bf16[64,128,768]{2,1,0:T(8,128)(2,1)} async-done(((bf16[2,128,768]{2,1,0:T(8,128)(2,1)}), bf16[64,128,768]{2,1,0:T(8,128)(2,1)}) %all-gather.12.cloned.1.call-update) | async-done | bytes 12582928 | tf_op jit(solution)/shard_map/all_gather | solution.py:275
  271.1 12.8 %shard_map.166 = bf16[96,768]{1,0:T(8,128)(2,1)} custom-call(bf16[96,768]{1,0:T(8,128)(2,1)} %multiply_convert_fusion.q_ref, bf16[32,2,128,768]{3,2,1,0:T(8,128)(2,1)} %bitcast.156, f32[1,4096]{1,0:T(1,128)} %select_convert_fusion.live_ref), custom_call_target="tpu_custom_call" | custom-call | tf_op jit(solution)/shard_map/pallas_call | solution.py:130
  283.9 1.8 fusion.149.part_ref
  285.7 17.2 %shard_map.167 = f32[24,3072]{1,0:T(8,128)S(1)} custom-call(f32[96,3072]{1,0:T(8,128)S(1)} %fusion.149.part_ref), custom_call_target="tpu_custom_call" | custom-call | tf_op jit(solution)/shard_map/pallas_call | solution.py:89
  303.0 1.0 fusion.47
  304.1 0.2 fusion.38
  304.4 0.8 fusion.41
  305.3 0.3 reduce-window.9
  305.7 0.6 select_reduce_fusion.4
  307.1 1.3 select_reduce_fusion
  311.3 0.6 select_reduce_fusion.2
  312.5 0.7 and_convert_fusion
  313.1 72.1 %all-gather.10.cloned.1.call-done = bf16[768,3072]{1,0:T(8,128)(2,1)} async-done(((bf16[24,3072]{1,0:T(8,128)(2,1)}), bf16[768,3072]{1,0:T(8,128)(2,1)}) %all-gather.10.cloned.1.call-update) | async-done | bytes 4718608 | tf_op jit(solution)/shard_map/all_gather | solution.py:294
  385.3 10.4 %convolution_convert_fusion.part_ref = bf16[768,3072]{1,0:T(8,128)(2,1)} fusion(bf16[384,3072]{1,0:T(8,128)(2,1)S(1)} %copy-done, bf16[768,3072]{1,0:T(8,128)(2,1)} %all-gather.10.cloned.1.call-done, bf16[3072,384]{1,0:T(8,128)(2,1)} %param.25), kind=kOutput, calls=%fused_computation | convolution fusion | flops 3628892160 | bytes 14155776 | tf_op jit(solution)/shard_map/dot_general | solution.py:300
  395.7 2.3 copy-done.1
  398.0 107.7 %shard_map.168 = f32[24,3072]{1,0:T(8,128)S(1)} custom-call(bf16[768,3072]{1,0:T(8,128)(2,1)S(1)} %copy-done.1), custom_call_target="tpu_custom_call" | custom-call | tf_op jit(solution)/shard_map/pallas_call | solution.py:89
  505.8 0.2 convert_reduce_fusion.2
  506.0 0.2 fusion.42
  506.2 0.9 multiply_convert_fusion.1
  507.4 0.3 copy.42
  507.6 2.1 collective-permute-start
  509.7 5.9 %collective-permute-start.1 = (bf16[6,1,8,16]{3,2,1,0:T(8,128)(2,1)S(1)}, bf16[6,1,8,16]{3,2,1,0:T(8,128)(2,1)S(1)}, u32[]{:S(2)}, u32[]{:S(2)}) collective-permute-start(bf16[6,1,8,16]{3,2,1,0:T(8,128)(2,1)S(1)} %get-tuple-element.22), channel_id=1, source_target_pairs={{4,0},{8,4},{12,8},{16,12},{20,16},{24,20},{28,24},{32,28},{36,32}... | collective-permute-start | bytes 4616 | tf_op jit(solution)/shard_map/ppermute | solution.py:33
  515.8 1.2 collective-permute-done.1
  517.0 1.3 collective-permute-start.3
  518.3 4.5 collective-permute-start.2
  523.0 0.2 fusion.65
  523.2 1.1 collective-permute-done.2
  524.3 0.1 fusion.80
  524.4 0.2 fusion.71
  524.6 0.1 fusion.88
  524.7 0.2 fusion.69
  524.9 0.2 fusion.13
  525.1 0.8 fusion.15
  (97 shorter events, 2.0 us)
Async XLA Ops:
  7.2 378.1 %copy-start = (bf16[384,3072]{1,0:T(8,128)(2,1)S(1)}, bf16[384,3072]{1,0:T(8,128)(2,1)}, u32[]{:S(2)}) copy-start(bf16[384,3072]{1,0:T(8,128)(2,1)} %param.26) | copy-start | bytes 7077892
  7.2 97.2 %all-gather.6.cloned.1.call-start = ((), (), s32[]{:S(2)}) async-start(), calls=%async_computation | async-start | bytes 7299072 | tf_op jit(solution)/shard_map/all_gather | solution.py:262
  9.0 127.3 %all-gather.8.cloned.1.call-start = ((), (), s32[]{:S(2)}) async-start(), calls=%async_computation.1 | async-start | bytes 21233664 | tf_op jit(solution)/shard_map/all_gather | solution.py:263
  104.4 0.7 copy-start.18
  104.4 0.8 copy-start.6
  104.4 1.1 copy-start.2
  104.4 1.6 copy-start.8
  104.4 166.7 %all-gather.12.cloned.1.call-start = ((), (), s32[]{:S(2)}) async-start(), calls=%async_computation.3 | async-start | bytes 12976128 | tf_op jit(solution)/shard_map/all_gather | solution.py:275
  143.4 0.9 copy-start.3
  151.2 1.5 copy-start.19
  151.2 1.5 copy-start.22
  151.2 2.2 copy-start.17
  151.2 234.0 %all-gather.10.cloned.1.call-start = ((), (), s32[]{:S(2)}) async-start(), calls=%async_computation.2 | async-start | bytes 4866048 | tf_op jit(solution)/shard_map/all_gather | solution.py:294
  153.6 0.7 copy-start.15
  159.5 1.1 copy-start.4
  161.5 122.4 %slice-start = ((s8[4718592]{0:T(1024)(128)(4,1)}), s8[524288]{0:T(1024)(128)(4,1)S(1)}, s32[]{:S(2)}) async-start(s8[4718592]{0:T(1024)(128)(4,1)} %bitcast.157), calls=%async_computation.4 | async-start | bytes 1048576
  271.1 12.8 %slice-start.1 = ((s8[4718592]{0:T(1024)(128)(4,1)}), s8[4194304]{0:T(1024)(128)(4,1)S(1)}, s32[]{:S(2)}) async-start(s8[4718592]{0:T(1024)(128)(4,1)} %bitcast.157), calls=%async_computation.5 | async-start | bytes 8388608
  285.7 17.3 %copy-start.12 = (f32[1,1,3072]{2,1,0:T(1,128)S(1)}, f32[1,1,3072]{2,1,0:T(1,128)}, u32[]{:S(2)}) copy-start(f32[1,1,3072]{2,1,0:T(1,128)} %get-tuple-element.17) | copy-start | bytes 36868
  285.7 18.7 %copy-start.9 = (f32[1,1,3072]{2,1,0:T(1,128)S(1)}, f32[1,1,3072]{2,1,0:T(1,128)}, u32[]{:S(2)}) copy-start(f32[1,1,3072]{2,1,0:T(1,128)} %get-tuple-element.12) | copy-start | bytes 36868
  285.7 18.7 %copy-start.10 = (f32[1,1,3072]{2,1,0:T(1,128)S(1)}, f32[1,1,3072]{2,1,0:T(1,128)}, u32[]{:S(2)}) copy-start(f32[1,1,3072]{2,1,0:T(1,128)} %get-tuple-element.13) | copy-start | bytes 36868
  285.7 20.0 %copy-start.23 = (s32[2]{0:T(128)S(1)}, s32[2]{0:T(128)}, u32[]{:S(2)}) copy-start(s32[2]{0:T(128)} %param.19) | copy-start | bytes 28
  303.0 8.3 %copy-start.16 = (s32[2]{0:T(128)S(1)}, s32[2]{0:T(128)}, u32[]{:S(2)}) copy-start(s32[2]{0:T(128)} %copy-done.15) | copy-start | bytes 28
  395.7 2.3 copy-start.1
  398.0 107.8 %copy-start.11 = (f32[1,1,3072]{2,1,0:T(1,128)S(1)}, f32[1,1,3072]{2,1,0:T(1,128)}, u32[]{:S(2)}) copy-start(f32[1,1,3072]{2,1,0:T(1,128)} %get-tuple-element.14) | copy-start | bytes 36868
  398.0 108.2 %copy-start.13 = (f32[1,1,3072]{2,1,0:T(1,128)S(1)}, f32[1,1,3072]{2,1,0:T(1,128)}, u32[]{:S(2)}) copy-start(f32[1,1,3072]{2,1,0:T(1,128)} %get-tuple-element.11) | copy-start | bytes 36868
  398.0 108.2 %copy-start.14 = (f32[1,1,3072]{2,1,0:T(1,128)S(1)}, f32[1,1,3072]{2,1,0:T(1,128)}, u32[]{:S(2)}) copy-start(f32[1,1,3072]{2,1,0:T(1,128)} %get-tuple-element.18) | copy-start | bytes 36868
  398.0 108.2 %copy-start.20 = (bf16[3072,64]{0,1:T(8,128)(2,1)S(1)}, bf16[3072,64]{0,1:T(8,128)(2,1)}, u32[]{:S(2)}) copy-start(bf16[3072,64]{0,1:T(8,128)(2,1)} %param.27) | copy-start | bytes 1179652
  398.0 108.2 %copy-start.21 = (f32[1,24,64]{2,1,0:T(8,128)S(1)}, f32[1,24,64]{2,1,0:T(8,128)}, u32[]{:S(2)}) copy-start(f32[1,24,64]{2,1,0:T(8,128)} %param.28) | copy-start | bytes 18436
  505.8 9.8 %copy-start.7 = (bf16[3,3,16,512]{3,2,1,0:T(8,128)(2,1)S(1)}, bf16[3,3,16,512]{3,2,1,0:T(8,128)(2,1)}, u32[]{:S(2)}) copy-start(bf16[3,3,16,512]{3,2,1,0:T(8,128)(2,1)} %param.29) | copy-start | bytes 442372
  506.0 18.6 %copy-start.5 = (bf16[24,3072]{1,0:T(8,128)(2,1)}, bf16[24,3072]{1,0:T(8,128)(2,1)S(1)}, u32[]{:S(2)}) copy-start(bf16[24,3072]{1,0:T(8,128)(2,1)S(1)} %get-tuple-element.8) | copy-start | bytes 442372
  507.6 8.1 %collective-permute-start = (bf16[6,1,8,16]{3,2,1,0:T(8,128)(2,1)S(1)}, bf16[6,1,8,16]{3,2,1,0:T(8,128)(2,1)S(1)}, u32[]{:S(2)}, u32[]{:S(2)}) collective-permute-start(bf16[6,1,8,16]{3,2,1,0:T(8,128)(2,1)S(1)} %get-tuple-element.21), channel_id=1, source_target_pairs={{0,4},{4,8},{8,12},{12,16},{16,20},{20,24},{24,28},{28,32},{32,36}... | collective-permute-start | bytes 4616 | tf_op jit(solution)/shard_map/ppermute | solution.py:31
  509.7 7.3 %collective-permute-start.1 = (bf16[6,1,8,16]{3,2,1,0:T(8,128)(2,1)S(1)}, bf16[6,1,8,16]{3,2,1,0:T(8,128)(2,1)S(1)}, u32[]{:S(2)}, u32[]{:S(2)}) collective-permute-start(bf16[6,1,8,16]{3,2,1,0:T(8,128)(2,1)S(1)} %get-tuple-element.22), channel_id=1, source_target_pairs={{4,0},{8,4},{12,8},{16,12},{20,16},{24,20},{28,24},{32,28},{36,32}... | collective-permute-start | bytes 4616 | tf_op jit(solution)/shard_map/ppermute | solution.py:33
  517.0 7.6 %collective-permute-start.3 = (bf16[6,4,1,16]{3,2,1,0:T(2,128)(2,1)S(1)}, bf16[6,4,1,16]{3,2,1,0:T(2,128)(2,1)S(1)}, u32[]{:S(2)}, u32[]{:S(2)}) collective-permute-start(bf16[6,4,1,16]{3,2,1,0:T(2,128)(2,1)S(1)} %get-tuple-element.20), channel_id=1, source_target_pairs={{1,0},{2,1},{3,2},{5,4},{6,5},{7,6},{9,8},{10,9},{11,10},{13,12},{... | collective-permute-start | bytes 2312 | tf_op jit(solution)/shard_map/ppermute | solution.py:33
  518.3 5.9 %collective-permute-start.2 = (bf16[6,4,1,16]{3,2,1,0:T(2,128)(2,1)S(1)}, bf16[6,4,1,16]{3,2,1,0:T(2,128)(2,1)S(1)}, u32[]{:S(2)}, u32[]{:S(2)}) collective-permute-start(bf16[6,4,1,16]{3,2,1,0:T(2,128)(2,1)S(1)} %get-tuple-element.19), channel_id=1, source_target_pairs={{0,1},{1,2},{2,3},{4,5},{5,6},{6,7},{8,9},{9,10},{10,11},{12,13},{... | collective-permute-start | bytes 2312 | tf_op jit(solution)/shard_map/ppermute | solution.py:31
Sparse Core Ops, SparseCore 0:
  10.6 93.6 all-gather.5
  106.2 30.1 all-gather.7
  151.4 119.6 all-gather.11
  305.3 79.9 all-gather.9

commit v4 on v3

--- a/solution.py
+++ b/solution.py
@@ -134,6 +134,119 @@
         out_specs=pl.BlockSpec(memory_space=pltpu.VMEM),
         compiler_params=pltpu.CompilerParams(vmem_limit_bytes=56 * 1024 * 1024),
     )(queries, gathered, live)
+
+
+def ring_scatter_kernel(zs, xs, part_ref, out_ref, landed, outgoing, own_sum, crossed, ring_send, ring_recv, cross_send, cross_recv):
+    me = lax.axis_index("row")
+    xm = me // zs
+    zm = me % zs
+    ahead = xm * zs + lax.rem(zm + 1, zs)
+    behind = xm * zs + lax.rem(zm + zs - 1, zs)
+    half = part_ref.shape[3] // 2
+    barrier = pltpu.get_barrier_semaphore()
+    targets = [ahead, behind] + [lax.rem(xm + k, xs) * zs + zm for k in range(1, xs)]
+    for peer in targets:
+        pl.semaphore_signal(barrier, inc=1, device_id=peer_on("row", peer), device_id_type=MESH_IDS)
+    pl.semaphore_wait(barrier, len(targets))
+    ways = ((0, ahead, behind, -1), (1, behind, ahead, 1))
+    pending = []
+    for step in range(zs - 1):
+        for way, dest, origin, sign in ways:
+            cols = pl.ds(way * half, half)
+            chunk = lax.rem(zm + sign * (1 + step) + 2 * zs, zs)
+            if step == 0:
+                source = part_ref.at[chunk, :, :, cols]
+            else:
+                arrived = pltpu.make_async_remote_copy(
+                    src_ref=outgoing.at[way, step - 1],
+                    dst_ref=landed.at[way, step - 1],
+                    send_sem=ring_send.at[way, step - 1],
+                    recv_sem=ring_recv.at[way, step - 1],
+                    device_id=peer_on("row", origin),
+                    device_id_type=MESH_IDS,
+                )
+                arrived.wait_recv()
+                outgoing[way, step] = (
+                    landed[way, step - 1].astype(jnp.float32)
+                    + part_ref[chunk, :, :, cols].astype(jnp.float32)
+                ).astype(outgoing.dtype)
+                source = outgoing.at[way, step]
+            copy = pltpu.make_async_remote_copy(
+                src_ref=source,
+                dst_ref=landed.at[way, step],
+                send_sem=ring_send.at[way, step],
+                recv_sem=ring_recv.at[way, step],
+                device_id=peer_on("row", dest),
+                device_id_type=MESH_IDS,
+            )
+            copy.start()
+            pending.append(copy)
+    last = zs - 2
+    for way, dest, origin, sign in ways:
+        cols = pl.ds(way * half, half)
+        pltpu.make_async_remote_copy(
+            src_ref=outgoing.at[way, last],
+            dst_ref=landed.at[way, last],
+            send_sem=ring_send.at[way, last],
+            recv_sem=ring_recv.at[way, last],
+            device_id=peer_on("row", origin),
+            device_id_type=MESH_IDS,
+        ).wait_recv()
+        own_sum[:, :, cols] = landed[way, last].astype(jnp.float32) + part_ref[zm, :, :, cols].astype(jnp.float32)
+    crossed[0] = own_sum[...].astype(crossed.dtype)
+    sends = []
+    for k in range(1, xs):
+        peer_x = lax.rem(xm + k, xs)
+        copy = pltpu.make_async_remote_copy(
+            src_ref=crossed.at[0, peer_x],
+            dst_ref=crossed.at[k, 0],
+            send_sem=cross_send.at[k],
+            recv_sem=cross_recv.at[k],
+            device_id=peer_on("row", peer_x * zs + zm),
+            device_id_type=MESH_IDS,
+        )
+        copy.start()
+        sends.append(copy)
+    total = own_sum[xm]
+    for k in range(1, xs):
+        origin_x = lax.rem(xm + xs - k, xs)
+        pltpu.make_async_remote_copy(
+            src_ref=crossed.at[0, 0],
+            dst_ref=crossed.at[k, 0],
+            send_sem=cross_send.at[k],
+            recv_sem=cross_recv.at[k],
+            device_id=peer_on("row", origin_x * zs + zm),
+            device_id_type=MESH_IDS,
+        ).wait_recv()
+        total = total + crossed[k, 0].astype(jnp.float32)
+    out_ref[...] = total
+    for copy in pending + sends:
+        copy.wait_send()
+
+
+def ring_scatter_sum(part, xs, zs, kernel_id):
+    rows = part.shape[0] // (xs * zs)
+    width = part.shape[1]
+    arranged = part.reshape(xs, zs, rows, width).transpose(1, 0, 2, 3)
+    return pl.pallas_call(
+        functools.partial(ring_scatter_kernel, zs, xs),
+        out_shape=jax.ShapeDtypeStruct((rows, width), jnp.float32),
+        in_specs=[pl.BlockSpec(memory_space=pltpu.VMEM)],
+        out_specs=pl.BlockSpec(memory_space=pltpu.VMEM),
+        scratch_shapes=[
+            pltpu.VMEM((2, zs - 1, xs, rows, width // 2), part.dtype),
+            pltpu.VMEM((2, zs - 1, xs, rows, width // 2), part.dtype),
+            pltpu.VMEM((xs, rows, width), jnp.float32),
+            pltpu.VMEM((xs, xs, rows, width), part.dtype),
+            pltpu.SemaphoreType.DMA((2, zs - 1)),
+            pltpu.SemaphoreType.DMA((2, zs - 1)),
+            pltpu.SemaphoreType.DMA((xs,)),
+            pltpu.SemaphoreType.DMA((xs,)),
+        ],
+        compiler_params=pltpu.CompilerParams(
+            collective_id=kernel_id, has_side_effects=True, vmem_limit_bytes=56 * 1024 * 1024
+        ),
+    )(arranged)
 
 
 def layer_norm(tensor, epsilon):
@@ -298,7 +411,7 @@
         approximate=True,
     ).astype(jnp.bfloat16)
     feed_terms = jnp.dot(hidden_units, w_down, preferred_element_type=jnp.float32)
-    feed_out = scatter_sum(feed_terms.astype(jnp.bfloat16), "row", 0)
+    feed_out = ring_scatter_sum(feed_terms.astype(jnp.bfloat16), 4, 8, 0)
     out_hidden = (mixed + adaptive[5] * feed_out).astype(jnp.bfloat16)
     final_norm = modulate(out_hidden.astype(jnp.float32), adaptive[6], adaptive[7])
     velocity = jnp.dot(final_norm, w_proj, preferred_element_type=jnp.float32)

time: 534 us -> 497 us (0.931)
  Pallas kernels: 138 us -> 95.9 us
    pallas_call x2 -> x1, Pallas kernels: 125 us -> 17.2 us  [scatter_sum(): pl.pallas_call(functools.partial(scatter_sum_kernel, axis, count, rows),...]
    pallas_call x0 -> x1, Pallas kernels: none -> 65.9 us  [ring_scatter_sum(): pl.pallas_call(functools.partial(ring_scatter_kernel, zs, xs), out_shape=...]
where the time goes in v4:
time: 497 us; the launch traced here: 494 us
  waiting for transfers between devices  306 us (62%)
  Pallas kernels  95.9 us (19%)
  matrix products  22.1 us (4%)
  other arithmetic  19.9 us (4%)
  between operations  18.2 us (4%)
  local copies, waits for them, and re-layouts  17.5 us (4%)
  starting transfers between devices  14.5 us (3%)
    all_gather x1, waiting for transfers between devices, shards(): gathered = lax.all_gather(both, 'row', axis=0, tiled=True)  108 us
    all_gather x1, waiting for transfers between devices, shards(): gathered_half = lax.all_gather(own_half, 'row', axis=1, tiled=True)  95.3 us
    all_gather x1, waiting for transfers between devices, shards(): lax.all_gather(second_norm, 'row', axis=0, tiled=True)  72.1 us
    pallas_call x1, Pallas kernels, ring_scatter_sum(): pl.pallas_call(functools.partial(ring_scatter_kernel, zs, xs), out_shape=...  65.9 us
    all_gather x1, waiting for transfers between devices, shards(): lax.all_gather(gathered_half, 'req', axis=2, tiled=True)  28.7 us
    pallas_call x1, Pallas kernels, scatter_sum(): pl.pallas_call(functools.partial(scatter_sum_kernel, axis, count, rows),...  17.2 us
    pallas_call x1, Pallas kernels, attention(): pl.pallas_call(functools.partial(attention_kernel, scale), out_shape=jax....  12.8 us
    dot_general x1, matrix products, shards(): jnp.dot(hidden_units, w_down, preferred_element_type=jnp.float32)  10.4 us
  transfers between devices with their start and end apart: 8, of which 6 were waited for; matrix products, arithmetic and copies ran while one was open for 4% of the time, Pallas kernels for 0%

profile of v4, /device:TPU:2, one launch (start us, length us, event | category | flops | bytes accessed | tf_op | source)
XLA Modules:
  0.0 494.5 jit_solution(212962933114394850)
XLA Ops:
  7.2 1.8 constant_dynamic-slice_fusion
  9.1 95.3 %all-gather.6.cloned.1.call-done = bf16[3,3072,384]{2,1,0:T(8,128)(2,1)} async-done(((bf16[3,96,384]{2,1,0:T(8,128)(2,1)}), bf16[3,3072,384]{2,1,0:T(8,128)(2,1)}) %all-gather.6.cloned.1.call-update) | async-done | bytes 7077904 | tf_op jit(solution)/shard_map/all_gather | solution.py:375
  104.4 0.6 copy-done.17
  105.3 0.2 fusion.57
  105.5 0.2 convert_reduce_fusion
  105.6 0.3 multiply_reduce_fusion
  106.0 0.7 slice_add_fusion
  106.7 0.7 fusion.60
  107.4 0.3 add_convert_fusion
  107.7 28.7 %all-gather.8.cloned.1.call-done = bf16[3,3072,768]{2,1,0:T(8,128)(2,1)} async-done(((bf16[3,3072,384]{2,1,0:T(8,128)(2,1)}), bf16[3,3072,768]{2,1,0:T(8,128)(2,1)}) %all-gather.8.cloned.1.call-update) | async-done | bytes 14155792 | tf_op jit(solution)/shard_map/all_gather | solution.py:376
  136.4 7.0 %fusion.20 = f32[3,768,100]{1,2,0:T(8,128)S(1)} fusion(bf16[3,3072,768]{2,1,0:T(8,128)(2,1)} %all-gather.8.cloned.1.call-done, bf16[4,3072]{1,0:T(4,128)(2,1)} %fusion.60, bf16[96,3072]{1,0:T(8,128)(2,1)S(1)} %add_convert_fusion), kind=kOutput, calls=%fused_computation.32 | convolution fusion | flops 1416806400 | bytes 15691776 | tf_op jit(solution)/shard_map/gld,cde->cgle/dot_general | solution.py:309
  143.4 0.9 copy-done.2
  144.3 0.7 slice.173
  145.1 1.1 copy.38
  146.4 0.9 copy.41
  147.3 0.9 copy.39
  148.2 1.0 fusion.48
  149.2 1.2 fusion.37
  150.4 0.8 fusion.28
  151.2 0.2 all-gather.10.cloned.1.call-start
  151.5 1.2 convert_element_type.103
  152.7 0.6 select_reduce_fusion.5
  153.4 0.2 slice_reduce_fusion.2
  153.6 0.7 fusion.128
  154.3 2.8 select_convert_fusion.live_ref
  157.1 1.6 copy.33
  158.6 0.8 fusion.145
  159.6 0.2 copy.36
  159.8 0.9 copy.35
  160.6 0.9 copy.34
  161.5 1.8 multiply_convert_fusion.q_ref
  163.3 107.8 %all-gather.12.cloned.1.call-done = bf16[64,128,768]{2,1,0:T(8,128)(2,1)} async-done(((bf16[2,128,768]{2,1,0:T(8,128)(2,1)}), bf16[64,128,768]{2,1,0:T(8,128)(2,1)}) %all-gather.12.cloned.1.call-update) | async-done | bytes 12582928 | tf_op jit(solution)/shard_map/all_gather | solution.py:388
  271.1 12.8 %shard_map.166 = bf16[96,768]{1,0:T(8,128)(2,1)} custom-call(bf16[96,768]{1,0:T(8,128)(2,1)} %multiply_convert_fusion.q_ref, bf16[32,2,128,768]{3,2,1,0:T(8,128)(2,1)} %bitcast.161, f32[1,4096]{1,0:T(1,128)} %select_convert_fusion.live_ref), custom_call_target="tpu_custom_call" | custom-call | tf_op jit(solution)/shard_map/pallas_call | solution.py:130
  283.9 1.8 fusion.149.part_ref
  285.7 17.2 %shard_map.167 = f32[24,3072]{1,0:T(8,128)S(1)} custom-call(f32[96,3072]{1,0:T(8,128)S(1)} %fusion.149.part_ref), custom_call_target="tpu_custom_call" | custom-call | tf_op jit(solution)/shard_map/pallas_call | solution.py:89
  303.0 1.0 fusion.47
  304.1 0.2 fusion.38
  304.4 0.8 fusion.41
  305.3 0.3 reduce-window.9
  305.7 0.6 select_reduce_fusion.4
  307.1 1.3 select_reduce_fusion
  311.3 0.6 select_reduce_fusion.2
  312.5 0.7 and_convert_fusion
  313.1 72.1 %all-gather.10.cloned.1.call-done = bf16[768,3072]{1,0:T(8,128)(2,1)} async-done(((bf16[24,3072]{1,0:T(8,128)(2,1)}), bf16[768,3072]{1,0:T(8,128)(2,1)}) %all-gather.10.cloned.1.call-update) | async-done | bytes 4718608 | tf_op jit(solution)/shard_map/all_gather | solution.py:407
  385.3 10.4 %convolution_convert_fusion = bf16[768,3072]{1,0:T(8,128)(2,1)} fusion(bf16[384,3072]{1,0:T(8,128)(2,1)S(1)} %copy-done, bf16[768,3072]{1,0:T(8,128)(2,1)} %all-gather.10.cloned.1.call-done, bf16[3072,384]{1,0:T(8,128)(2,1)} %param.25), kind=kOutput, calls=%fused_computation | convolution fusion | flops 3628892160 | bytes 14155776 | tf_op jit(solution)/shard_map/dot_general | solution.py:413
  395.7 4.9 copy.55
  400.6 65.9 %shard_map.168 = f32[24,3072]{1,0:T(8,128)} custom-call(bf16[8,4,24,3072]{3,2,1,0:T(8,128)(2,1)} %bitcast.160), custom_call_target="tpu_custom_call" | custom-call | tf_op jit(solution)/shard_map/pallas_call | solution.py:231
  466.6 1.2 convert_reduce_fusion.2
  467.7 0.2 fusion.42
  468.0 0.9 multiply_convert_fusion.1
  469.1 0.3 copy.44
  469.4 3.9 collective-permute-start
  473.3 4.4 collective-permute-start.1
  477.8 1.2 collective-permute-done.1
  479.1 1.3 collective-permute-start.3
  480.4 4.5 collective-permute-start.2
  485.1 0.2 fusion.65
  485.2 1.1 collective-permute-done.2
  486.3 0.1 fusion.80
  486.5 0.2 fusion.71
  486.7 0.2 fusion.88
  486.8 0.2 fusion.69
  487.0 0.2 fusion.13
  487.1 0.8 fusion.15
  (96 shorter events, 2.0 us)
Async XLA Ops:
  7.2 378.1 %copy-start = (bf16[384,3072]{1,0:T(8,128)(2,1)S(1)}, bf16[384,3072]{1,0:T(8,128)(2,1)}, u32[]{:S(2)}) copy-start(bf16[384,3072]{1,0:T(8,128)(2,1)} %param.26) | copy-start | bytes 7077892
  7.2 97.2 %all-gather.6.cloned.1.call-start = ((), (), s32[]{:S(2)}) async-start(), calls=%async_computation | async-start | bytes 7299072 | tf_op jit(solution)/shard_map/all_gather | solution.py:375
  9.0 127.3 %all-gather.8.cloned.1.call-start = ((), (), s32[]{:S(2)}) async-start(), calls=%async_computation.1 | async-start | bytes 21233664 | tf_op jit(solution)/shard_map/all_gather | solution.py:376
  104.4 0.7 copy-start.17
  104.4 0.8 copy-start.5
  104.4 1.1 copy-start.1
  104.4 1.6 copy-start.7
  104.4 166.7 %all-gather.12.cloned.1.call-start = ((), (), s32[]{:S(2)}) async-start(), calls=%async_computation.3 | async-start | bytes 12976128 | tf_op jit(solution)/shard_map/all_gather | solution.py:388
  143.4 0.9 copy-start.2
  151.2 1.5 copy-start.18
  151.2 1.5 copy-start.21
  151.2 2.2 copy-start.16
  151.2 234.0 %all-gather.10.cloned.1.call-start = ((), (), s32[]{:S(2)}) async-start(), calls=%async_computation.2 | async-start | bytes 4866048 | tf_op jit(solution)/shard_map/all_gather | solution.py:407
  153.6 0.7 copy-start.14
  159.5 1.1 copy-start.3
  161.5 122.4 %slice-start = ((s8[4718592]{0:T(1024)(128)(4,1)}), s8[524288]{0:T(1024)(128)(4,1)S(1)}, s32[]{:S(2)}) async-start(s8[4718592]{0:T(1024)(128)(4,1)} %bitcast.162), calls=%async_computation.4 | async-start | bytes 1048576
  271.1 12.8 %slice-start.1 = ((s8[4718592]{0:T(1024)(128)(4,1)}), s8[4194304]{0:T(1024)(128)(4,1)S(1)}, s32[]{:S(2)}) async-start(s8[4718592]{0:T(1024)(128)(4,1)} %bitcast.162), calls=%async_computation.5 | async-start | bytes 8388608
  285.7 17.3 %copy-start.11 = (f32[1,1,3072]{2,1,0:T(1,128)S(1)}, f32[1,1,3072]{2,1,0:T(1,128)}, u32[]{:S(2)}) copy-start(f32[1,1,3072]{2,1,0:T(1,128)} %get-tuple-element.17) | copy-start | bytes 36868
  285.7 18.7 %copy-start.8 = (f32[1,1,3072]{2,1,0:T(1,128)S(1)}, f32[1,1,3072]{2,1,0:T(1,128)}, u32[]{:S(2)}) copy-start(f32[1,1,3072]{2,1,0:T(1,128)} %get-tuple-element.12) | copy-start | bytes 36868
  285.7 18.7 %copy-start.9 = (f32[1,1,3072]{2,1,0:T(1,128)S(1)}, f32[1,1,3072]{2,1,0:T(1,128)}, u32[]{:S(2)}) copy-start(f32[1,1,3072]{2,1,0:T(1,128)} %get-tuple-element.13) | copy-start | bytes 36868
  285.7 20.0 %copy-start.22 = (s32[2]{0:T(128)S(1)}, s32[2]{0:T(128)}, u32[]{:S(2)}) copy-start(s32[2]{0:T(128)} %param.19) | copy-start | bytes 28
  303.0 8.3 %copy-start.15 = (s32[2]{0:T(128)S(1)}, s32[2]{0:T(128)}, u32[]{:S(2)}) copy-start(s32[2]{0:T(128)} %copy-done.14) | copy-start | bytes 28
  400.6 66.0 %copy-start.10 = (f32[1,1,3072]{2,1,0:T(1,128)S(1)}, f32[1,1,3072]{2,1,0:T(1,128)}, u32[]{:S(2)}) copy-start(f32[1,1,3072]{2,1,0:T(1,128)} %get-tuple-element.14) | copy-start | bytes 36868
  400.6 67.4 %copy-start.12 = (f32[1,1,3072]{2,1,0:T(1,128)S(1)}, f32[1,1,3072]{2,1,0:T(1,128)}, u32[]{:S(2)}) copy-start(f32[1,1,3072]{2,1,0:T(1,128)} %get-tuple-element.11) | copy-start | bytes 36868
  400.6 67.4 %copy-start.13 = (f32[1,1,3072]{2,1,0:T(1,128)S(1)}, f32[1,1,3072]{2,1,0:T(1,128)}, u32[]{:S(2)}) copy-start(f32[1,1,3072]{2,1,0:T(1,128)} %get-tuple-element.18) | copy-start | bytes 36868
  400.6 67.4 %copy-start.19 = (bf16[3072,64]{0,1:T(8,128)(2,1)S(1)}, bf16[3072,64]{0,1:T(8,128)(2,1)}, u32[]{:S(2)}) copy-start(bf16[3072,64]{0,1:T(8,128)(2,1)} %param.27) | copy-start | bytes 1179652
  400.6 67.4 %copy-start.20 = (f32[1,24,64]{2,1,0:T(8,128)S(1)}, f32[1,24,64]{2,1,0:T(8,128)}, u32[]{:S(2)}) copy-start(f32[1,24,64]{2,1,0:T(8,128)} %param.28) | copy-start | bytes 18436
  466.5 11.2 %copy-start.6 = (bf16[3,3,16,512]{3,2,1,0:T(8,128)(2,1)S(1)}, bf16[3,3,16,512]{3,2,1,0:T(8,128)(2,1)}, u32[]{:S(2)}) copy-start(bf16[3,3,16,512]{3,2,1,0:T(8,128)(2,1)} %param.29) | copy-start | bytes 442372
  467.7 18.9 %copy-start.4 = (bf16[24,3072]{1,0:T(8,128)(2,1)}, bf16[24,3072]{1,0:T(8,128)(2,1)S(1)}, u32[]{:S(2)}) copy-start(bf16[24,3072]{1,0:T(8,128)(2,1)S(1)} %get-tuple-element.8) | copy-start | bytes 442372
  469.4 8.4 %collective-permute-start = (bf16[6,1,8,16]{3,2,1,0:T(8,128)(2,1)S(1)}, bf16[6,1,8,16]{3,2,1,0:T(8,128)(2,1)S(1)}, u32[]{:S(2)}, u32[]{:S(2)}) collective-permute-start(bf16[6,1,8,16]{3,2,1,0:T(8,128)(2,1)S(1)} %get-tuple-element.21), channel_id=1, source_target_pairs={{0,4},{4,8},{8,12},{12,16},{16,20},{20,24},{24,28},{28,32},{32,36}... | collective-permute-start | bytes 4616 | tf_op jit(solution)/shard_map/ppermute | solution.py:31
  473.3 5.8 %collective-permute-start.1 = (bf16[6,1,8,16]{3,2,1,0:T(8,128)(2,1)S(1)}, bf16[6,1,8,16]{3,2,1,0:T(8,128)(2,1)S(1)}, u32[]{:S(2)}, u32[]{:S(2)}) collective-permute-start(bf16[6,1,8,16]{3,2,1,0:T(8,128)(2,1)S(1)} %get-tuple-element.22), channel_id=1, source_target_pairs={{4,0},{8,4},{12,8},{16,12},{20,16},{24,20},{28,24},{32,28},{36,32}... | collective-permute-start | bytes 4616 | tf_op jit(solution)/shard_map/ppermute | solution.py:33
  479.1 7.6 %collective-permute-start.3 = (bf16[6,4,1,16]{3,2,1,0:T(2,128)(2,1)S(1)}, bf16[6,4,1,16]{3,2,1,0:T(2,128)(2,1)S(1)}, u32[]{:S(2)}, u32[]{:S(2)}) collective-permute-start(bf16[6,4,1,16]{3,2,1,0:T(2,128)(2,1)S(1)} %get-tuple-element.20), channel_id=1, source_target_pairs={{1,0},{2,1},{3,2},{5,4},{6,5},{7,6},{9,8},{10,9},{11,10},{13,12},{... | collective-permute-start | bytes 2312 | tf_op jit(solution)/shard_map/ppermute | solution.py:33
  480.4 5.9 %collective-permute-start.2 = (bf16[6,4,1,16]{3,2,1,0:T(2,128)(2,1)S(1)}, bf16[6,4,1,16]{3,2,1,0:T(2,128)(2,1)S(1)}, u32[]{:S(2)}, u32[]{:S(2)}) collective-permute-start(bf16[6,4,1,16]{3,2,1,0:T(2,128)(2,1)S(1)} %get-tuple-element.19), channel_id=1, source_target_pairs={{0,1},{1,2},{2,3},{4,5},{5,6},{6,7},{8,9},{9,10},{10,11},{12,13},{... | collective-permute-start | bytes 2312 | tf_op jit(solution)/shard_map/ppermute | solution.py:31
Sparse Core Ops, SparseCore 0:
  10.6 93.6 all-gather.5
  106.2 30.1 all-gather.7
  151.4 119.6 all-gather.11
  305.3 79.9 all-gather.9

commit v5 on v4

--- a/solution.py
+++ b/solution.py
@@ -227,7 +227,7 @@
 def ring_scatter_sum(part, xs, zs, kernel_id):
     rows = part.shape[0] // (xs * zs)
     width = part.shape[1]
-    arranged = part.reshape(xs, zs, rows, width).transpose(1, 0, 2, 3)
+    arranged = part.reshape(zs, xs, rows, width)
     return pl.pallas_call(
         functools.partial(ring_scatter_kernel, zs, xs),
         out_shape=jax.ShapeDtypeStruct((rows, width), jnp.float32),
@@ -247,6 +247,95 @@
             collective_id=kernel_id, has_side_effects=True, vmem_limit_bytes=56 * 1024 * 1024
         ),
     )(arranged)
+
+
+def ring_gather_kernel(zs, xs, block_ref, out_ref, held, own_sem, ring_send, ring_recv, cross_send, cross_recv):
+    me = lax.axis_index("row")
+    xm = me // zs
+    zm = me % zs
+    ahead = xm * zs + lax.rem(zm + 1, zs)
+    behind = xm * zs + lax.rem(zm + zs - 1, zs)
+    barrier = pltpu.get_barrier_semaphore()
+    targets = [ahead, behind] + [lax.rem(xm + k, xs) * zs + zm for k in range(1, xs)]
+    for peer in targets:
+        pl.semaphore_signal(barrier, inc=1, device_id=peer_on("row", peer), device_id_type=MESH_IDS)
+    pl.semaphore_wait(barrier, len(targets))
+    own = pltpu.make_async_copy(block_ref, held.at[zm, xm], own_sem)
+    own.start()
+    pending = []
+    for k in range(1, xs):
+        peer_x = lax.rem(xm + k, xs)
+        copy = pltpu.make_async_remote_copy(
+            src_ref=block_ref,
+            dst_ref=held.at[zm, xm],
+            send_sem=cross_send.at[k],
+            recv_sem=cross_recv.at[k],
+            device_id=peer_on("row", peer_x * zs + zm),
+            device_id_type=MESH_IDS,
+        )
+        copy.start()
+        pending.append(copy)
+    own.wait()
+    for k in range(1, xs):
+        origin_x = lax.rem(xm + xs - k, xs)
+        pltpu.make_async_remote_copy(
+            src_ref=block_ref,
+            dst_ref=held.at[zm, origin_x],
+            send_sem=cross_send.at[k],
+            recv_sem=cross_recv.at[k],
+            device_id=peer_on("row", origin_x * zs + zm),
+            device_id_type=MESH_IDS,
+        ).wait_recv()
+    split = xs // 2
+    ways = ((0, ahead, behind, -1, pl.ds(0, split)), (1, behind, ahead, 1, pl.ds(split, xs - split)))
+    for step in range(zs):
+        for way, dest, origin, sign, part in ways:
+            group = lax.rem(zm + sign * step + zs, zs)
+            if step > 0:
+                pltpu.make_async_remote_copy(
+                    src_ref=held.at[group, part],
+                    dst_ref=held.at[group, part],
+                    send_sem=ring_send.at[way, step - 1],
+                    recv_sem=ring_recv.at[way, step - 1],
+                    device_id=peer_on("row", origin),
+                    device_id_type=MESH_IDS,
+                ).wait_recv()
+            if step < zs - 1:
+                copy = pltpu.make_async_remote_copy(
+                    src_ref=held.at[group, part],
+                    dst_ref=held.at[group, part],
+                    send_sem=ring_send.at[way, step],
+                    recv_sem=ring_recv.at[way, step],
+                    device_id=peer_on("row", dest),
+                    device_id_type=MESH_IDS,
+                )
+                copy.start()
+                pending.append(copy)
+    for copy in pending:
+        copy.wait_send()
+    out = pltpu.make_async_copy(held, out_ref, own_sem)
+    out.start()
+    out.wait()
+
+
+def ring_gather(block, xs, zs, kernel_id):
+    return pl.pallas_call(
+        functools.partial(ring_gather_kernel, zs, xs),
+        out_shape=jax.ShapeDtypeStruct((zs, xs) + block.shape, block.dtype),
+        in_specs=[pl.BlockSpec(memory_space=pltpu.VMEM)],
+        out_specs=pl.BlockSpec(memory_space=pl.ANY),
+        scratch_shapes=[
+            pltpu.VMEM((zs, xs) + block.shape, block.dtype),
+            pltpu.SemaphoreType.DMA(()),
+            pltpu.SemaphoreType.DMA((2, zs - 1)),
+            pltpu.SemaphoreType.DMA((2, zs - 1)),
+            pltpu.SemaphoreType.DMA((xs,)),
+            pltpu.SemaphoreType.DMA((xs,)),
+        ],
+        compiler_params=pltpu.CompilerParams(
+            collective_id=kernel_id, has_side_effects=True, vmem_limit_bytes=56 * 1024 * 1024
+        ),
+    )(block)
 
 
 def layer_norm(tensor, epsilon):
@@ -404,7 +493,7 @@
     second_norm = modulate(mixed, adaptive[3], adaptive[4])
     hidden_units = jax.nn.gelu(
         jnp.dot(
-            lax.all_gather(second_norm, "row", axis=0, tiled=True),
+            ring_gather(second_norm, 4, 8, 2).reshape(-1, second_norm.shape[1]),
             w_up,
             preferred_element_type=jnp.float32,
         ),

time: 497 us -> 481 us (0.968)
  waiting for transfers between devices: 306 us -> 226 us
  Pallas kernels: 95.9 us -> 164 us
    all_gather x1 -> x0, waiting for transfers between devices: 72.1 us -> none  [shards(): lax.all_gather(second_norm, 'row', axis=0, tiled=True)]
    pallas_call x0 -> x1, Pallas kernels: none -> 66.2 us  [ring_gather(): pl.pallas_call(functools.partial(ring_gather_kernel, zs, xs), out_shape=j...]
    all_gather x1, waiting for transfers between devices: 108 us -> 100 us  [shards(): gathered = lax.all_gather(both, 'row', axis=0, tiled=True)]
  transfers between devices with their start and end apart: 8 -> 7, of which waited for: 6 -> 5; matrix products, arithmetic and copies ran while one was open for 4% -> 4% of each run, Pallas kernels for 0% -> 0%
where the time goes in v5:
time: 481 us; the launch traced here: 478 us
  waiting for transfers between devices  226 us (47%)
  Pallas kernels  164 us (34%)
  matrix products  22.1 us (5%)
  other arithmetic  19.9 us (4%)
  between operations  18.3 us (4%)
  starting transfers between devices  14.9 us (3%)
  local copies, waits for them, and re-layouts  12.7 us (3%)
    all_gather x1, waiting for transfers between devices, shards(): gathered = lax.all_gather(both, 'row', axis=0, tiled=True)  100 us
    all_gather x1, waiting for transfers between devices, shards(): gathered_half = lax.all_gather(own_half, 'row', axis=1, tiled=True)  95.3 us
    pallas_call x1, Pallas kernels, ring_scatter_sum(): pl.pallas_call(functools.partial(ring_scatter_kernel, zs, xs), out_shape=...  67.4 us
    pallas_call x1, Pallas kernels, ring_gather(): pl.pallas_call(functools.partial(ring_gather_kernel, zs, xs), out_shape=j...  66.2 us
    all_gather x1, waiting for transfers between devices, shards(): lax.all_gather(gathered_half, 'req', axis=2, tiled=True)  28.7 us
    pallas_call x1, Pallas kernels, scatter_sum(): pl.pallas_call(functools.partial(scatter_sum_kernel, axis, count, rows),...  17.2 us
    pallas_call x1, Pallas kernels, attention(): pl.pallas_call(functools.partial(attention_kernel, scale), out_shape=jax....  13 us
    dot_general x1, matrix products, shards(): jnp.dot(hidden_units, w_down, preferred_element_type=jnp.float32)  10.4 us
  transfers between devices with their start and end apart: 7, of which 5 were waited for; matrix products, arithmetic and copies ran while one was open for 4% of the time, Pallas kernels for 0%

profile of v5, /device:TPU:2, one launch (start us, length us, event | category | flops | bytes accessed | tf_op | source)
XLA Modules:
  0.0 478.1 jit_solution(13290869338221949970)
XLA Ops:
  7.2 1.8 constant_dynamic-slice_fusion
  9.1 95.3 %all-gather.5.cloned.1.call-done = bf16[3,3072,384]{2,1,0:T(8,128)(2,1)} async-done(((bf16[3,96,384]{2,1,0:T(8,128)(2,1)}), bf16[3,3072,384]{2,1,0:T(8,128)(2,1)}) %all-gather.5.cloned.1.call-update) | async-done | bytes 7077904 | tf_op jit(solution)/shard_map/all_gather | solution.py:464
  104.4 0.6 copy-done.15
  105.3 0.2 fusion.57
  105.5 0.2 convert_reduce_fusion
  105.6 0.3 multiply_reduce_fusion
  106.0 0.7 slice_add_fusion
  106.7 0.7 fusion.60
  107.4 0.3 add_convert_fusion
  107.7 28.7 %all-gather.7.cloned.1.call-done = bf16[3,3072,768]{2,1,0:T(8,128)(2,1)} async-done(((bf16[3,3072,384]{2,1,0:T(8,128)(2,1)}), bf16[3,3072,768]{2,1,0:T(8,128)(2,1)}) %all-gather.7.cloned.1.call-update) | async-done | bytes 14155792 | tf_op jit(solution)/shard_map/all_gather | solution.py:465
  136.4 7.0 %fusion.20 = f32[3,768,100]{1,2,0:T(8,128)S(1)} fusion(bf16[3,3072,768]{2,1,0:T(8,128)(2,1)} %all-gather.7.cloned.1.call-done, bf16[4,3072]{1,0:T(4,128)(2,1)} %fusion.60, bf16[96,3072]{1,0:T(8,128)(2,1)S(1)} %add_convert_fusion), kind=kOutput, calls=%fused_computation.31 | convolution fusion | flops 1416806400 | bytes 15691776 | tf_op jit(solution)/shard_map/gld,cde->cgle/dot_general | solution.py:398
  143.4 0.9 copy-done.2
  144.3 0.7 slice.173
  145.1 1.1 copy.37
  146.4 0.9 copy.40
  147.3 0.9 copy.38
  148.2 1.0 fusion.48
  149.2 1.2 fusion.37
  150.4 0.8 fusion.28
  151.2 1.2 convert_element_type.103
  152.5 0.3 reduce-window.9
  152.9 0.6 select_reduce_fusion.4
  154.4 1.3 select_reduce_fusion
  158.5 0.2 slice_reduce_fusion.2
  158.7 0.6 select_reduce_fusion.2
  160.0 0.7 and_convert_fusion
  160.7 0.6 select_reduce_fusion.5
  161.3 0.7 fusion.128
  162.0 2.8 select_convert_fusion.live_ref
  164.8 1.6 copy.32
  166.4 0.8 fusion.145
  167.3 0.2 copy.35
  167.5 0.9 copy.34
  168.4 0.9 copy.33
  169.3 1.8 multiply_convert_fusion.q_ref
  171.1 100.0 %all-gather.9.cloned.1.call-done = bf16[64,128,768]{2,1,0:T(8,128)(2,1)} async-done(((bf16[2,128,768]{2,1,0:T(8,128)(2,1)}), bf16[64,128,768]{2,1,0:T(8,128)(2,1)}) %all-gather.9.cloned.1.call-update) | async-done | bytes 12582928 | tf_op jit(solution)/shard_map/all_gather | solution.py:477
  271.1 13.0 %shard_map.166 = bf16[96,768]{1,0:T(8,128)(2,1)} custom-call(bf16[96,768]{1,0:T(8,128)(2,1)} %multiply_convert_fusion.q_ref, bf16[32,2,128,768]{3,2,1,0:T(8,128)(2,1)} %bitcast.158, f32[1,4096]{1,0:T(1,128)} %select_convert_fusion.live_ref), custom_call_target="tpu_custom_call" | custom-call | tf_op jit(solution)/shard_map/pallas_call | solution.py:130
  284.1 1.8 fusion.149.part_ref
  285.9 17.2 %shard_map.167 = f32[24,3072]{1,0:T(8,128)S(1)} custom-call(f32[96,3072]{1,0:T(8,128)S(1)} %fusion.149.part_ref), custom_call_target="tpu_custom_call" | custom-call | tf_op jit(solution)/shard_map/pallas_call | solution.py:89
  303.2 1.0 fusion.47
  304.3 0.2 fusion.38
  304.6 0.8 fusion.41.block_ref
  305.4 66.2 %shard_map.168 = bf16[8,4,24,3072]{3,2,1,0:T(8,128)(2,1)} custom-call(bf16[24,3072]{1,0:T(8,128)(2,1)} %fusion.41.block_ref), custom_call_target="tpu_custom_call" | custom-call | tf_op jit(solution)/shard_map/pallas_call | solution.py:322
  371.6 10.4 %convolution_convert_fusion = bf16[768,3072]{1,0:T(8,128)(2,1)} fusion(bf16[384,3072]{1,0:T(8,128)(2,1)S(1)} %copy-done, bf16[768,3072]{1,0:T(8,128)(2,1)} %bitcast.161, bf16[3072,384]{1,0:T(8,128)(2,1)} %param.25), kind=kOutput, calls=%fused_computation | convolution fusion | flops 3628892160 | bytes 14155776 | tf_op jit(solution)/shard_map/dot_general | solution.py:502
  382.0 67.4 %shard_map.169 = f32[24,3072]{1,0:T(8,128)} custom-call(bf16[8,4,24,3072]{3,2,1,0:T(8,128)(2,1)} %bitcast.162), custom_call_target="tpu_custom_call" | custom-call | tf_op jit(solution)/shard_map/pallas_call | solution.py:231
  449.4 1.2 convert_reduce_fusion.2
  450.6 0.2 fusion.42
  450.9 0.9 multiply_convert_fusion.1
  452.0 0.3 copy.42
  452.3 2.4 collective-permute-start
  454.7 5.5 %collective-permute-start.1 = (bf16[6,1,8,16]{3,2,1,0:T(8,128)(2,1)S(1)}, bf16[6,1,8,16]{3,2,1,0:T(8,128)(2,1)S(1)}, u32[]{:S(2)}, u32[]{:S(2)}) collective-permute-start(bf16[6,1,8,16]{3,2,1,0:T(8,128)(2,1)S(1)} %get-tuple-element.22), channel_id=1, source_target_pairs={{4,0},{8,4},{12,8},{16,12},{20,16},{24,20},{28,24},{32,28},{36,32}... | collective-permute-start | bytes 4616 | tf_op jit(solution)/shard_map/ppermute | solution.py:33
  460.2 0.1 fusion.109
  460.4 1.2 collective-permute-done.1
  461.6 1.3 collective-permute-start.3
  462.9 5.6 %collective-permute-start.2 = (bf16[6,4,1,16]{3,2,1,0:T(2,128)(2,1)S(1)}, bf16[6,4,1,16]{3,2,1,0:T(2,128)(2,1)S(1)}, u32[]{:S(2)}, u32[]{:S(2)}) collective-permute-start(bf16[6,4,1,16]{3,2,1,0:T(2,128)(2,1)S(1)} %get-tuple-element.19), channel_id=1, source_target_pairs={{0,1},{1,2},{2,3},{4,5},{5,6},{6,7},{8,9},{9,10},{10,11},{12,13},{... | collective-permute-start | bytes 2312 | tf_op jit(solution)/shard_map/ppermute | solution.py:31
  468.5 0.1 fusion.61
  468.7 0.2 fusion.65
  468.8 1.1 collective-permute-done.2
  469.9 0.1 fusion.80
  470.1 0.2 fusion.71
  470.2 0.1 fusion.88
  470.4 0.2 fusion.69
  470.5 0.2 fusion.13
  470.7 0.8 fusion.15
  (89 shorter events, 1.7 us)
Async XLA Ops:
  7.2 364.4 %copy-start = (bf16[384,3072]{1,0:T(8,128)(2,1)S(1)}, bf16[384,3072]{1,0:T(8,128)(2,1)}, u32[]{:S(2)}) copy-start(bf16[384,3072]{1,0:T(8,128)(2,1)} %param.26) | copy-start | bytes 7077892
  7.2 97.2 %all-gather.5.cloned.1.call-start = ((), (), s32[]{:S(2)}) async-start(), calls=%async_computation | async-start | bytes 7299072 | tf_op jit(solution)/shard_map/all_gather | solution.py:464
  9.0 127.3 %all-gather.7.cloned.1.call-start = ((), (), s32[]{:S(2)}) async-start(), calls=%async_computation.1 | async-start | bytes 21233664 | tf_op jit(solution)/shard_map/all_gather | solution.py:465
  104.4 0.7 copy-start.15
  104.4 0.8 copy-start.5
  104.4 1.1 copy-start.1
  104.4 1.6 copy-start.7
  104.4 166.7 %all-gather.9.cloned.1.call-start = ((), (), s32[]{:S(2)}) async-start(), calls=%async_computation.2 | async-start | bytes 12976128 | tf_op jit(solution)/shard_map/all_gather | solution.py:477
  143.4 0.9 copy-start.2
  151.2 1.7 copy-start.19
  151.2 7.2 %copy-start.16 = (f32[64]{0:T(128)S(1)}, f32[64]{0:T(128)}, u32[]{:S(2)}) copy-start(f32[64]{0:T(128)} %param.21) | copy-start | bytes 772
  151.2 7.3 %copy-start.14 = (s32[2,2]{1,0:T(2,128)S(1)}, s32[2,2]{1,0:T(2,128)}, u32[]{:S(2)}) copy-start(s32[2,2]{1,0:T(2,128)} %param.18) | copy-start | bytes 52
  151.2 9.4 %copy-start.20 = (s32[2]{0:T(128)S(1)}, s32[2]{0:T(128)}, u32[]{:S(2)}) copy-start(s32[2]{0:T(128)} %param.17) | copy-start | bytes 28
  167.3 1.1 copy-start.3
  169.3 114.8 %slice-start = ((s8[4718592]{0:T(1024)(128)(4,1)}), s8[524288]{0:T(1024)(128)(4,1)S(1)}, s32[]{:S(2)}) async-start(s8[4718592]{0:T(1024)(128)(4,1)} %bitcast.159), calls=%async_computation.3 | async-start | bytes 1048576
  271.1 13.0 %slice-start.1 = ((s8[4718592]{0:T(1024)(128)(4,1)}), s8[4194304]{0:T(1024)(128)(4,1)S(1)}, s32[]{:S(2)}) async-start(s8[4718592]{0:T(1024)(128)(4,1)} %bitcast.159), calls=%async_computation.4 | async-start | bytes 8388608
  285.9 17.3 %copy-start.11 = (f32[1,1,3072]{2,1,0:T(1,128)S(1)}, f32[1,1,3072]{2,1,0:T(1,128)}, u32[]{:S(2)}) copy-start(f32[1,1,3072]{2,1,0:T(1,128)} %get-tuple-element.17) | copy-start | bytes 36868
  285.9 18.7 %copy-start.8 = (f32[1,1,3072]{2,1,0:T(1,128)S(1)}, f32[1,1,3072]{2,1,0:T(1,128)}, u32[]{:S(2)}) copy-start(f32[1,1,3072]{2,1,0:T(1,128)} %get-tuple-element.12) | copy-start | bytes 36868
  285.9 18.7 %copy-start.9 = (f32[1,1,3072]{2,1,0:T(1,128)S(1)}, f32[1,1,3072]{2,1,0:T(1,128)}, u32[]{:S(2)}) copy-start(f32[1,1,3072]{2,1,0:T(1,128)} %get-tuple-element.13) | copy-start | bytes 36868
  381.9 67.5 %copy-start.10 = (f32[1,1,3072]{2,1,0:T(1,128)S(1)}, f32[1,1,3072]{2,1,0:T(1,128)}, u32[]{:S(2)}) copy-start(f32[1,1,3072]{2,1,0:T(1,128)} %get-tuple-element.14) | copy-start | bytes 36868
  381.9 68.9 %copy-start.12 = (f32[1,1,3072]{2,1,0:T(1,128)S(1)}, f32[1,1,3072]{2,1,0:T(1,128)}, u32[]{:S(2)}) copy-start(f32[1,1,3072]{2,1,0:T(1,128)} %get-tuple-element.11) | copy-start | bytes 36868
  381.9 68.9 %copy-start.13 = (f32[1,1,3072]{2,1,0:T(1,128)S(1)}, f32[1,1,3072]{2,1,0:T(1,128)}, u32[]{:S(2)}) copy-start(f32[1,1,3072]{2,1,0:T(1,128)} %get-tuple-element.18) | copy-start | bytes 36868
  381.9 68.9 %copy-start.17 = (bf16[3072,64]{0,1:T(8,128)(2,1)S(1)}, bf16[3072,64]{0,1:T(8,128)(2,1)}, u32[]{:S(2)}) copy-start(bf16[3072,64]{0,1:T(8,128)(2,1)} %param.27) | copy-start | bytes 1179652
  382.0 68.9 %copy-start.18 = (f32[1,24,64]{2,1,0:T(8,128)S(1)}, f32[1,24,64]{2,1,0:T(8,128)}, u32[]{:S(2)}) copy-start(f32[1,24,64]{2,1,0:T(8,128)} %param.28) | copy-start | bytes 18436
  449.4 10.8 %copy-start.6 = (bf16[3,3,16,512]{3,2,1,0:T(8,128)(2,1)S(1)}, bf16[3,3,16,512]{3,2,1,0:T(8,128)(2,1)}, u32[]{:S(2)}) copy-start(bf16[3,3,16,512]{3,2,1,0:T(8,128)(2,1)} %param.29) | copy-start | bytes 442372
  450.6 19.6 %copy-start.4 = (bf16[24,3072]{1,0:T(8,128)(2,1)}, bf16[24,3072]{1,0:T(8,128)(2,1)S(1)}, u32[]{:S(2)}) copy-start(bf16[24,3072]{1,0:T(8,128)(2,1)S(1)} %get-tuple-element.8) | copy-start | bytes 442372
  452.3 8.1 %collective-permute-start = (bf16[6,1,8,16]{3,2,1,0:T(8,128)(2,1)S(1)}, bf16[6,1,8,16]{3,2,1,0:T(8,128)(2,1)S(1)}, u32[]{:S(2)}, u32[]{:S(2)}) collective-permute-start(bf16[6,1,8,16]{3,2,1,0:T(8,128)(2,1)S(1)} %get-tuple-element.21), channel_id=1, source_target_pairs={{0,4},{4,8},{8,12},{12,16},{16,20},{20,24},{24,28},{28,32},{32,36}... | collective-permute-start | bytes 4616 | tf_op jit(solution)/shard_map/ppermute | solution.py:31
  454.7 6.9 %collective-permute-start.1 = (bf16[6,1,8,16]{3,2,1,0:T(8,128)(2,1)S(1)}, bf16[6,1,8,16]{3,2,1,0:T(8,128)(2,1)S(1)}, u32[]{:S(2)}, u32[]{:S(2)}) collective-permute-start(bf16[6,1,8,16]{3,2,1,0:T(8,128)(2,1)S(1)} %get-tuple-element.22), channel_id=1, source_target_pairs={{4,0},{8,4},{12,8},{16,12},{20,16},{24,20},{28,24},{32,28},{36,32}... | collective-permute-start | bytes 4616 | tf_op jit(solution)/shard_map/ppermute | solution.py:33
  461.6 8.6 %collective-permute-start.3 = (bf16[6,4,1,16]{3,2,1,0:T(2,128)(2,1)S(1)}, bf16[6,4,1,16]{3,2,1,0:T(2,128)(2,1)S(1)}, u32[]{:S(2)}, u32[]{:S(2)}) collective-permute-start(bf16[6,4,1,16]{3,2,1,0:T(2,128)(2,1)S(1)} %get-tuple-element.20), channel_id=1, source_target_pairs={{1,0},{2,1},{3,2},{5,4},{6,5},{7,6},{9,8},{10,9},{11,10},{13,12},{... | collective-permute-start | bytes 2312 | tf_op jit(solution)/shard_map/ppermute | solution.py:33
  462.9 7.0 %collective-permute-start.2 = (bf16[6,4,1,16]{3,2,1,0:T(2,128)(2,1)S(1)}, bf16[6,4,1,16]{3,2,1,0:T(2,128)(2,1)S(1)}, u32[]{:S(2)}, u32[]{:S(2)}) collective-permute-start(bf16[6,4,1,16]{3,2,1,0:T(2,128)(2,1)S(1)} %get-tuple-element.19), channel_id=1, source_target_pairs={{0,1},{1,2},{2,3},{4,5},{5,6},{6,7},{8,9},{9,10},{10,11},{12,13},{... | collective-permute-start | bytes 2312 | tf_op jit(solution)/shard_map/ppermute | solution.py:31
Sparse Core Ops, SparseCore 0:
  10.6 93.6 all-gather.4
  106.2 30.1 all-gather.6
  151.4 119.6 all-gather.8

commit v6 on v5

--- a/solution.py
+++ b/solution.py
@@ -338,6 +338,126 @@
     )(block)
 
 
+def device_at(**coords):
+    return tuple(coords.get(name, lax.axis_index(name)) for name in ("req", "row", "col"))
+
+
+def paired_gather_kernel(zs, xs, block_ref, out_ref, held, own_sem, ring_send, ring_recv, cross_send, cross_recv, pair_send, pair_recv):
+    me = lax.axis_index("row")
+    mine = lax.axis_index("req")
+    other = 1 - mine
+    xm = me // zs
+    zm = me % zs
+    ahead = xm * zs + lax.rem(zm + 1, zs)
+    behind = xm * zs + lax.rem(zm + zs - 1, zs)
+    barrier = pltpu.get_barrier_semaphore()
+    targets = [device_at(row=ahead), device_at(row=behind)]
+    targets += [device_at(row=lax.rem(xm + k, xs) * zs + zm) for k in range(1, xs)]
+    targets.append(device_at(req=other))
+    for peer in targets:
+        pl.semaphore_signal(barrier, inc=1, device_id=peer, device_id_type=MESH_IDS)
+    pl.semaphore_wait(barrier, len(targets))
+    own = pltpu.make_async_copy(block_ref, held.at[mine, zm, xm], own_sem)
+    own.start()
+    pending = []
+    for k in range(1, xs):
+        peer_x = lax.rem(xm + k, xs)
+        copy = pltpu.make_async_remote_copy(
+            src_ref=block_ref,
+            dst_ref=held.at[mine, zm, xm],
+            send_sem=cross_send.at[k],
+            recv_sem=cross_recv.at[k],
+            device_id=device_at(row=peer_x * zs + zm),
+            device_id_type=MESH_IDS,
+        )
+        copy.start()
+        pending.append(copy)
+    own.wait()
+    for k in range(1, xs):
+        origin_x = lax.rem(xm + xs - k, xs)
+        pltpu.make_async_remote_copy(
+            src_ref=block_ref,
+            dst_ref=held.at[mine, zm, origin_x],
+            send_sem=cross_send.at[k],
+            recv_sem=cross_recv.at[k],
+            device_id=device_at(row=origin_x * zs + zm),
+            device_id_type=MESH_IDS,
+        ).wait_recv()
+    split = xs // 2
+    ways = ((0, ahead, behind, -1, pl.ds(0, split)), (1, behind, ahead, 1, pl.ds(split, xs - split)))
+    for step in range(zs):
+        for way, dest, origin, sign, part in ways:
+            group = lax.rem(zm + sign * step + zs, zs)
+            if step > 0:
+                pltpu.make_async_remote_copy(
+                    src_ref=held.at[mine, group, part],
+                    dst_ref=held.at[mine, group, part],
+                    send_sem=ring_send.at[way, step - 1],
+                    recv_sem=ring_recv.at[way, step - 1],
+                    device_id=device_at(row=origin),
+                    device_id_type=MESH_IDS,
+                ).wait_recv()
+            if step < zs - 1:
+                copy = pltpu.make_async_remote_copy(
+                    src_ref=held.at[mine, group, part],
+                    dst_ref=held.at[mine, group, part],
+                    send_sem=ring_send.at[way, step],
+                    recv_sem=ring_recv.at[way, step],
+                    device_id=device_at(row=dest),
+                    device_id_type=MESH_IDS,
+                )
+                copy.start()
+                pending.append(copy)
+            copy = pltpu.make_async_remote_copy(
+                src_ref=held.at[mine, group, part],
+                dst_ref=held.at[mine, group, part],
+                send_sem=pair_send.at[way, step],
+                recv_sem=pair_recv.at[way, step],
+                device_id=device_at(req=other),
+                device_id_type=MESH_IDS,
+            )
+            copy.start()
+            pending.append(copy)
+    for step in range(zs):
+        for way, dest, origin, sign, part in ways:
+            group = lax.rem(zm + sign * step + zs, zs)
+            pltpu.make_async_remote_copy(
+                src_ref=held.at[other, group, part],
+                dst_ref=held.at[other, group, part],
+                send_sem=pair_send.at[way, step],
+                recv_sem=pair_recv.at[way, step],
+                device_id=device_at(req=other),
+                device_id_type=MESH_IDS,
+            ).wait_recv()
+    for copy in pending:
+        copy.wait_send()
+    out = pltpu.make_async_copy(held, out_ref, own_sem)
+    out.start()
+    out.wait()
+
+
+def paired_gather(block, xs, zs, kernel_id):
+    return pl.pallas_call(
+        functools.partial(paired_gather_kernel, zs, xs),
+        out_shape=jax.ShapeDtypeStruct((2, zs, xs) + block.shape, block.dtype),
+        in_specs=[pl.BlockSpec(memory_space=pltpu.VMEM)],
+        out_specs=pl.BlockSpec(memory_space=pl.ANY),
+        scratch_shapes=[
+            pltpu.VMEM((2, zs, xs) + block.shape, block.dtype),
+            pltpu.SemaphoreType.DMA(()),
+            pltpu.SemaphoreType.DMA((2, zs - 1)),
+            pltpu.SemaphoreType.DMA((2, zs - 1)),
+            pltpu.SemaphoreType.DMA((xs,)),
+            pltpu.SemaphoreType.DMA((xs,)),
+            pltpu.SemaphoreType.DMA((2, zs)),
+            pltpu.SemaphoreType.DMA((2, zs)),
+        ],
+        compiler_params=pltpu.CompilerParams(
+            collective_id=kernel_id, has_side_effects=True, vmem_limit_bytes=56 * 1024 * 1024
+        ),
+    )(block)
+
+
 def layer_norm(tensor, epsilon):
     average = jnp.mean(tensor, axis=-1, keepdims=True)
     centered = tensor - average
@@ -461,8 +581,21 @@
     owners = jnp.reshape(request_id, (1,))
     half_cols = w_qkv.shape[2] // 2
     own_half = lax.dynamic_slice_in_dim(w_qkv, request_id * half_cols, half_cols, 2)
-    gathered_half = lax.all_gather(own_half, "row", axis=1, tiled=True)
-    qkv = projector(stacked, lax.all_gather(gathered_half, "req", axis=2, tiled=True))
+    both_halves = paired_gather(own_half.transpose(1, 0, 2), 4, 8, 3)
+    depth = w_qkv.shape[1]
+    reordered = joined.reshape(span, 4, 8, depth).transpose(0, 2, 1, 3).reshape(span, -1)
+    qkv = jnp.concatenate(
+        [
+            jnp.einsum(
+                "lk,kce->cle",
+                reordered,
+                both_halves[h].reshape(-1, 3, half_cols),
+                preferred_element_type=jnp.float32,
+            )
+            for h in range(2)
+        ],
+        axis=2,
+    )[:, None]
     groups = stacked.shape[0]
     heads_here = qkv.shape[3] // head_dim
     shaped = qkv.reshape(3, groups, span, heads_here, head_dim)

time: 481 us -> 500 us (1.040)
  waiting for transfers between devices: 226 us -> 100 us
  Pallas kernels: 164 us -> 284 us
  local copies, waits for them, and re-layouts: 12.7 us -> 32.9 us
  other arithmetic: 19.9 us -> 30.1 us
    all_gather x2 -> x0, waiting for transfers between devices: 124 us -> none  [the longest x1 95.3 us: shards(): gathered_half = lax.all_gather(own_half, 'row', axis=1, tiled=True)]
    pallas_call x0 -> x1, Pallas kernels: none -> 121 us  [paired_gather(): pl.pallas_call(functools.partial(paired_gather_kernel, zs, xs), out_shape...]
    slice x1 -> x2, local copies, waits for them, and re-layouts: 0.07 us -> 13.1 us  [the longest x1 13 us: shards(): both_halves[h].reshape(-1, 3, half_cols)]
  transfers between devices with their start and end apart: 7 -> 5, of which waited for: 5 -> 3; matrix products, arithmetic and copies ran while one was open for 4% -> 4% of each run, Pallas kernels for 0% -> 0%
where the time goes in v6:
time: 500 us; the launch traced here: 498 us
  Pallas kernels  284 us (57%)
  waiting for transfers between devices  100 us (20%)
  local copies, waits for them, and re-layouts  32.9 us (7%)
  other arithmetic  30.1 us (6%)
  between operations  18.6 us (4%)
  matrix products  17.6 us (4%)
  starting transfers between devices  13.8 us (3%)
    pallas_call x1, Pallas kernels, paired_gather(): pl.pallas_call(functools.partial(paired_gather_kernel, zs, xs), out_shape...  121 us
    all_gather x1, waiting for transfers between devices, shards(): gathered = lax.all_gather(both, 'row', axis=0, tiled=True)  98.2 us
    pallas_call x1, Pallas kernels, ring_scatter_sum(): pl.pallas_call(functools.partial(ring_scatter_kernel, zs, xs), out_shape=...  66.8 us
    pallas_call x1, Pallas kernels, ring_gather(): pl.pallas_call(functools.partial(ring_gather_kernel, zs, xs), out_shape=j...  66.3 us
    pallas_call x1, Pallas kernels, scatter_sum(): pl.pallas_call(functools.partial(scatter_sum_kernel, axis, count, rows),...  17.2 us
    slice x1, local copies, waits for them, and re-layouts, shards(): both_halves[h].reshape(-1, 3, half_cols)  13 us
    pallas_call x1, Pallas kernels, attention(): pl.pallas_call(functools.partial(attention_kernel, scale), out_shape=jax....  12.8 us
    dot_general x1, matrix products, shards(): jnp.dot(hidden_units, w_down, preferred_element_type=jnp.float32)  10.4 us
  transfers between devices with their start and end apart: 5, of which 3 were waited for; matrix products, arithmetic and copies ran while one was open for 4% of the time, Pallas kernels for 0%

profile of v6, /device:TPU:2, one launch (start us, length us, event | category | flops | bytes accessed | tf_op | source)
XLA Modules:
  0.0 497.7 jit_solution(4657779610813237564)
XLA Ops:
  7.3 1.4 convert_reduce_fusion
  8.7 2.8 reshape.536
  11.7 0.7 slice_add_fusion
  12.5 0.3 fusion.23
  12.9 0.2 fusion.71
  13.1 2.1 fusion.7
  15.3 1.5 maximum_bitcast_fusion
  16.8 3.3 reshape.539
  20.1 0.9 copy.104
  21.0 121.0 %shard_map.166 = bf16[2,8,4,96,3,384]{5,4,3,2,1,0:T(4,128)(2,1)} custom-call(bf16[96,3,384]{2,1,0:T(4,128)(2,1)} %bitcast.167), custom_call_target="tpu_custom_call" | custom-call | tf_op jit(solution)/shard_map/pallas_call | solution.py:440
  142.1 13.0 %fusion.155 = (bf16[1,8,4,96,3,384]{5,4,3,2,1,0:T(4,128)(2,1)S(1)}, bf16[1,8,4,96,3,384]{5,4,3,2,1,0:T(4,128)(2,1)S(1)}) fusion(bf16[2,8,4,96,3,384]{5,4,3,2,1,0:T(4,128)(2,1)} %shard_map.166), kind=kLoop, calls=%fused_computation.236 | loop fusion | bytes 28311552 | tf_op jit(solution)/shard_map/slice | solution.py:592
  155.1 1.1 fusion.8
  156.2 1.1 fusion.11
  157.4 0.8 fusion.48
  158.3 0.7 fusion.50
  159.0 1.9 copy.61
  160.9 1.1 reduce_sum.186
  161.9 1.1 multiply_reduce_fusion
  163.0 0.8 mul.323
  163.8 1.9 copy.64
  165.7 0.8 sub.151
  166.4 1.9 copy.62
  168.4 1.2 multiply_convert_fusion
  169.7 1.7 fusion.41
  171.4 1.2 convert_element_type.102
  172.7 0.3 reduce-window.9
  173.1 0.6 select_reduce_fusion.4
  174.5 1.3 select_reduce_fusion
  178.5 2.0 pad_maximum_fusion
  180.6 1.6 copy.57
  182.2 0.8 fusion.156
  183.1 0.9 copy.60
  184.0 0.9 copy.59
  184.8 0.9 copy.58
  185.8 0.2 slice_reduce_fusion.3
  186.0 0.6 select_reduce_fusion.2
  187.3 0.7 and_convert_fusion
  187.9 0.6 select_reduce_fusion.5
  188.6 0.7 fusion.139
  189.3 1.9 multiply_convert_fusion.1.q_ref
  191.1 2.6 select_convert_fusion.live_ref
  193.8 98.2 %all-gather.3.cloned.1.call-done = bf16[64,128,768]{2,1,0:T(8,128)(2,1)} async-done(((bf16[2,128,768]{2,1,0:T(8,128)(2,1)}), bf16[64,128,768]{2,1,0:T(8,128)(2,1)}) %all-gather.3.cloned.1.call-update) | async-done | bytes 12582928 | tf_op jit(solution)/shard_map/all_gather | solution.py:610
  291.9 12.8 %shard_map.167 = bf16[96,768]{1,0:T(8,128)(2,1)} custom-call(bf16[96,768]{1,0:T(8,128)(2,1)} %multiply_convert_fusion.1.q_ref, bf16[32,2,128,768]{3,2,1,0:T(8,128)(2,1)} %bitcast.140, f32[1,4096]{1,0:T(1,128)} %select_convert_fusion.live_ref), custom_call_target="tpu_custom_call" | custom-call | tf_op jit(solution)/shard_map/pallas_call | solution.py:130
  304.7 2.0 fusion.160.part_ref
  306.8 17.2 %shard_map.168 = f32[24,3072]{1,0:T(8,128)S(1)} custom-call(f32[96,3072]{1,0:T(8,128)S(1)} %fusion.160.part_ref), custom_call_target="tpu_custom_call" | custom-call | tf_op jit(solution)/shard_map/pallas_call | solution.py:89
  324.0 1.0 fusion.60
  325.2 0.2 fusion.51
  325.4 0.8 fusion.54.block_ref
  326.2 66.3 %shard_map.169 = bf16[8,4,24,3072]{3,2,1,0:T(8,128)(2,1)} custom-call(bf16[24,3072]{1,0:T(8,128)(2,1)} %fusion.54.block_ref), custom_call_target="tpu_custom_call" | custom-call | tf_op jit(solution)/shard_map/pallas_call | solution.py:322
  392.5 10.4 %convolution_convert_fusion = bf16[768,3072]{1,0:T(8,128)(2,1)} fusion(bf16[384,3072]{1,0:T(8,128)(2,1)S(1)} %copy-done, bf16[768,3072]{1,0:T(8,128)(2,1)} %bitcast.145, bf16[3072,384]{1,0:T(8,128)(2,1)} %param.25), kind=kOutput, calls=%fused_computation.4 | convolution fusion | flops 3628892160 | bytes 14155776 | tf_op jit(solution)/shard_map/dot_general | solution.py:635
  402.9 66.8 %shard_map.170 = f32[24,3072]{1,0:T(8,128)} custom-call(bf16[8,4,24,3072]{3,2,1,0:T(8,128)(2,1)} %bitcast.146), custom_call_target="tpu_custom_call" | custom-call | tf_op jit(solution)/shard_map/pallas_call | solution.py:231
  469.8 1.2 convert_reduce_fusion.2
  470.9 0.2 fusion.55
  471.2 0.9 multiply_convert_fusion.2
  472.3 0.3 copy.66
  472.6 2.5 collective-permute-start
  475.1 5.5 %collective-permute-start.1 = (bf16[6,1,8,16]{3,2,1,0:T(8,128)(2,1)S(1)}, bf16[6,1,8,16]{3,2,1,0:T(8,128)(2,1)S(1)}, u32[]{:S(2)}, u32[]{:S(2)}) collective-permute-start(bf16[6,1,8,16]{3,2,1,0:T(8,128)(2,1)S(1)} %get-tuple-element.26), channel_id=1, source_target_pairs={{4,0},{8,4},{12,8},{16,12},{20,16},{24,20},{28,24},{32,28},{36,32}... | collective-permute-start | bytes 4616 | tf_op jit(solution)/shard_map/ppermute | solution.py:33
  480.7 1.2 collective-permute-done.1
  482.0 1.3 collective-permute-start.3
  483.3 4.5 collective-permute-start.2
  488.1 1.1 collective-permute-done.2
  489.7 0.2 fusion.80
  489.8 0.2 fusion.29
  490.0 0.8 fusion.31
  (100 shorter events, 2.8 us)
Async XLA Ops:
  7.2 385.3 %copy-start = (bf16[384,3072]{1,0:T(8,128)(2,1)S(1)}, bf16[384,3072]{1,0:T(8,128)(2,1)}, u32[]{:S(2)}) copy-start(bf16[384,3072]{1,0:T(8,128)(2,1)} %param.26) | copy-start | bytes 7077892
  7.2 5.4 %copy-start.1 = (bf16[1,96,3072]{2,1,0:T(8,128)(2,1)S(1)}, bf16[1,96,3072]{2,1,0:T(8,128)(2,1)}, u32[]{:S(2)}) copy-start(bf16[1,96,3072]{2,1,0:T(8,128)(2,1)} %param.15) | copy-start | bytes 1769476
  7.2 4.3 copy-start.6
  7.2 4.5 copy-start.9
  7.2 284.7 %all-gather.3.cloned.1.call-start = ((), (), s32[]{:S(2)}) async-start(), calls=%async_computation | async-start | bytes 12976128 | tf_op jit(solution)/shard_map/all_gather | solution.py:610
  15.3 4.8 copy-start.8
  142.0 13.0 %copy-start.4 = (bf16[100,3072,1]{1,0,2:T(8,128)(2,1)S(1)}, bf16[100,3072,1]{1,0,2:T(8,128)(2,1)}, u32[]{:S(2)}) copy-start(bf16[100,3072,1]{1,0,2:T(8,128)(2,1)} %reshape.539) | copy-start | bytes 1843204
  157.4 0.9 copy-start.2
  160.8 7.5 %copy-start.17 = (f32[64]{0:T(128)S(1)}, f32[64]{0:T(128)}, u32[]{:S(2)}) copy-start(f32[64]{0:T(128)} %param.22) | copy-start | bytes 772
  169.6 3.4 copy-start.21
  182.9 2.8 copy-start.18
  182.9 2.9 copy-start.16
  183.0 1.8 copy-start.3
  183.0 4.9 copy-start.22
  184.8 119.9 %slice-start = ((s8[4718592]{0:T(1024)(128)(4,1)}), s8[524288]{0:T(1024)(128)(4,1)S(1)}, s32[]{:S(2)}) async-start(s8[4718592]{0:T(1024)(128)(4,1)} %bitcast.143), calls=%async_computation.1 | async-start | bytes 1048576
  291.9 12.8 %slice-start.1 = ((s8[4718592]{0:T(1024)(128)(4,1)}), s8[4194304]{0:T(1024)(128)(4,1)S(1)}, s32[]{:S(2)}) async-start(s8[4718592]{0:T(1024)(128)(4,1)} %bitcast.143), calls=%async_computation.2 | async-start | bytes 8388608
  304.7 19.3 %copy-start.13 = (f32[1,1,3072]{2,1,0:T(1,128)S(1)}, f32[1,1,3072]{2,1,0:T(1,128)}, u32[]{:S(2)}) copy-start(f32[1,1,3072]{2,1,0:T(1,128)} %get-tuple-element.21) | copy-start | bytes 36868
  306.8 18.6 %copy-start.10 = (f32[1,1,3072]{2,1,0:T(1,128)S(1)}, f32[1,1,3072]{2,1,0:T(1,128)}, u32[]{:S(2)}) copy-start(f32[1,1,3072]{2,1,0:T(1,128)} %get-tuple-element.16) | copy-start | bytes 36868
  306.8 18.6 %copy-start.11 = (f32[1,1,3072]{2,1,0:T(1,128)S(1)}, f32[1,1,3072]{2,1,0:T(1,128)}, u32[]{:S(2)}) copy-start(f32[1,1,3072]{2,1,0:T(1,128)} %get-tuple-element.18) | copy-start | bytes 36868
  402.9 66.9 %copy-start.12 = (f32[1,1,3072]{2,1,0:T(1,128)S(1)}, f32[1,1,3072]{2,1,0:T(1,128)}, u32[]{:S(2)}) copy-start(f32[1,1,3072]{2,1,0:T(1,128)} %get-tuple-element.17) | copy-start | bytes 36868
  402.9 68.3 %copy-start.14 = (f32[1,1,3072]{2,1,0:T(1,128)S(1)}, f32[1,1,3072]{2,1,0:T(1,128)}, u32[]{:S(2)}) copy-start(f32[1,1,3072]{2,1,0:T(1,128)} %get-tuple-element.15) | copy-start | bytes 36868
  402.9 68.3 %copy-start.15 = (f32[1,1,3072]{2,1,0:T(1,128)S(1)}, f32[1,1,3072]{2,1,0:T(1,128)}, u32[]{:S(2)}) copy-start(f32[1,1,3072]{2,1,0:T(1,128)} %get-tuple-element.22) | copy-start | bytes 36868
  402.9 68.3 %copy-start.19 = (bf16[3072,64]{0,1:T(8,128)(2,1)S(1)}, bf16[3072,64]{0,1:T(8,128)(2,1)}, u32[]{:S(2)}) copy-start(bf16[3072,64]{0,1:T(8,128)(2,1)} %param.27) | copy-start | bytes 1179652
  402.9 68.3 %copy-start.20 = (f32[1,24,64]{2,1,0:T(8,128)S(1)}, f32[1,24,64]{2,1,0:T(8,128)}, u32[]{:S(2)}) copy-start(f32[1,24,64]{2,1,0:T(8,128)} %param.28) | copy-start | bytes 18436
  469.7 10.8 %copy-start.7 = (bf16[3,3,16,512]{3,2,1,0:T(8,128)(2,1)S(1)}, bf16[3,3,16,512]{3,2,1,0:T(8,128)(2,1)}, u32[]{:S(2)}) copy-start(bf16[3,3,16,512]{3,2,1,0:T(8,128)(2,1)} %param.29) | copy-start | bytes 442372
  470.9 18.9 %copy-start.5 = (bf16[24,3072]{1,0:T(8,128)(2,1)}, bf16[24,3072]{1,0:T(8,128)(2,1)S(1)}, u32[]{:S(2)}) copy-start(bf16[24,3072]{1,0:T(8,128)(2,1)S(1)} %get-tuple-element.10) | copy-start | bytes 442372
  472.6 8.1 %collective-permute-start = (bf16[6,1,8,16]{3,2,1,0:T(8,128)(2,1)S(1)}, bf16[6,1,8,16]{3,2,1,0:T(8,128)(2,1)S(1)}, u32[]{:S(2)}, u32[]{:S(2)}) collective-permute-start(bf16[6,1,8,16]{3,2,1,0:T(8,128)(2,1)S(1)} %get-tuple-element.25), channel_id=1, source_target_pairs={{0,4},{4,8},{8,12},{12,16},{16,20},{20,24},{24,28},{28,32},{32,36}... | collective-permute-start | bytes 4616 | tf_op jit(solution)/shard_map/ppermute | solution.py:31
  475.1 6.9 %collective-permute-start.1 = (bf16[6,1,8,16]{3,2,1,0:T(8,128)(2,1)S(1)}, bf16[6,1,8,16]{3,2,1,0:T(8,128)(2,1)S(1)}, u32[]{:S(2)}, u32[]{:S(2)}) collective-permute-start(bf16[6,1,8,16]{3,2,1,0:T(8,128)(2,1)S(1)} %get-tuple-element.26), channel_id=1, source_target_pairs={{4,0},{8,4},{12,8},{16,12},{20,16},{24,20},{28,24},{32,28},{36,32}... | collective-permute-start | bytes 4616 | tf_op jit(solution)/shard_map/ppermute | solution.py:33
  482.0 7.5 %collective-permute-start.3 = (bf16[6,4,1,16]{3,2,1,0:T(2,128)(2,1)S(1)}, bf16[6,4,1,16]{3,2,1,0:T(2,128)(2,1)S(1)}, u32[]{:S(2)}, u32[]{:S(2)}) collective-permute-start(bf16[6,4,1,16]{3,2,1,0:T(2,128)(2,1)S(1)} %get-tuple-element.24), channel_id=1, source_target_pairs={{1,0},{2,1},{3,2},{5,4},{6,5},{7,6},{9,8},{10,9},{11,10},{13,12},{... | collective-permute-start | bytes 2312 | tf_op jit(solution)/shard_map/ppermute | solution.py:33
  483.3 5.9 %collective-permute-start.2 = (bf16[6,4,1,16]{3,2,1,0:T(2,128)(2,1)S(1)}, bf16[6,4,1,16]{3,2,1,0:T(2,128)(2,1)S(1)}, u32[]{:S(2)}, u32[]{:S(2)}) collective-permute-start(bf16[6,4,1,16]{3,2,1,0:T(2,128)(2,1)S(1)} %get-tuple-element.23), channel_id=1, source_target_pairs={{0,1},{1,2},{2,3},{4,5},{5,6},{6,7},{8,9},{9,10},{10,11},{12,13},{... | collective-permute-start | bytes 2312 | tf_op jit(solution)/shard_map/ppermute | solution.py:31
Sparse Core Ops, SparseCore 0:
  171.5 120.3 all-gather.2

commit v7 on v5

--- a/solution.py
+++ b/solution.py
@@ -338,6 +338,36 @@
     )(block)
 
 
+def swap_kernel(src_ref, out_ref, landed, sems):
+    other = 1 - lax.axis_index("req")
+    barrier = pltpu.get_barrier_semaphore()
+    pl.semaphore_signal(barrier, inc=1, device_id=peer_on("req", other), device_id_type=MESH_IDS)
+    pl.semaphore_wait(barrier, 1)
+    copy = pltpu.make_async_remote_copy(
+        src_ref=src_ref,
+        dst_ref=landed,
+        send_sem=sems.at[0],
+        recv_sem=sems.at[1],
+        device_id=peer_on("req", other),
+        device_id_type=MESH_IDS,
+    )
+    copy.start()
+    copy.wait_send()
+    copy.wait_recv()
+    out_ref[...] = landed[...]
+
+
+def partner_swap(value, kernel_id):
+    return pl.pallas_call(
+        swap_kernel,
+        out_shape=jax.ShapeDtypeStruct(value.shape, value.dtype),
+        in_specs=[pl.BlockSpec(memory_space=pltpu.VMEM)],
+        out_specs=pl.BlockSpec(memory_space=pltpu.VMEM),
+        scratch_shapes=[pltpu.VMEM(value.shape, value.dtype), pltpu.SemaphoreType.DMA((2,))],
+        compiler_params=pltpu.CompilerParams(collective_id=kernel_id, has_side_effects=True),
+    )(value)
+
+
 def layer_norm(tensor, epsilon):
     average = jnp.mean(tensor, axis=-1, keepdims=True)
     centered = tensor - average
@@ -462,16 +492,29 @@
     half_cols = w_qkv.shape[2] // 2
     own_half = lax.dynamic_slice_in_dim(w_qkv, request_id * half_cols, half_cols, 2)
     gathered_half = lax.all_gather(own_half, "row", axis=1, tiled=True)
-    qkv = projector(stacked, lax.all_gather(gathered_half, "req", axis=2, tiled=True))
-    groups = stacked.shape[0]
-    heads_here = qkv.shape[3] // head_dim
-    shaped = qkv.reshape(3, groups, span, heads_here, head_dim)
-    queries = head_norm(shaped[0, :, :block_tokens], q_gain)
-    key_block = head_norm(shaped[1], k_gain)
-    value_block = shaped[2].astype(jnp.bfloat16)
+    half_heads = half_cols // head_dim
+
+    def project(rows):
+        mixed_cols = jnp.einsum("ld,cde->cle", rows, gathered_half, preferred_element_type=jnp.float32)
+        split = mixed_cols.reshape(3, span, half_heads, head_dim)
+        return jnp.stack(
+            [head_norm(split[0], q_gain), head_norm(split[1], k_gain), split[2].astype(jnp.bfloat16)]
+        )
+
+    mine = project(joined)
+    theirs = project(partner_swap(joined, 4))
+    received = partner_swap(theirs.reshape(3 * span, half_cols), 5).reshape(theirs.shape)
+    full = jnp.concatenate(
+        [jnp.where(request_id == 0, mine, received), jnp.where(request_id == 0, received, mine)], axis=2
+    )
+    groups = 1
+    heads_here = full.shape[2]
+    queries = full[0, :block_tokens][None]
+    key_block = full[1][None]
+    value_block = full[2][None]
     attend = attention_step(queries, owners, grid, text_len, span, block_tokens, tile, text_rows)
     empty_state = (jnp.zeros(queries.shape, jnp.float32), jnp.zeros(queries.shape[:3], jnp.float32))
-    padded_span = 128 * pl.cdiv(span, 128)
+    padded_span = 16 * pl.cdiv(span, 16)
     both = jnp.stack([key_block[0], value_block[0]], axis=0).reshape(2, span, heads_here * head_dim)
     both = jnp.pad(both, ((0, 0), (0, padded_span - span), (0, 0)))[None]
     gathered = lax.all_gather(both, "row", axis=0, tiled=True)

time: 481 us -> 467 us (0.971)
  waiting for transfers between devices: 226 us -> 184 us
  other arithmetic: 19.9 us -> 32.8 us
  local copies, waits for them, and re-layouts: 12.7 us -> 24.7 us
  Pallas kernels: 164 us -> 169 us
    all_gather x1 -> x0, waiting for transfers between devices: 28.7 us -> none  [shards(): lax.all_gather(gathered_half, 'req', axis=2, tiled=True)]
    all_gather x1, waiting for transfers between devices: 95.3 us -> 85.5 us  [shards(): gathered_half = lax.all_gather(own_half, 'row', axis=1, tiled=True)]
    all_gather x1, waiting for transfers between devices: 100 us -> 92.1 us  [shards(): gathered = lax.all_gather(both, 'row', axis=0, tiled=True)]
    reshape x0 -> x4, local copies, waits for them, and re-layouts: none -> 7.49 us  [the longest x2 4.18 us: shards(): partner_swap(theirs.reshape(3 * span, half_cols), 5).reshape(theirs.shape)]
    pallas_call x0 -> x2, Pallas kernels: none -> 7.23 us  [partner_swap(): pl.pallas_call(swap_kernel, out_shape=jax.ShapeDtypeStruct(value.shape, v...]
    slice x3 -> x11, local copies, waits for them, and re-layouts: 1.94 us -> 8.21 us  [the longest x4 4.2 us: project(): split[0]]
    ppermute x2, waiting for transfers between devices: 1.09 us -> 6.69 us  [extended(): lax.ppermute(tail, axis, [(i, (i + 1) % count) for i in range(ends)])]
  transfers between devices with their start and end apart: 7 -> 6, of which waited for: 5 -> 4; matrix products, arithmetic and copies ran while one was open for 4% -> 4% of each run, Pallas kernels for 0% -> 1%
where the time goes in v7:
time: 467 us; the launch traced here: 465 us
  waiting for transfers between devices  184 us (39%)
  Pallas kernels  169 us (36%)
  other arithmetic  32.8 us (7%)
  local copies, waits for them, and re-layouts  24.7 us (5%)
  matrix products  20.6 us (4%)
  between operations  18.4 us (4%)
  starting transfers between devices  14.9 us (3%)
    all_gather x1, waiting for transfers between devices, shards(): gathered = lax.all_gather(both, 'row', axis=0, tiled=True)  92.1 us
    all_gather x1, waiting for transfers between devices, shards(): gathered_half = lax.all_gather(own_half, 'row', axis=1, tiled=True)  85.5 us
    pallas_call x1, Pallas kernels, ring_scatter_sum(): pl.pallas_call(functools.partial(ring_scatter_kernel, zs, xs), out_shape=...  66.7 us
    pallas_call x1, Pallas kernels, ring_gather(): pl.pallas_call(functools.partial(ring_gather_kernel, zs, xs), out_shape=j...  66.4 us
    pallas_call x1, Pallas kernels, scatter_sum(): pl.pallas_call(functools.partial(scatter_sum_kernel, axis, count, rows),...  17.2 us
    pallas_call x1, Pallas kernels, attention(): pl.pallas_call(functools.partial(attention_kernel, scale), out_shape=jax....  11.4 us
    dot_general x1, matrix products, shards(): jnp.dot(hidden_units, w_down, preferred_element_type=jnp.float32)  10.4 us
  transfers between devices with their start and end apart: 6, of which 4 were waited for; matrix products, arithmetic and copies ran while one was open for 4% of the time, Pallas kernels for 1%

profile of v7, /device:TPU:2, one launch (start us, length us, event | category | flops | bytes accessed | tf_op | source)
XLA Modules:
  0.0 464.6 jit_solution(14315522216869051871)
XLA Ops:
  7.3 1.8 constant_dynamic-slice_fusion
  9.2 0.9 convert_reduce_fusion.3
  10.1 0.9 fusion.47
  11.0 1.2 convert_reduce_fusion
  12.6 0.7 slice_add_fusion
  14.0 0.9 pad_maximum_fusion.src_ref
  14.9 4.0 shard_map.166
  18.9 85.5 %all-gather.4.cloned.1.call-done = bf16[3,3072,384]{2,1,0:T(8,128)(2,1)} async-done(((bf16[3,96,384]{2,1,0:T(8,128)(2,1)}), bf16[3,3072,384]{2,1,0:T(8,128)(2,1)}) %all-gather.4.cloned.1.call-update) | async-done | bytes 7077904 | tf_op jit(solution)/shard_map/all_gather | solution.py:494
  104.4 4.4 convolution_bitcast_fusion
  108.8 0.6 slice.251
  109.4 0.8 fusion.135
  110.2 1.2 convolution_bitcast_fusion.1
  111.4 0.7 fusion.134
  112.1 0.6 slice.252
  112.7 1.6 copy.47
  114.7 0.6 multiply_reduce_fusion.1
  116.0 1.0 copy.38
  117.0 1.7 copy.43
  118.7 1.5 reduce_sum.224
  120.3 0.7 broadcast_multiply_fusion.1
  121.5 1.6 multiply_reduce_fusion.2
  123.7 0.7 broadcast_multiply_fusion.3
  124.5 0.7 add_rsqrt_fusion
  125.2 0.7 add_rsqrt_fusion.1
  125.9 1.4 multiply_convert_fusion.2
  127.3 1.7 multiply_convert_fusion.3
  129.0 1.2 copy.66
  130.2 2.1 reshape.568.src_ref
  132.4 3.2 shard_map.167
  135.6 2.1 reshape.569
  137.7 2.1 copy.51
  139.7 0.8 copy.42
  140.5 1.2 broadcast_select_fusion.1
  141.7 0.8 pad_maximum_fusion.1
  142.5 1.9 copy.70
  144.4 1.7 pad.7.clone
  146.2 1.1 convert_element_type.134
  147.8 1.3 select_reduce_fusion.4
  149.9 1.2 select_reduce_fusion
  153.9 0.6 select_reduce_fusion.2
  155.2 0.7 and_convert_fusion
  155.9 1.3 select_reduce_fusion.5
  157.2 0.7 fusion.118
  157.9 2.8 select_convert_fusion.live_ref
  160.7 0.7 pad_maximum_fusion.4
  161.4 1.7 copy.54.q_ref
  163.1 92.1 %all-gather.6.cloned.1.call-done = bf16[64,112,768]{2,1,0:T(8,128)(2,1)} async-done(((bf16[2,112,768]{2,1,0:T(8,128)(2,1)}), bf16[64,112,768]{2,1,0:T(8,128)(2,1)}) %all-gather.6.cloned.1.call-update) | async-done | bytes 11010064 | tf_op jit(solution)/shard_map/all_gather | solution.py:520
  255.2 11.4 %shard_map.168 = bf16[96,768]{1,0:T(8,128)(2,1)} custom-call(bf16[96,768]{1,0:T(8,128)(2,1)} %copy.54.q_ref, bf16[32,2,112,768]{3,2,1,0:T(8,128)(2,1)} %bitcast.149, f32[1,3584]{1,0:T(1,128)} %select_convert_fusion.live_ref), custom_call_target="tpu_custom_call" | custom-call | tf_op jit(solution)/shard_map/pallas_call | solution.py:130
  266.6 1.8 fusion.139.part_ref
  268.4 17.2 %shard_map.169 = f32[24,3072]{1,0:T(8,128)S(1)} custom-call(f32[96,3072]{1,0:T(8,128)S(1)} %fusion.139.part_ref), custom_call_target="tpu_custom_call" | custom-call | tf_op jit(solution)/shard_map/pallas_call | solution.py:89
  285.6 1.0 fusion.38
  287.0 0.8 fusion.32.block_ref
  287.8 66.4 %shard_map.170 = bf16[8,4,24,3072]{3,2,1,0:T(8,128)(2,1)} custom-call(bf16[24,3072]{1,0:T(8,128)(2,1)} %fusion.32.block_ref), custom_call_target="tpu_custom_call" | custom-call | tf_op jit(solution)/shard_map/pallas_call | solution.py:322
  354.2 10.4 %convolution_convert_fusion = bf16[768,3072]{1,0:T(8,128)(2,1)} fusion(bf16[384,3072]{1,0:T(8,128)(2,1)S(1)} %copy-done, bf16[768,3072]{1,0:T(8,128)(2,1)} %bitcast.152, bf16[3072,384]{1,0:T(8,128)(2,1)} %param.25), kind=kOutput, calls=%fused_computation | convolution fusion | flops 3628892160 | bytes 14155776 | tf_op jit(solution)/shard_map/dot_general | solution.py:545
  364.6 66.7 %shard_map.171 = f32[24,3072]{1,0:T(8,128)} custom-call(bf16[8,4,24,3072]{3,2,1,0:T(8,128)(2,1)} %bitcast.153), custom_call_target="tpu_custom_call" | custom-call | tf_op jit(solution)/shard_map/pallas_call | solution.py:231
  431.3 1.2 convert_reduce_fusion.2
  432.7 0.9 multiply_convert_fusion.4
  434.1 5.8 %collective-permute-start.1 = (bf16[6,1,8,16]{3,2,1,0:T(8,128)(2,1)S(1)}, bf16[6,1,8,16]{3,2,1,0:T(8,128)(2,1)S(1)}, u32[]{:S(2)}, u32[]{:S(2)}) collective-permute-start(bf16[6,1,8,16]{3,2,1,0:T(8,128)(2,1)S(1)} %get-tuple-element.26), channel_id=1, source_target_pairs={{4,0},{8,4},{12,8},{16,12},{20,16},{24,20},{28,24},{32,28},{36,32}... | collective-permute-start | bytes 4616 | tf_op jit(solution)/shard_map/ppermute | solution.py:33
  440.0 1.9 collective-permute-start
  442.1 5.6 %collective-permute-done = bf16[6,1,8,16]{3,2,1,0:T(8,128)(2,1)S(1)} collective-permute-done((bf16[6,1,8,16]{3,2,1,0:T(8,128)(2,1)S(1)}, bf16[6,1,8,16]{3,2,1,0:T(8,128)(2,1)S(1)}, u32[]{:S(2)}, u32[]{:S(2)}) %collective-permute-start) | collective-permute-done | bytes 1568 | tf_op jit(solution)/shard_map/ppermute | solution.py:31
  447.7 1.3 collective-permute-start.3
  449.0 5.7 %collective-permute-start.2 = (bf16[6,4,1,16]{3,2,1,0:T(2,128)(2,1)S(1)}, bf16[6,4,1,16]{3,2,1,0:T(2,128)(2,1)S(1)}, u32[]{:S(2)}, u32[]{:S(2)}) collective-permute-start(bf16[6,4,1,16]{3,2,1,0:T(2,128)(2,1)S(1)} %get-tuple-element.23), channel_id=1, source_target_pairs={{0,1},{1,2},{2,3},{4,5},{5,6},{6,7},{8,9},{9,10},{10,11},{12,13},{... | collective-permute-start | bytes 2312 | tf_op jit(solution)/shard_map/ppermute | solution.py:31
  455.1 1.1 collective-permute-done.2
  456.9 0.8 fusion.15
  (101 shorter events, 6.6 us)
Async XLA Ops:
  7.2 347.0 %copy-start = (bf16[384,3072]{1,0:T(8,128)(2,1)S(1)}, bf16[384,3072]{1,0:T(8,128)(2,1)}, u32[]{:S(2)}) copy-start(bf16[384,3072]{1,0:T(8,128)(2,1)} %param.26) | copy-start | bytes 7077892
  7.2 6.1 %copy-start.7 = (bf16[1,4,3072]{2,1,0:T(4,128)(2,1)S(1)}, bf16[1,4,3072]{2,1,0:T(4,128)(2,1)}, u32[]{:S(2)}) copy-start(bf16[1,4,3072]{2,1,0:T(4,128)(2,1)} %param.16) | copy-start | bytes 73732
  7.2 5.1 %copy-start.1 = (bf16[1,96,3072]{2,1,0:T(8,128)(2,1)S(1)}, bf16[1,96,3072]{2,1,0:T(8,128)(2,1)}, u32[]{:S(2)}) copy-start(bf16[1,96,3072]{2,1,0:T(8,128)(2,1)} %param.15) | copy-start | bytes 1769476
  7.2 5.4 %copy-start.9 = (f32[1,8,3072]{2,1,0:T(8,128)S(1)}, f32[1,8,3072]{2,1,0:T(8,128)}, u32[]{:S(2)}) copy-start(f32[1,8,3072]{2,1,0:T(8,128)} %param.20) | copy-start | bytes 294916
  7.2 97.2 %all-gather.4.cloned.1.call-start = ((), (), s32[]{:S(2)}) async-start(), calls=%async_computation | async-start | bytes 7299072 | tf_op jit(solution)/shard_map/all_gather | solution.py:494
  9.1 246.1 %all-gather.6.cloned.1.call-start = ((), (), s32[]{:S(2)}) async-start(), calls=%async_computation.1 | async-start | bytes 11354112 | tf_op jit(solution)/shard_map/all_gather | solution.py:520
  13.4 0.6 copy-start.10
  104.4 5.8 %copy-start.2 = (bf16[3,3072,384]{2,1,0:T(8,128)(2,1)S(1)}, bf16[3,3072,384]{2,1,0:T(8,128)(2,1)}, u32[]{:S(2)}) copy-start(bf16[3,3072,384]{2,1,0:T(8,128)(2,1)} %all-gather.4.cloned.1.call-done) | copy-start | bytes 21233668
  104.4 5.8 %copy-start.11 = (bf16[4,3072]{1,0:T(4,128)(2,1)S(1)}, bf16[4,3072]{1,0:T(4,128)(2,1)}, u32[]{:S(2)}) copy-start(bf16[4,3072]{1,0:T(4,128)(2,1)} %copy-done.10) | copy-start | bytes 73732
  111.4 3.1 copy-start.3
  115.3 0.6 copy-start.15
  121.0 0.6 copy-start.16
  123.7 5.2 %copy-start.5 = (bf16[1,100,384]{1,2,0:T(8,128)(2,1)S(1)}, bf16[1,100,384]{1,2,0:T(8,128)(2,1)}, u32[]{:S(2)}) copy-start(bf16[1,100,384]{1,2,0:T(8,128)(2,1)} %copy.47) | copy-start | bytes 230404
  132.3 7.4 %copy-start.6 = (bf16[1,100,384]{2,1,0:T(8,128)(2,1)S(1)}, bf16[1,100,384]{2,1,0:T(8,128)(2,1)}, u32[]{:S(2)}) copy-start(bf16[1,100,384]{2,1,0:T(8,128)(2,1)} %slice.252) | copy-start | bytes 230404
  146.1 7.6 %copy-start.19 = (s32[2,2]{1,0:T(2,128)S(1)}, s32[2,2]{1,0:T(2,128)}, u32[]{:S(2)}) copy-start(s32[2,2]{1,0:T(2,128)} %param.18) | copy-start | bytes 52
  160.7 105.9 %slice-start = ((s8[4718592]{0:T(1024)(128)(4,1)}), s8[524288]{0:T(1024)(128)(4,1)S(1)}, s32[]{:S(2)}) async-start(s8[4718592]{0:T(1024)(128)(4,1)} %bitcast.150), calls=%async_computation.2 | async-start | bytes 1048576
  255.2 11.4 %slice-start.1 = ((s8[4718592]{0:T(1024)(128)(4,1)}), s8[4194304]{0:T(1024)(128)(4,1)S(1)}, s32[]{:S(2)}) async-start(s8[4718592]{0:T(1024)(128)(4,1)} %bitcast.150), calls=%async_computation.3 | async-start | bytes 8388608
  268.4 17.2 %copy-start.14 = (f32[1,1,3072]{2,1,0:T(1,128)S(1)}, f32[1,1,3072]{2,1,0:T(1,128)}, u32[]{:S(2)}) copy-start(f32[1,1,3072]{2,1,0:T(1,128)} %get-tuple-element.21) | copy-start | bytes 36868
  268.4 18.6 %copy-start.12 = (f32[1,1,3072]{2,1,0:T(1,128)S(1)}, f32[1,1,3072]{2,1,0:T(1,128)}, u32[]{:S(2)}) copy-start(f32[1,1,3072]{2,1,0:T(1,128)} %get-tuple-element.17) | copy-start | bytes 36868
  364.6 66.7 %copy-start.13 = (f32[1,1,3072]{2,1,0:T(1,128)S(1)}, f32[1,1,3072]{2,1,0:T(1,128)}, u32[]{:S(2)}) copy-start(f32[1,1,3072]{2,1,0:T(1,128)} %get-tuple-element.18) | copy-start | bytes 36868
  364.6 68.1 %copy-start.17 = (f32[1,1,3072]{2,1,0:T(1,128)S(1)}, f32[1,1,3072]{2,1,0:T(1,128)}, u32[]{:S(2)}) copy-start(f32[1,1,3072]{2,1,0:T(1,128)} %get-tuple-element.15) | copy-start | bytes 36868
  364.6 68.2 %copy-start.18 = (f32[1,1,3072]{2,1,0:T(1,128)S(1)}, f32[1,1,3072]{2,1,0:T(1,128)}, u32[]{:S(2)}) copy-start(f32[1,1,3072]{2,1,0:T(1,128)} %get-tuple-element.22) | copy-start | bytes 36868
  364.6 68.2 %copy-start.20 = (bf16[3072,64]{0,1:T(8,128)(2,1)S(1)}, bf16[3072,64]{0,1:T(8,128)(2,1)}, u32[]{:S(2)}) copy-start(bf16[3072,64]{0,1:T(8,128)(2,1)} %param.27) | copy-start | bytes 1179652
  364.6 68.2 %copy-start.21 = (f32[1,24,64]{2,1,0:T(8,128)S(1)}, f32[1,24,64]{2,1,0:T(8,128)}, u32[]{:S(2)}) copy-start(f32[1,24,64]{2,1,0:T(8,128)} %param.28) | copy-start | bytes 18436
  431.3 10.6 %copy-start.8 = (bf16[3,3,16,512]{3,2,1,0:T(8,128)(2,1)S(1)}, bf16[3,3,16,512]{3,2,1,0:T(8,128)(2,1)}, u32[]{:S(2)}) copy-start(bf16[3,3,16,512]{3,2,1,0:T(8,128)(2,1)} %param.29) | copy-start | bytes 442372
  432.5 24.0 %copy-start.4 = (bf16[24,3072]{1,0:T(8,128)(2,1)}, bf16[24,3072]{1,0:T(8,128)(2,1)S(1)}, u32[]{:S(2)}) copy-start(bf16[24,3072]{1,0:T(8,128)(2,1)S(1)} %get-tuple-element.8) | copy-start | bytes 442372
  434.1 7.9 %collective-permute-start.1 = (bf16[6,1,8,16]{3,2,1,0:T(8,128)(2,1)S(1)}, bf16[6,1,8,16]{3,2,1,0:T(8,128)(2,1)S(1)}, u32[]{:S(2)}, u32[]{:S(2)}) collective-permute-start(bf16[6,1,8,16]{3,2,1,0:T(8,128)(2,1)S(1)} %get-tuple-element.26), channel_id=1, source_target_pairs={{4,0},{8,4},{12,8},{16,12},{20,16},{24,20},{28,24},{32,28},{36,32}... | collective-permute-start | bytes 4616 | tf_op jit(solution)/shard_map/ppermute | solution.py:33
  440.0 7.7 %collective-permute-start = (bf16[6,1,8,16]{3,2,1,0:T(8,128)(2,1)S(1)}, bf16[6,1,8,16]{3,2,1,0:T(8,128)(2,1)S(1)}, u32[]{:S(2)}, u32[]{:S(2)}) collective-permute-start(bf16[6,1,8,16]{3,2,1,0:T(8,128)(2,1)S(1)} %get-tuple-element.25), channel_id=1, source_target_pairs={{0,4},{4,8},{8,12},{12,16},{16,20},{20,24},{24,28},{28,32},{32,36}... | collective-permute-start | bytes 4616 | tf_op jit(solution)/shard_map/ppermute | solution.py:31
  447.7 8.7 %collective-permute-start.3 = (bf16[6,4,1,16]{3,2,1,0:T(2,128)(2,1)S(1)}, bf16[6,4,1,16]{3,2,1,0:T(2,128)(2,1)S(1)}, u32[]{:S(2)}, u32[]{:S(2)}) collective-permute-start(bf16[6,4,1,16]{3,2,1,0:T(2,128)(2,1)S(1)} %get-tuple-element.24), channel_id=1, source_target_pairs={{1,0},{2,1},{3,2},{5,4},{6,5},{7,6},{9,8},{10,9},{11,10},{13,12},{... | collective-permute-start | bytes 2312 | tf_op jit(solution)/shard_map/ppermute | solution.py:33
  449.0 7.1 %collective-permute-start.2 = (bf16[6,4,1,16]{3,2,1,0:T(2,128)(2,1)S(1)}, bf16[6,4,1,16]{3,2,1,0:T(2,128)(2,1)S(1)}, u32[]{:S(2)}, u32[]{:S(2)}) collective-permute-start(bf16[6,4,1,16]{3,2,1,0:T(2,128)(2,1)S(1)} %get-tuple-element.23), channel_id=1, source_target_pairs={{0,1},{1,2},{2,3},{4,5},{5,6},{6,7},{8,9},{9,10},{10,11},{12,13},{... | collective-permute-start | bytes 2312 | tf_op jit(solution)/shard_map/ppermute | solution.py:31
Sparse Core Ops, SparseCore 0:
  10.6 93.7 all-gather.3
  146.3 108.8 all-gather.5

commit v8 on v7

--- a/solution.py
+++ b/solution.py
@@ -494,15 +494,15 @@
     gathered_half = lax.all_gather(own_half, "row", axis=1, tiled=True)
     half_heads = half_cols // head_dim
 
-    def project(rows):
-        mixed_cols = jnp.einsum("ld,cde->cle", rows, gathered_half, preferred_element_type=jnp.float32)
-        split = mixed_cols.reshape(3, span, half_heads, head_dim)
-        return jnp.stack(
-            [head_norm(split[0], q_gain), head_norm(split[1], k_gain), split[2].astype(jnp.bfloat16)]
-        )
-
-    mine = project(joined)
-    theirs = project(partner_swap(joined, 4))
+    both_rows = jnp.concatenate([joined, partner_swap(joined, 4)], axis=0)
+    projected_rows = jnp.einsum(
+        "ld,cde->cle", both_rows, gathered_half, preferred_element_type=jnp.float32
+    ).reshape(3, 2 * span, half_heads, head_dim)
+    normed_q = head_norm(projected_rows[0], q_gain)
+    normed_k = head_norm(projected_rows[1], k_gain)
+    plain_v = projected_rows[2].astype(jnp.bfloat16)
+    mine = jnp.stack([normed_q[:span], normed_k[:span], plain_v[:span]])
+    theirs = jnp.stack([normed_q[span:], normed_k[span:], plain_v[span:]])
     received = partner_swap(theirs.reshape(3 * span, half_cols), 5).reshape(theirs.shape)
     full = jnp.concatenate(
         [jnp.where(request_id == 0, mine, received), jnp.where(request_id == 0, received, mine)], axis=2

time: 467 us -> 458 us (0.981)
  other arithmetic: 32.8 us -> 26.3 us
where the time goes in v8:
time: 458 us; the launch traced here: 456 us
  waiting for transfers between devices  184 us (40%)
  Pallas kernels  168 us (37%)
  other arithmetic  26.3 us (6%)
  local copies, waits for them, and re-layouts  22.5 us (5%)
  matrix products  20.9 us (5%)
  between operations  18.4 us (4%)
  starting transfers between devices  15.6 us (3%)
    all_gather x1, waiting for transfers between devices, shards(): gathered = lax.all_gather(both, 'row', axis=0, tiled=True)  92.1 us
    all_gather x1, waiting for transfers between devices, shards(): gathered_half = lax.all_gather(own_half, 'row', axis=1, tiled=True)  85.4 us
    pallas_call x1, Pallas kernels, ring_gather(): pl.pallas_call(functools.partial(ring_gather_kernel, zs, xs), out_shape=j...  66.5 us
    pallas_call x1, Pallas kernels, ring_scatter_sum(): pl.pallas_call(functools.partial(ring_scatter_kernel, zs, xs), out_shape=...  65.2 us
    pallas_call x1, Pallas kernels, scatter_sum(): pl.pallas_call(functools.partial(scatter_sum_kernel, axis, count, rows),...  17.2 us
    pallas_call x1, Pallas kernels, attention(): pl.pallas_call(functools.partial(attention_kernel, scale), out_shape=jax....  11.3 us
    dot_general x1, matrix products, shards(): jnp.dot(hidden_units, w_down, preferred_element_type=jnp.float32)  10.4 us
  transfers between devices with their start and end apart: 6, of which 4 were waited for; matrix products, arithmetic and copies ran while one was open for 4% of the time, Pallas kernels for 1%

profile of v8, /device:TPU:2, one launch (start us, length us, event | category | flops | bytes accessed | tf_op | source)
XLA Modules:
  0.0 455.6 jit_solution(9834879676313016949)
XLA Ops:
  7.3 1.8 constant_dynamic-slice_fusion
  9.1 0.9 convert_reduce_fusion.3
  10.0 0.9 fusion.49
  11.0 1.2 convert_reduce_fusion
  12.2 0.3 multiply_reduce_fusion
  12.6 0.7 slice_add_fusion
  13.4 0.3 add_convert_fusion
  13.7 0.3 copy-done.7
  14.0 0.9 pad_maximum_fusion.src_ref
  14.8 4.1 shard_map.166
  19.0 85.4 %all-gather.4.cloned.1.call-done = bf16[3,3072,384]{2,1,0:T(8,128)(2,1)} async-done(((bf16[3,96,384]{2,1,0:T(8,128)(2,1)}), bf16[3,3072,384]{2,1,0:T(8,128)(2,1)}) %all-gather.4.cloned.1.call-update) | async-done | bytes 7077904 | tf_op jit(solution)/shard_map/all_gather | solution.py:494
  104.4 5.8 %fusion.140 = (bf16[3,200,384]{2,1,0:T(8,128)(2,1)S(1)}, f32[3,200,384]{2,1,0:T(8,128)}) fusion(bf16[3,3072,384]{2,1,0:T(8,128)(2,1)} %all-gather.4.cloned.1.call-done, bf16[100,3072]{1,0:T(8,128)(2,1)} %shard_map.166, bf16[4,3072]{1,0:T(4,128)(2,1)} %copy-done.7, bf16[96,3072]{1,0:T(8,128)(2,1)S(1)} %add_convert_fusion), kind=kOutput, calls=%fused_computation.228 | convolution fusion | flops 1419494400 | bytes 9689088 | tf_op jit(solution)/shard_map/ld,cde->cle/dot_general | solution.py:498
  110.3 1.9 fusion.137
  112.3 1.1 copy.33
  113.6 1.9 copy.32
  115.4 1.6 reduce_sum.184
  117.1 0.7 broadcast_multiply_fusion.1
  117.8 1.1 multiply_reduce_fusion.2
  119.0 0.8 multiply_convert_fusion.1
  119.8 0.8 slice_bitcast_fusion.2
  120.6 1.2 copy.54
  121.8 2.1 reshape.435.src_ref
  123.9 3.2 shard_map.167
  127.1 2.1 reshape.436
  129.2 2.1 copy.39
  131.3 0.7 copy.34
  132.0 1.2 broadcast_select_fusion.1
  133.2 0.8 pad_maximum_fusion.1
  134.0 1.9 copy.58
  135.9 1.7 pad.7.clone
  137.7 1.1 convert_element_type.80
  138.9 0.3 reduce-window.9
  139.3 1.3 select_reduce_fusion.4
  141.4 1.2 select_reduce_fusion
  145.2 0.2 slice_reduce_fusion.2
  145.4 0.6 select_reduce_fusion.2
  146.7 0.7 and_convert_fusion
  147.4 1.3 select_reduce_fusion.5
  148.7 0.7 fusion.120
  149.4 2.8 select_convert_fusion.live_ref
  152.2 0.7 pad_maximum_fusion.4
  152.9 1.7 copy.42.q_ref
  154.6 92.1 %all-gather.6.cloned.1.call-done = bf16[64,112,768]{2,1,0:T(8,128)(2,1)} async-done(((bf16[2,112,768]{2,1,0:T(8,128)(2,1)}), bf16[64,112,768]{2,1,0:T(8,128)(2,1)}) %all-gather.6.cloned.1.call-update) | async-done | bytes 11010064 | tf_op jit(solution)/shard_map/all_gather | solution.py:520
  246.7 11.3 %shard_map.168 = bf16[96,768]{1,0:T(8,128)(2,1)} custom-call(bf16[96,768]{1,0:T(8,128)(2,1)} %copy.42.q_ref, bf16[32,2,112,768]{3,2,1,0:T(8,128)(2,1)} %bitcast.147, f32[1,3584]{1,0:T(1,128)} %select_convert_fusion.live_ref), custom_call_target="tpu_custom_call" | custom-call | tf_op jit(solution)/shard_map/pallas_call | solution.py:130
  258.1 1.8 fusion.143.part_ref
  259.9 17.2 %shard_map.169 = f32[24,3072]{1,0:T(8,128)S(1)} custom-call(f32[96,3072]{1,0:T(8,128)S(1)} %fusion.143.part_ref), custom_call_target="tpu_custom_call" | custom-call | tf_op jit(solution)/shard_map/pallas_call | solution.py:89
  277.1 1.0 fusion.40
  278.3 0.2 fusion.31
  278.5 0.8 fusion.34.block_ref
  279.3 66.5 %shard_map.170 = bf16[8,4,24,3072]{3,2,1,0:T(8,128)(2,1)} custom-call(bf16[24,3072]{1,0:T(8,128)(2,1)} %fusion.34.block_ref), custom_call_target="tpu_custom_call" | custom-call | tf_op jit(solution)/shard_map/pallas_call | solution.py:322
  345.9 10.4 %convolution_convert_fusion = bf16[768,3072]{1,0:T(8,128)(2,1)} fusion(bf16[384,3072]{1,0:T(8,128)(2,1)S(1)} %copy-done, bf16[768,3072]{1,0:T(8,128)(2,1)} %bitcast.156, bf16[3072,384]{1,0:T(8,128)(2,1)} %param.25), kind=kOutput, calls=%fused_computation | convolution fusion | flops 3628892160 | bytes 14155776 | tf_op jit(solution)/shard_map/dot_general | solution.py:545
  356.3 65.2 %shard_map.171 = f32[24,3072]{1,0:T(8,128)} custom-call(bf16[8,4,24,3072]{3,2,1,0:T(8,128)(2,1)} %bitcast.157), custom_call_target="tpu_custom_call" | custom-call | tf_op jit(solution)/shard_map/pallas_call | solution.py:231
  421.5 1.2 convert_reduce_fusion.2
  422.7 0.2 fusion.35
  423.0 0.9 multiply_convert_fusion.2
  424.1 0.3 copy.44
  424.4 6.5 %collective-permute-start.1 = (bf16[6,1,8,16]{3,2,1,0:T(8,128)(2,1)S(1)}, bf16[6,1,8,16]{3,2,1,0:T(8,128)(2,1)S(1)}, u32[]{:S(2)}, u32[]{:S(2)}) collective-permute-start(bf16[6,1,8,16]{3,2,1,0:T(8,128)(2,1)S(1)} %get-tuple-element.30), channel_id=1, source_target_pairs={{4,0},{8,4},{12,8},{16,12},{20,16},{24,20},{28,24},{32,28},{36,32}... | collective-permute-start | bytes 4616 | tf_op jit(solution)/shard_map/ppermute | solution.py:33
  430.9 1.9 collective-permute-start
  433.0 5.6 %collective-permute-done = bf16[6,1,8,16]{3,2,1,0:T(8,128)(2,1)S(1)} collective-permute-done((bf16[6,1,8,16]{3,2,1,0:T(8,128)(2,1)S(1)}, bf16[6,1,8,16]{3,2,1,0:T(8,128)(2,1)S(1)}, u32[]{:S(2)}, u32[]{:S(2)}) %collective-permute-start) | collective-permute-done | bytes 1568 | tf_op jit(solution)/shard_map/ppermute | solution.py:31
  438.6 1.3 collective-permute-start.3
  439.9 5.8 %collective-permute-start.2 = (bf16[6,4,1,16]{3,2,1,0:T(2,128)(2,1)S(1)}, bf16[6,4,1,16]{3,2,1,0:T(2,128)(2,1)S(1)}, u32[]{:S(2)}, u32[]{:S(2)}) collective-permute-start(bf16[6,4,1,16]{3,2,1,0:T(2,128)(2,1)S(1)} %get-tuple-element.27), channel_id=1, source_target_pairs={{0,1},{1,2},{2,3},{4,5},{5,6},{6,7},{8,9},{9,10},{10,11},{12,13},{... | collective-permute-start | bytes 2312 | tf_op jit(solution)/shard_map/ppermute | solution.py:31
  446.1 1.1 collective-permute-done.2
  447.8 0.2 fusion.17
  447.9 0.8 fusion.19
  (81 shorter events, 2.6 us)
Async XLA Ops:
  7.2 338.7 %copy-start = (bf16[384,3072]{1,0:T(8,128)(2,1)S(1)}, bf16[384,3072]{1,0:T(8,128)(2,1)}, u32[]{:S(2)}) copy-start(bf16[384,3072]{1,0:T(8,128)(2,1)} %param.26) | copy-start | bytes 7077892
  7.2 6.1 %copy-start.4 = (bf16[1,4,3072]{2,1,0:T(4,128)(2,1)S(1)}, bf16[1,4,3072]{2,1,0:T(4,128)(2,1)}, u32[]{:S(2)}) copy-start(bf16[1,4,3072]{2,1,0:T(4,128)(2,1)} %param.16) | copy-start | bytes 73732
  7.2 5.0 %copy-start.1 = (bf16[1,96,3072]{2,1,0:T(8,128)(2,1)S(1)}, bf16[1,96,3072]{2,1,0:T(8,128)(2,1)}, u32[]{:S(2)}) copy-start(bf16[1,96,3072]{2,1,0:T(8,128)(2,1)} %param.15) | copy-start | bytes 1769476
  7.2 5.4 %copy-start.6 = (f32[1,8,3072]{2,1,0:T(8,128)S(1)}, f32[1,8,3072]{2,1,0:T(8,128)}, u32[]{:S(2)}) copy-start(f32[1,8,3072]{2,1,0:T(8,128)} %param.20) | copy-start | bytes 294916
  7.2 97.2 %all-gather.4.cloned.1.call-start = ((), (), s32[]{:S(2)}) async-start(), calls=%async_computation | async-start | bytes 7299072 | tf_op jit(solution)/shard_map/all_gather | solution.py:494
  9.1 237.7 %all-gather.6.cloned.1.call-start = ((), (), s32[]{:S(2)}) async-start(), calls=%async_computation.1 | async-start | bytes 11354112 | tf_op jit(solution)/shard_map/all_gather | solution.py:520
  13.4 0.6 copy-start.7
  113.4 5.5 %copy-start.14 = (f32[64]{0:T(128)S(1)}, f32[64]{0:T(128)}, u32[]{:S(2)}) copy-start(f32[64]{0:T(128)} %param.22) | copy-start | bytes 772
  117.1 1.9 copy-start.2
  137.6 7.6 %copy-start.13 = (s32[2,2]{1,0:T(2,128)S(1)}, s32[2,2]{1,0:T(2,128)}, u32[]{:S(2)}) copy-start(s32[2,2]{1,0:T(2,128)} %param.18) | copy-start | bytes 52
  152.2 105.9 %slice-start = ((s8[4718592]{0:T(1024)(128)(4,1)}), s8[524288]{0:T(1024)(128)(4,1)S(1)}, s32[]{:S(2)}) async-start(s8[4718592]{0:T(1024)(128)(4,1)} %bitcast.154), calls=%async_computation.2 | async-start | bytes 1048576
  246.7 11.4 %slice-start.1 = ((s8[4718592]{0:T(1024)(128)(4,1)}), s8[4194304]{0:T(1024)(128)(4,1)S(1)}, s32[]{:S(2)}) async-start(s8[4718592]{0:T(1024)(128)(4,1)} %bitcast.154), calls=%async_computation.3 | async-start | bytes 8388608
  259.9 17.2 %copy-start.10 = (f32[1,1,3072]{2,1,0:T(1,128)S(1)}, f32[1,1,3072]{2,1,0:T(1,128)}, u32[]{:S(2)}) copy-start(f32[1,1,3072]{2,1,0:T(1,128)} %get-tuple-element.25) | copy-start | bytes 36868
  259.9 18.6 %copy-start.8 = (f32[1,1,3072]{2,1,0:T(1,128)S(1)}, f32[1,1,3072]{2,1,0:T(1,128)}, u32[]{:S(2)}) copy-start(f32[1,1,3072]{2,1,0:T(1,128)} %get-tuple-element.21) | copy-start | bytes 36868
  356.2 65.3 %copy-start.9 = (f32[1,1,3072]{2,1,0:T(1,128)S(1)}, f32[1,1,3072]{2,1,0:T(1,128)}, u32[]{:S(2)}) copy-start(f32[1,1,3072]{2,1,0:T(1,128)} %get-tuple-element.22) | copy-start | bytes 36868
  356.3 66.7 %copy-start.11 = (f32[1,1,3072]{2,1,0:T(1,128)S(1)}, f32[1,1,3072]{2,1,0:T(1,128)}, u32[]{:S(2)}) copy-start(f32[1,1,3072]{2,1,0:T(1,128)} %get-tuple-element.19) | copy-start | bytes 36868
  356.3 66.7 %copy-start.12 = (f32[1,1,3072]{2,1,0:T(1,128)S(1)}, f32[1,1,3072]{2,1,0:T(1,128)}, u32[]{:S(2)}) copy-start(f32[1,1,3072]{2,1,0:T(1,128)} %get-tuple-element.26) | copy-start | bytes 36868
  356.3 66.7 %copy-start.15 = (bf16[3072,64]{0,1:T(8,128)(2,1)S(1)}, bf16[3072,64]{0,1:T(8,128)(2,1)}, u32[]{:S(2)}) copy-start(bf16[3072,64]{0,1:T(8,128)(2,1)} %param.27) | copy-start | bytes 1179652
  356.3 66.7 %copy-start.16 = (f32[1,24,64]{2,1,0:T(8,128)S(1)}, f32[1,24,64]{2,1,0:T(8,128)}, u32[]{:S(2)}) copy-start(f32[1,24,64]{2,1,0:T(8,128)} %param.28) | copy-start | bytes 18436
  421.5 11.3 %copy-start.5 = (bf16[3,3,16,512]{3,2,1,0:T(8,128)(2,1)S(1)}, bf16[3,3,16,512]{3,2,1,0:T(8,128)(2,1)}, u32[]{:S(2)}) copy-start(bf16[3,3,16,512]{3,2,1,0:T(8,128)(2,1)} %param.29) | copy-start | bytes 442372
  422.7 24.8 %copy-start.3 = (bf16[24,3072]{1,0:T(8,128)(2,1)}, bf16[24,3072]{1,0:T(8,128)(2,1)S(1)}, u32[]{:S(2)}) copy-start(bf16[24,3072]{1,0:T(8,128)(2,1)S(1)} %get-tuple-element.8) | copy-start | bytes 442372
  424.4 8.6 %collective-permute-start.1 = (bf16[6,1,8,16]{3,2,1,0:T(8,128)(2,1)S(1)}, bf16[6,1,8,16]{3,2,1,0:T(8,128)(2,1)S(1)}, u32[]{:S(2)}, u32[]{:S(2)}) collective-permute-start(bf16[6,1,8,16]{3,2,1,0:T(8,128)(2,1)S(1)} %get-tuple-element.30), channel_id=1, source_target_pairs={{4,0},{8,4},{12,8},{16,12},{20,16},{24,20},{28,24},{32,28},{36,32}... | collective-permute-start | bytes 4616 | tf_op jit(solution)/shard_map/ppermute | solution.py:33
  430.9 7.7 %collective-permute-start = (bf16[6,1,8,16]{3,2,1,0:T(8,128)(2,1)S(1)}, bf16[6,1,8,16]{3,2,1,0:T(8,128)(2,1)S(1)}, u32[]{:S(2)}, u32[]{:S(2)}) collective-permute-start(bf16[6,1,8,16]{3,2,1,0:T(8,128)(2,1)S(1)} %get-tuple-element.29), channel_id=1, source_target_pairs={{0,4},{4,8},{8,12},{12,16},{16,20},{20,24},{24,28},{28,32},{32,36}... | collective-permute-start | bytes 4616 | tf_op jit(solution)/shard_map/ppermute | solution.py:31
  438.6 8.8 %collective-permute-start.3 = (bf16[6,4,1,16]{3,2,1,0:T(2,128)(2,1)S(1)}, bf16[6,4,1,16]{3,2,1,0:T(2,128)(2,1)S(1)}, u32[]{:S(2)}, u32[]{:S(2)}) collective-permute-start(bf16[6,4,1,16]{3,2,1,0:T(2,128)(2,1)S(1)} %get-tuple-element.28), channel_id=1, source_target_pairs={{1,0},{2,1},{3,2},{5,4},{6,5},{7,6},{9,8},{10,9},{11,10},{13,12},{... | collective-permute-start | bytes 2312 | tf_op jit(solution)/shard_map/ppermute | solution.py:33
  439.9 7.2 %collective-permute-start.2 = (bf16[6,4,1,16]{3,2,1,0:T(2,128)(2,1)S(1)}, bf16[6,4,1,16]{3,2,1,0:T(2,128)(2,1)S(1)}, u32[]{:S(2)}, u32[]{:S(2)}) collective-permute-start(bf16[6,4,1,16]{3,2,1,0:T(2,128)(2,1)S(1)} %get-tuple-element.27), channel_id=1, source_target_pairs={{0,1},{1,2},{2,3},{4,5},{5,6},{6,7},{8,9},{9,10},{10,11},{12,13},{... | collective-permute-start | bytes 2312 | tf_op jit(solution)/shard_map/ppermute | solution.py:31
Sparse Core Ops, SparseCore 0:
  10.6 93.7 all-gather.3
  137.8 108.8 all-gather.5

commit v9 on v8

--- a/solution.py
+++ b/solution.py
@@ -368,6 +368,86 @@
     )(value)
 
 
+def halo_kernel(tile_ref, out_ref, slots, send_sems, recv_sems):
+    req = lax.axis_index("req")
+    row = lax.axis_index("row")
+    col = lax.axis_index("col")
+    rows = lax.axis_size("row")
+    cols = lax.axis_size("col")
+    offsets = [(a, b) for a in (-1, 0, 1) for b in (-1, 0, 1) if (a, b) != (0, 0)]
+
+    def present(a, b):
+        return (row + a >= 0) & (row + a < rows) & (col + b >= 0) & (col + b < cols)
+
+    def link(a, b):
+        return pltpu.make_async_remote_copy(
+            src_ref=tile_ref,
+            dst_ref=slots.at[1 - a, 1 - b],
+            send_sem=send_sems.at[1 + a, 1 + b],
+            recv_sem=recv_sems.at[1 - a, 1 - b],
+            device_id=(req, row + a, col + b),
+            device_id_type=MESH_IDS,
+        )
+
+    barrier = pltpu.get_barrier_semaphore()
+    for a, b in offsets:
+        @pl.when(present(a, b))
+        def _():
+            pl.semaphore_signal(barrier, inc=1, device_id=(req, row + a, col + b), device_id_type=MESH_IDS)
+    up = (row + rows - 1) // rows
+    down = (2 * rows - 2 - row) // rows
+    left = (col + cols - 1) // cols
+    right = (2 * cols - 2 - col) // cols
+    pl.semaphore_wait(barrier, (1 + up + down) * (1 + left + right) - 1)
+    for a, b in offsets:
+        @pl.when(present(a, b))
+        def _():
+            link(a, b).start()
+    for a, b in offsets:
+        @pl.when(present(a, b))
+        def _():
+            copy = link(a, b)
+            copy.wait_send()
+            pltpu.make_async_remote_copy(
+                src_ref=tile_ref,
+                dst_ref=slots.at[1 + a, 1 + b],
+                send_sem=send_sems.at[1 + a, 1 + b],
+                recv_sem=recv_sems.at[1 + a, 1 + b],
+                device_id=(req, row + a, col + b),
+                device_id_type=MESH_IDS,
+            ).wait_recv()
+            out_ref[1 + a, 1 + b] = slots[1 + a, 1 + b]
+
+        @pl.when(jnp.logical_not(present(a, b)))
+        def _():
+            out_ref[1 + a, 1 + b] = jnp.zeros(out_ref.shape[2:], out_ref.dtype)
+    out_ref[1, 1] = tile_ref[...]
+
+
+def halo_extend(tile):
+    gathered = pl.pallas_call(
+        halo_kernel,
+        out_shape=jax.ShapeDtypeStruct((3, 3) + tile.shape, tile.dtype),
+        in_specs=[pl.BlockSpec(memory_space=pltpu.VMEM)],
+        out_specs=pl.BlockSpec(memory_space=pltpu.VMEM),
+        scratch_shapes=[
+            pltpu.VMEM((3, 3) + tile.shape, tile.dtype),
+            pltpu.SemaphoreType.DMA((3, 3)),
+            pltpu.SemaphoreType.DMA((3, 3)),
+        ],
+        compiler_params=pltpu.CompilerParams(collective_id=6, has_side_effects=True),
+    )(tile)
+    bands = []
+    for a, pick_rows in ((0, slice(-1, None)), (1, slice(None)), (2, slice(0, 1))):
+        pieces = [
+            gathered[a, 0][:, pick_rows, -1:],
+            gathered[a, 1][:, pick_rows, :],
+            gathered[a, 2][:, pick_rows, :1],
+        ]
+        bands.append(jnp.concatenate(pieces, axis=2))
+    return jnp.concatenate(bands, axis=1)
+
+
 def layer_norm(tensor, epsilon):
     average = jnp.mean(tensor, axis=-1, keepdims=True)
     centered = tensor - average
@@ -561,7 +641,7 @@
         .reshape(FR, 2 * TR, 2 * TC, CH)
     )
     scaled = (pixels / latent_scale).astype(jnp.bfloat16)
-    padded = extended(scaled, (("row", 1), ("col", 2)), 1)
+    padded = halo_extend(scaled)
     running = jnp.zeros((FR, 2 * TR, 2 * TC, conv_w.shape[3]), jnp.float32)
     for row_tap in range(3):
         for col_tap in range(3):

time: 458 us -> 450 us (0.983)
  starting transfers between devices: 15.6 us -> 0.08 us
  Pallas kernels: 168 us -> 179 us
  waiting for transfers between devices: 184 us -> 178 us
    ppermute x4 -> x0, starting transfers between devices: 15.6 us -> none  [the longest x2 7.81 us: extended(): lax.ppermute(head, axis, [((i + 1) % count, i) for i in range(ends)])]
    pallas_call x0 -> x1, Pallas kernels: none -> 9.83 us  [halo_extend(): pl.pallas_call(halo_kernel, out_shape=jax.ShapeDtypeStruct((3, 3) + tile....]
    ppermute x4 -> x0, waiting for transfers between devices: 6.7 us -> none  [the longest x2 6.69 us: extended(): lax.ppermute(tail, axis, [(i, (i + 1) % count) for i in range(ends)])]
  transfers between devices with their start and end apart: 6 -> 2, of which waited for: 4 -> 2; matrix products, arithmetic and copies ran while one was open for 4% -> 4% of each run, Pallas kernels for 1% -> 1%
where the time goes in v9:
time: 450 us; the launch traced here: 447 us
  Pallas kernels  179 us (40%)
  waiting for transfers between devices  178 us (40%)
  other arithmetic  26.3 us (6%)
  local copies, waits for them, and re-layouts  24 us (5%)
  matrix products  21.6 us (5%)
  between operations  18.5 us (4%)
    all_gather x1, waiting for transfers between devices, shards(): gathered = lax.all_gather(both, 'row', axis=0, tiled=True)  92.1 us
    all_gather x1, waiting for transfers between devices, shards(): gathered_half = lax.all_gather(own_half, 'row', axis=1, tiled=True)  85.4 us
    pallas_call x1, Pallas kernels, ring_scatter_sum(): pl.pallas_call(functools.partial(ring_scatter_kernel, zs, xs), out_shape=...  67.3 us
    pallas_call x1, Pallas kernels, ring_gather(): pl.pallas_call(functools.partial(ring_gather_kernel, zs, xs), out_shape=j...  66.1 us
    pallas_call x1, Pallas kernels, scatter_sum(): pl.pallas_call(functools.partial(scatter_sum_kernel, axis, count, rows),...  17.2 us
    pallas_call x1, Pallas kernels, attention(): pl.pallas_call(functools.partial(attention_kernel, scale), out_shape=jax....  11.3 us
    dot_general x1, matrix products, shards(): jnp.dot(hidden_units, w_down, preferred_element_type=jnp.float32)  10.4 us
    pallas_call x1, Pallas kernels, halo_extend(): pl.pallas_call(halo_kernel, out_shape=jax.ShapeDtypeStruct((3, 3) + tile....  9.83 us
  transfers between devices with their start and end apart: 2, of which 2 were waited for; matrix products, arithmetic and copies ran while one was open for 4% of the time, Pallas kernels for 1%

profile of v9, /device:TPU:2, one launch (start us, length us, event | category | flops | bytes accessed | tf_op | source)
XLA Modules:
  0.0 447.2 jit_solution(335205102406903692)
XLA Ops:
  7.3 1.8 constant_dynamic-slice_fusion
  9.1 0.9 convert_reduce_fusion.3
  10.0 0.9 fusion.43
  11.0 1.2 convert_reduce_fusion
  12.2 0.3 multiply_reduce_fusion
  12.6 0.7 slice_add_fusion
  13.4 0.3 add_convert_fusion
  13.7 0.3 copy-done.7
  14.0 0.9 pad_maximum_fusion.src_ref
  14.8 4.1 shard_map.166
  19.0 85.4 %all-gather.4.cloned.1.call-done = bf16[3,3072,384]{2,1,0:T(8,128)(2,1)} async-done(((bf16[3,96,384]{2,1,0:T(8,128)(2,1)}), bf16[3,3072,384]{2,1,0:T(8,128)(2,1)}) %all-gather.4.cloned.1.call-update) | async-done | bytes 7077904 | tf_op jit(solution)/shard_map/all_gather | solution.py:574
  104.4 5.8 %fusion.93 = (bf16[3,200,384]{2,1,0:T(8,128)(2,1)S(1)}, f32[3,200,384]{2,1,0:T(8,128)}) fusion(bf16[3,3072,384]{2,1,0:T(8,128)(2,1)} %all-gather.4.cloned.1.call-done, bf16[100,3072]{1,0:T(8,128)(2,1)} %shard_map.166, bf16[4,3072]{1,0:T(4,128)(2,1)} %copy-done.7, bf16[96,3072]{1,0:T(8,128)(2,1)S(1)} %add_convert_fusion), kind=kOutput, calls=%fused_computation.191 | convolution fusion | flops 1419494400 | bytes 9689088 | tf_op jit(solution)/shard_map/ld,cde->cle/dot_general | solution.py:578
  110.3 1.9 fusion.91
  112.3 1.1 copy.33
  113.6 1.9 copy.32
  115.4 1.6 reduce_sum.184
  117.1 0.7 broadcast_multiply_fusion.1
  117.8 1.1 multiply_reduce_fusion.2
  119.0 0.8 multiply_convert_fusion.1
  119.8 0.8 slice_bitcast_fusion.2
  120.6 1.2 copy.54
  121.8 2.1 reshape.431.src_ref
  123.9 3.2 shard_map.167
  127.1 2.1 reshape.432
  129.2 2.1 copy.39
  131.3 0.7 copy.34
  132.0 1.2 broadcast_select_fusion.1
  133.2 0.8 pad_maximum_fusion.1
  134.0 1.9 copy.58
  135.9 1.7 pad.7.clone
  137.7 1.1 convert_element_type.74
  138.9 0.3 reduce-window.9
  139.3 1.3 select_reduce_fusion.4
  141.4 1.2 select_reduce_fusion
  145.2 0.2 slice_reduce_fusion.2
  145.4 0.6 select_reduce_fusion.2
  146.7 0.7 and_convert_fusion
  147.4 1.3 select_reduce_fusion.5
  148.7 0.7 fusion.80
  149.4 2.8 select_convert_fusion.live_ref
  152.2 0.7 pad_maximum_fusion.4
  152.9 1.7 copy.42.q_ref
  154.6 92.1 %all-gather.6.cloned.1.call-done = bf16[64,112,768]{2,1,0:T(8,128)(2,1)} async-done(((bf16[2,112,768]{2,1,0:T(8,128)(2,1)}), bf16[64,112,768]{2,1,0:T(8,128)(2,1)}) %all-gather.6.cloned.1.call-update) | async-done | bytes 11010064 | tf_op jit(solution)/shard_map/all_gather | solution.py:600
  246.7 11.3 %shard_map.168 = bf16[96,768]{1,0:T(8,128)(2,1)} custom-call(bf16[96,768]{1,0:T(8,128)(2,1)} %copy.42.q_ref, bf16[32,2,112,768]{3,2,1,0:T(8,128)(2,1)} %bitcast.165, f32[1,3584]{1,0:T(1,128)} %select_convert_fusion.live_ref), custom_call_target="tpu_custom_call" | custom-call | tf_op jit(solution)/shard_map/pallas_call | solution.py:130
  258.1 1.8 fusion.96.part_ref
  259.9 17.2 %shard_map.169 = f32[24,3072]{1,0:T(8,128)S(1)} custom-call(f32[96,3072]{1,0:T(8,128)S(1)} %fusion.96.part_ref), custom_call_target="tpu_custom_call" | custom-call | tf_op jit(solution)/shard_map/pallas_call | solution.py:89
  277.1 1.0 fusion.34
  278.3 0.2 fusion.25
  278.5 0.8 fusion.28.block_ref
  279.3 66.1 %shard_map.170 = bf16[8,4,24,3072]{3,2,1,0:T(8,128)(2,1)} custom-call(bf16[24,3072]{1,0:T(8,128)(2,1)} %fusion.28.block_ref), custom_call_target="tpu_custom_call" | custom-call | tf_op jit(solution)/shard_map/pallas_call | solution.py:322
  345.5 10.4 %convolution_convert_fusion = bf16[768,3072]{1,0:T(8,128)(2,1)} fusion(bf16[384,3072]{1,0:T(8,128)(2,1)S(1)} %copy-done, bf16[768,3072]{1,0:T(8,128)(2,1)} %bitcast.174, bf16[3072,384]{1,0:T(8,128)(2,1)} %param.25), kind=kOutput, calls=%fused_computation | convolution fusion | flops 3628892160 | bytes 14155776 | tf_op jit(solution)/shard_map/dot_general | solution.py:625
  355.9 67.3 %shard_map.171 = f32[24,3072]{1,0:T(8,128)} custom-call(bf16[8,4,24,3072]{3,2,1,0:T(8,128)(2,1)} %bitcast.175), custom_call_target="tpu_custom_call" | custom-call | tf_op jit(solution)/shard_map/pallas_call | solution.py:231
  423.2 1.1 convert_reduce_fusion.2
  424.4 0.2 fusion.29
  424.6 0.9 multiply_convert_fusion.2
  425.8 0.9 copy.44
  426.6 9.8 %shard_map.172 = bf16[3,3,6,2,8,16]{5,4,3,2,1,0:T(8,128)(2,1)} custom-call(bf16[6,2,8,16]{3,2,1,0:T(8,128)(2,1)} %bitcast.186), custom_call_target="tpu_custom_call" | custom-call | tf_op jit(solution)/shard_map/pallas_call | solution.py:428
  436.5 0.9 slice_bitcast_fusion.6
  437.7 0.2 convolution_add_fusion.7
  438.1 0.2 convolution_add_fusion.5
  438.2 0.9 convolution_add_fusion.4
  439.1 0.2 convolution_add_fusion.3
  439.4 0.2 convolution_add_fusion.1
  439.6 0.8 fusion.13
  (82 shorter events, 2.1 us)
Async XLA Ops:
  7.2 338.3 %copy-start = (bf16[384,3072]{1,0:T(8,128)(2,1)S(1)}, bf16[384,3072]{1,0:T(8,128)(2,1)}, u32[]{:S(2)}) copy-start(bf16[384,3072]{1,0:T(8,128)(2,1)} %param.26) | copy-start | bytes 7077892
  7.2 6.1 %copy-start.4 = (bf16[1,4,3072]{2,1,0:T(4,128)(2,1)S(1)}, bf16[1,4,3072]{2,1,0:T(4,128)(2,1)}, u32[]{:S(2)}) copy-start(bf16[1,4,3072]{2,1,0:T(4,128)(2,1)} %param.16) | copy-start | bytes 73732
  7.2 5.0 %copy-start.1 = (bf16[1,96,3072]{2,1,0:T(8,128)(2,1)S(1)}, bf16[1,96,3072]{2,1,0:T(8,128)(2,1)}, u32[]{:S(2)}) copy-start(bf16[1,96,3072]{2,1,0:T(8,128)(2,1)} %param.15) | copy-start | bytes 1769476
  7.2 5.4 %copy-start.6 = (f32[1,8,3072]{2,1,0:T(8,128)S(1)}, f32[1,8,3072]{2,1,0:T(8,128)}, u32[]{:S(2)}) copy-start(f32[1,8,3072]{2,1,0:T(8,128)} %param.20) | copy-start | bytes 294916
  7.2 97.2 %all-gather.4.cloned.1.call-start = ((), (), s32[]{:S(2)}) async-start(), calls=%async_computation | async-start | bytes 7299072 | tf_op jit(solution)/shard_map/all_gather | solution.py:574
  9.1 237.7 %all-gather.6.cloned.1.call-start = ((), (), s32[]{:S(2)}) async-start(), calls=%async_computation.1 | async-start | bytes 11354112 | tf_op jit(solution)/shard_map/all_gather | solution.py:600
  13.4 0.6 copy-start.7
  113.4 5.5 %copy-start.14 = (f32[64]{0:T(128)S(1)}, f32[64]{0:T(128)}, u32[]{:S(2)}) copy-start(f32[64]{0:T(128)} %param.22) | copy-start | bytes 772
  117.1 1.9 copy-start.2
  137.6 7.6 %copy-start.13 = (s32[2,2]{1,0:T(2,128)S(1)}, s32[2,2]{1,0:T(2,128)}, u32[]{:S(2)}) copy-start(s32[2,2]{1,0:T(2,128)} %param.18) | copy-start | bytes 52
  152.2 105.9 %slice-start = ((s8[4718592]{0:T(1024)(128)(4,1)}), s8[524288]{0:T(1024)(128)(4,1)S(1)}, s32[]{:S(2)}) async-start(s8[4718592]{0:T(1024)(128)(4,1)} %bitcast.172), calls=%async_computation.2 | async-start | bytes 1048576
  246.7 11.4 %slice-start.1 = ((s8[4718592]{0:T(1024)(128)(4,1)}), s8[4194304]{0:T(1024)(128)(4,1)S(1)}, s32[]{:S(2)}) async-start(s8[4718592]{0:T(1024)(128)(4,1)} %bitcast.172), calls=%async_computation.3 | async-start | bytes 8388608
  259.9 17.2 %copy-start.10 = (f32[1,1,3072]{2,1,0:T(1,128)S(1)}, f32[1,1,3072]{2,1,0:T(1,128)}, u32[]{:S(2)}) copy-start(f32[1,1,3072]{2,1,0:T(1,128)} %get-tuple-element.34) | copy-start | bytes 36868
  259.9 18.6 %copy-start.8 = (f32[1,1,3072]{2,1,0:T(1,128)S(1)}, f32[1,1,3072]{2,1,0:T(1,128)}, u32[]{:S(2)}) copy-start(f32[1,1,3072]{2,1,0:T(1,128)} %get-tuple-element.30) | copy-start | bytes 36868
  355.8 67.3 %copy-start.9 = (f32[1,1,3072]{2,1,0:T(1,128)S(1)}, f32[1,1,3072]{2,1,0:T(1,128)}, u32[]{:S(2)}) copy-start(f32[1,1,3072]{2,1,0:T(1,128)} %get-tuple-element.31) | copy-start | bytes 36868
  355.9 68.7 %copy-start.11 = (f32[1,1,3072]{2,1,0:T(1,128)S(1)}, f32[1,1,3072]{2,1,0:T(1,128)}, u32[]{:S(2)}) copy-start(f32[1,1,3072]{2,1,0:T(1,128)} %get-tuple-element.28) | copy-start | bytes 36868
  355.9 68.7 %copy-start.12 = (f32[1,1,3072]{2,1,0:T(1,128)S(1)}, f32[1,1,3072]{2,1,0:T(1,128)}, u32[]{:S(2)}) copy-start(f32[1,1,3072]{2,1,0:T(1,128)} %get-tuple-element.35) | copy-start | bytes 36868
  355.9 68.7 %copy-start.15 = (bf16[3072,64]{0,1:T(8,128)(2,1)S(1)}, bf16[3072,64]{0,1:T(8,128)(2,1)}, u32[]{:S(2)}) copy-start(bf16[3072,64]{0,1:T(8,128)(2,1)} %param.27) | copy-start | bytes 1179652
  355.9 68.7 %copy-start.16 = (f32[1,24,64]{2,1,0:T(8,128)S(1)}, f32[1,24,64]{2,1,0:T(8,128)}, u32[]{:S(2)}) copy-start(f32[1,24,64]{2,1,0:T(8,128)} %param.28) | copy-start | bytes 18436
  424.3 13.4 %copy-start.3 = (bf16[24,3072]{1,0:T(8,128)(2,1)}, bf16[24,3072]{1,0:T(8,128)(2,1)S(1)}, u32[]{:S(2)}) copy-start(bf16[24,3072]{1,0:T(8,128)(2,1)S(1)} %get-tuple-element.8) | copy-start | bytes 442372
  424.3 13.2 %copy-start.5 = (bf16[3,3,16,512]{3,2,1,0:T(8,128)(2,1)S(1)}, bf16[3,3,16,512]{3,2,1,0:T(8,128)(2,1)}, u32[]{:S(2)}) copy-start(bf16[3,3,16,512]{3,2,1,0:T(8,128)(2,1)} %param.29) | copy-start | bytes 442372
Sparse Core Ops, SparseCore 0:
  10.6 93.7 all-gather.3
  137.8 108.8 all-gather.5

commit v10 on v9

--- a/solution.py
+++ b/solution.py
@@ -608,7 +608,7 @@
         head_dim ** (-0.5),
     )
     partial_out = jnp.dot(attended, w_out, preferred_element_type=jnp.float32)
-    projected = scatter_sum(partial_out, "col", 1)
+    projected = scatter_sum(partial_out.astype(jnp.bfloat16), "col", 1)
     own_rows = lax.dynamic_slice_in_dim(source, col_id * tile, tile, 0)
     mixed = lax.optimization_barrier(
         (own_rows + adaptive[2] * projected).astype(jnp.bfloat16)

time: 450 us -> 442 us (0.982)
  Pallas kernels: 179 us -> 172 us
    pallas_call x1, Pallas kernels: 17.2 us -> 11 us  [scatter_sum(): pl.pallas_call(functools.partial(scatter_sum_kernel, axis, count, rows),...]
where the time goes in v10:
time: 442 us; the launch traced here: 440 us
  waiting for transfers between devices  178 us (40%)
  Pallas kernels  172 us (39%)
  other arithmetic  26.3 us (6%)
  local copies, waits for them, and re-layouts  24 us (5%)
  matrix products  21.6 us (5%)
  between operations  18.5 us (4%)
    all_gather x1, waiting for transfers between devices, shards(): gathered = lax.all_gather(both, 'row', axis=0, tiled=True)  92.1 us
    all_gather x1, waiting for transfers between devices, shards(): gathered_half = lax.all_gather(own_half, 'row', axis=1, tiled=True)  85.4 us
    pallas_call x1, Pallas kernels, ring_gather(): pl.pallas_call(functools.partial(ring_gather_kernel, zs, xs), out_shape=j...  66.5 us
    pallas_call x1, Pallas kernels, ring_scatter_sum(): pl.pallas_call(functools.partial(ring_scatter_kernel, zs, xs), out_shape=...  65.5 us
    pallas_call x1, Pallas kernels, attention(): pl.pallas_call(functools.partial(attention_kernel, scale), out_shape=jax....  11.3 us
    pallas_call x1, Pallas kernels, scatter_sum(): pl.pallas_call(functools.partial(scatter_sum_kernel, axis, count, rows),...  11 us
    pallas_call x1, Pallas kernels, halo_extend(): pl.pallas_call(halo_kernel, out_shape=jax.ShapeDtypeStruct((3, 3) + tile....  10.5 us
    dot_general x1, matrix products, shards(): jnp.dot(hidden_units, w_down, preferred_element_type=jnp.float32)  10.4 us
  transfers between devices with their start and end apart: 2, of which 2 were waited for; matrix products, arithmetic and copies ran while one was open for 4% of the time, Pallas kernels for 1%

profile of v10, /device:TPU:2, one launch (start us, length us, event | category | flops | bytes accessed | tf_op | source)
XLA Modules:
  0.0 440.2 jit_solution(13154797528514807563)
XLA Ops:
  7.3 1.8 constant_dynamic-slice_fusion
  9.1 0.9 convert_reduce_fusion.3
  10.0 0.9 fusion.43
  11.0 1.2 convert_reduce_fusion
  12.2 0.3 multiply_reduce_fusion
  12.6 0.7 slice_add_fusion
  13.4 0.3 add_convert_fusion
  13.7 0.3 copy-done.7
  14.0 0.9 pad_maximum_fusion.src_ref
  14.8 4.1 shard_map.166
  19.0 85.4 %all-gather.4.cloned.1.call-done = bf16[3,3072,384]{2,1,0:T(8,128)(2,1)} async-done(((bf16[3,96,384]{2,1,0:T(8,128)(2,1)}), bf16[3,3072,384]{2,1,0:T(8,128)(2,1)}) %all-gather.4.cloned.1.call-update) | async-done | bytes 7077904 | tf_op jit(solution)/shard_map/all_gather | solution.py:574
  104.4 5.8 %fusion.93 = (bf16[3,200,384]{2,1,0:T(8,128)(2,1)S(1)}, f32[3,200,384]{2,1,0:T(8,128)}) fusion(bf16[3,3072,384]{2,1,0:T(8,128)(2,1)} %all-gather.4.cloned.1.call-done, bf16[100,3072]{1,0:T(8,128)(2,1)} %shard_map.166, bf16[4,3072]{1,0:T(4,128)(2,1)} %copy-done.7, bf16[96,3072]{1,0:T(8,128)(2,1)S(1)} %add_convert_fusion), kind=kOutput, calls=%fused_computation.192 | convolution fusion | flops 1419494400 | bytes 9689088 | tf_op jit(solution)/shard_map/ld,cde->cle/dot_general | solution.py:578
  110.3 1.9 fusion.91
  112.3 1.1 copy.33
  113.6 1.9 copy.32
  115.4 1.6 reduce_sum.184
  117.1 0.7 broadcast_multiply_fusion.1
  117.8 1.1 multiply_reduce_fusion.2
  119.0 0.8 multiply_convert_fusion.1
  119.8 0.8 slice_bitcast_fusion.2
  120.6 1.2 copy.54
  121.8 2.1 reshape.431.src_ref
  123.9 3.2 shard_map.167
  127.1 2.1 reshape.432
  129.2 2.1 copy.39
  131.3 0.7 copy.34
  132.0 1.2 broadcast_select_fusion.1
  133.2 0.8 pad_maximum_fusion.1
  134.0 1.9 copy.58
  135.9 1.7 pad.7.clone
  137.7 1.1 convert_element_type.77
  138.9 0.3 reduce-window.9
  139.3 1.3 select_reduce_fusion.4
  141.4 1.2 select_reduce_fusion
  145.2 0.2 slice_reduce_fusion.2
  145.4 0.6 select_reduce_fusion.2
  146.7 0.7 and_convert_fusion
  147.4 1.3 select_reduce_fusion.5
  148.7 0.7 fusion.80
  149.4 2.8 select_convert_fusion.live_ref
  152.2 0.7 pad_maximum_fusion.4
  152.9 1.7 copy.42.q_ref
  154.6 92.1 %all-gather.6.cloned.1.call-done = bf16[64,112,768]{2,1,0:T(8,128)(2,1)} async-done(((bf16[2,112,768]{2,1,0:T(8,128)(2,1)}), bf16[64,112,768]{2,1,0:T(8,128)(2,1)}) %all-gather.6.cloned.1.call-update) | async-done | bytes 11010064 | tf_op jit(solution)/shard_map/all_gather | solution.py:600
  246.7 11.3 %shard_map.168 = bf16[96,768]{1,0:T(8,128)(2,1)} custom-call(bf16[96,768]{1,0:T(8,128)(2,1)} %copy.42.q_ref, bf16[32,2,112,768]{3,2,1,0:T(8,128)(2,1)} %bitcast.165, f32[1,3584]{1,0:T(1,128)} %select_convert_fusion.live_ref), custom_call_target="tpu_custom_call" | custom-call | tf_op jit(solution)/shard_map/pallas_call | solution.py:130
  258.1 1.8 convolution_convert_fusion.1.part_ref
  259.9 11.0 %shard_map.169 = f32[24,3072]{1,0:T(8,128)S(1)} custom-call(bf16[96,3072]{1,0:T(8,128)(2,1)S(1)} %convolution_convert_fusion.1.part_ref), custom_call_target="tpu_custom_call" | custom-call | tf_op jit(solution)/shard_map/pallas_call | solution.py:89
  270.9 1.0 fusion.34
  272.1 0.2 fusion.25
  272.3 0.8 fusion.28.block_ref
  273.1 66.5 %shard_map.170 = bf16[8,4,24,3072]{3,2,1,0:T(8,128)(2,1)} custom-call(bf16[24,3072]{1,0:T(8,128)(2,1)} %fusion.28.block_ref), custom_call_target="tpu_custom_call" | custom-call | tf_op jit(solution)/shard_map/pallas_call | solution.py:322
  339.7 10.4 %convolution_convert_fusion = bf16[768,3072]{1,0:T(8,128)(2,1)} fusion(bf16[384,3072]{1,0:T(8,128)(2,1)S(1)} %copy-done, bf16[768,3072]{1,0:T(8,128)(2,1)} %bitcast.172, bf16[3072,384]{1,0:T(8,128)(2,1)} %param.25), kind=kOutput, calls=%fused_computation | convolution fusion | flops 3628892160 | bytes 14155776 | tf_op jit(solution)/shard_map/dot_general | solution.py:625
  350.1 65.5 %shard_map.171 = f32[24,3072]{1,0:T(8,128)} custom-call(bf16[8,4,24,3072]{3,2,1,0:T(8,128)(2,1)} %bitcast.173), custom_call_target="tpu_custom_call" | custom-call | tf_op jit(solution)/shard_map/pallas_call | solution.py:231
  415.6 1.1 convert_reduce_fusion.2
  416.7 0.2 fusion.29
  417.0 0.9 multiply_convert_fusion.2
  418.1 0.9 copy.44
  419.0 10.5 %shard_map.172 = bf16[3,3,6,2,8,16]{5,4,3,2,1,0:T(8,128)(2,1)} custom-call(bf16[6,2,8,16]{3,2,1,0:T(8,128)(2,1)} %bitcast.186), custom_call_target="tpu_custom_call" | custom-call | tf_op jit(solution)/shard_map/pallas_call | solution.py:428
  429.5 0.9 slice_bitcast_fusion.6
  430.9 0.2 convolution_add_fusion.6
  431.1 0.2 convolution_add_fusion.5
  431.2 0.9 convolution_add_fusion.4
  432.1 0.2 convolution_add_fusion.3
  432.4 0.2 convolution_add_fusion.1
  432.6 0.8 fusion.13
  (82 shorter events, 2.1 us)
Async XLA Ops:
  7.2 332.5 %copy-start = (bf16[384,3072]{1,0:T(8,128)(2,1)S(1)}, bf16[384,3072]{1,0:T(8,128)(2,1)}, u32[]{:S(2)}) copy-start(bf16[384,3072]{1,0:T(8,128)(2,1)} %param.26) | copy-start | bytes 7077892
  7.2 6.1 %copy-start.4 = (bf16[1,4,3072]{2,1,0:T(4,128)(2,1)S(1)}, bf16[1,4,3072]{2,1,0:T(4,128)(2,1)}, u32[]{:S(2)}) copy-start(bf16[1,4,3072]{2,1,0:T(4,128)(2,1)} %param.16) | copy-start | bytes 73732
  7.2 5.0 %copy-start.1 = (bf16[1,96,3072]{2,1,0:T(8,128)(2,1)S(1)}, bf16[1,96,3072]{2,1,0:T(8,128)(2,1)}, u32[]{:S(2)}) copy-start(bf16[1,96,3072]{2,1,0:T(8,128)(2,1)} %param.15) | copy-start | bytes 1769476
  7.2 5.4 %copy-start.6 = (f32[1,8,3072]{2,1,0:T(8,128)S(1)}, f32[1,8,3072]{2,1,0:T(8,128)}, u32[]{:S(2)}) copy-start(f32[1,8,3072]{2,1,0:T(8,128)} %param.20) | copy-start | bytes 294916
  7.2 97.2 %all-gather.4.cloned.1.call-start = ((), (), s32[]{:S(2)}) async-start(), calls=%async_computation | async-start | bytes 7299072 | tf_op jit(solution)/shard_map/all_gather | solution.py:574
  9.1 237.7 %all-gather.6.cloned.1.call-start = ((), (), s32[]{:S(2)}) async-start(), calls=%async_computation.1 | async-start | bytes 11354112 | tf_op jit(solution)/shard_map/all_gather | solution.py:600
  13.4 0.6 copy-start.7
  113.4 5.5 %copy-start.14 = (f32[64]{0:T(128)S(1)}, f32[64]{0:T(128)}, u32[]{:S(2)}) copy-start(f32[64]{0:T(128)} %param.22) | copy-start | bytes 772
  117.1 1.9 copy-start.2
  137.6 7.6 %copy-start.13 = (s32[2,2]{1,0:T(2,128)S(1)}, s32[2,2]{1,0:T(2,128)}, u32[]{:S(2)}) copy-start(s32[2,2]{1,0:T(2,128)} %param.18) | copy-start | bytes 52
  152.2 105.9 %slice-start = ((s8[4718592]{0:T(1024)(128)(4,1)}), s8[524288]{0:T(1024)(128)(4,1)S(1)}, s32[]{:S(2)}) async-start(s8[4718592]{0:T(1024)(128)(4,1)} %bitcast.174), calls=%async_computation.2 | async-start | bytes 1048576
  246.7 11.4 %slice-start.1 = ((s8[4718592]{0:T(1024)(128)(4,1)}), s8[4194304]{0:T(1024)(128)(4,1)S(1)}, s32[]{:S(2)}) async-start(s8[4718592]{0:T(1024)(128)(4,1)} %bitcast.174), calls=%async_computation.3 | async-start | bytes 8388608
  258.1 12.8 %copy-start.10 = (f32[1,1,3072]{2,1,0:T(1,128)S(1)}, f32[1,1,3072]{2,1,0:T(1,128)}, u32[]{:S(2)}) copy-start(f32[1,1,3072]{2,1,0:T(1,128)} %get-tuple-element.34) | copy-start | bytes 36868
  259.9 12.4 %copy-start.8 = (f32[1,1,3072]{2,1,0:T(1,128)S(1)}, f32[1,1,3072]{2,1,0:T(1,128)}, u32[]{:S(2)}) copy-start(f32[1,1,3072]{2,1,0:T(1,128)} %get-tuple-element.30) | copy-start | bytes 36868
  350.0 65.5 %copy-start.9 = (f32[1,1,3072]{2,1,0:T(1,128)S(1)}, f32[1,1,3072]{2,1,0:T(1,128)}, u32[]{:S(2)}) copy-start(f32[1,1,3072]{2,1,0:T(1,128)} %get-tuple-element.31) | copy-start | bytes 36868
  350.0 66.9 %copy-start.11 = (f32[1,1,3072]{2,1,0:T(1,128)S(1)}, f32[1,1,3072]{2,1,0:T(1,128)}, u32[]{:S(2)}) copy-start(f32[1,1,3072]{2,1,0:T(1,128)} %get-tuple-element.28) | copy-start | bytes 36868
  350.0 66.9 %copy-start.12 = (f32[1,1,3072]{2,1,0:T(1,128)S(1)}, f32[1,1,3072]{2,1,0:T(1,128)}, u32[]{:S(2)}) copy-start(f32[1,1,3072]{2,1,0:T(1,128)} %get-tuple-element.35) | copy-start | bytes 36868
  350.0 66.9 %copy-start.15 = (bf16[3072,64]{0,1:T(8,128)(2,1)S(1)}, bf16[3072,64]{0,1:T(8,128)(2,1)}, u32[]{:S(2)}) copy-start(bf16[3072,64]{0,1:T(8,128)(2,1)} %param.27) | copy-start | bytes 1179652
  350.1 66.9 %copy-start.16 = (f32[1,24,64]{2,1,0:T(8,128)S(1)}, f32[1,24,64]{2,1,0:T(8,128)}, u32[]{:S(2)}) copy-start(f32[1,24,64]{2,1,0:T(8,128)} %param.28) | copy-start | bytes 18436
  416.7 14.1 %copy-start.3 = (bf16[24,3072]{1,0:T(8,128)(2,1)}, bf16[24,3072]{1,0:T(8,128)(2,1)S(1)}, u32[]{:S(2)}) copy-start(bf16[24,3072]{1,0:T(8,128)(2,1)S(1)} %get-tuple-element.8) | copy-start | bytes 442372
  416.7 13.9 %copy-start.5 = (bf16[3,3,16,512]{3,2,1,0:T(8,128)(2,1)S(1)}, bf16[3,3,16,512]{3,2,1,0:T(8,128)(2,1)}, u32[]{:S(2)}) copy-start(bf16[3,3,16,512]{3,2,1,0:T(8,128)(2,1)} %param.29) | copy-start | bytes 442372
Sparse Core Ops, SparseCore 0:
  10.6 93.7 all-gather.3
  137.8 108.8 all-gather.5

commit v11 on v10

--- a/solution.py
+++ b/solution.py
@@ -575,18 +575,13 @@
     half_heads = half_cols // head_dim
 
     both_rows = jnp.concatenate([joined, partner_swap(joined, 4)], axis=0)
-    projected_rows = jnp.einsum(
-        "ld,cde->cle", both_rows, gathered_half, preferred_element_type=jnp.float32
-    ).reshape(3, 2 * span, half_heads, head_dim)
-    normed_q = head_norm(projected_rows[0], q_gain)
-    normed_k = head_norm(projected_rows[1], k_gain)
-    plain_v = projected_rows[2].astype(jnp.bfloat16)
-    mine = jnp.stack([normed_q[:span], normed_k[:span], plain_v[:span]])
-    theirs = jnp.stack([normed_q[span:], normed_k[span:], plain_v[span:]])
-    received = partner_swap(theirs.reshape(3 * span, half_cols), 5).reshape(theirs.shape)
-    full = jnp.concatenate(
-        [jnp.where(request_id == 0, mine, received), jnp.where(request_id == 0, received, mine)], axis=2
-    )
+    projected_rows = jnp.einsum("ld,cde->cle", both_rows, gathered_half, preferred_element_type=jnp.float32)
+    own_raw = projected_rows[:, :span]
+    received_raw = partner_swap(projected_rows[:, span:], 5)
+    raw = jnp.concatenate(
+        [jnp.where(request_id == 0, own_raw, received_raw), jnp.where(request_id == 0, received_raw, own_raw)], axis=2
+    ).reshape(3, span, 2 * half_heads, head_dim)
+    full = jnp.stack([head_norm(raw[0], q_gain), head_norm(raw[1], k_gain), raw[2].astype(jnp.bfloat16)])
     groups = 1
     heads_here = full.shape[2]
     queries = full[0, :block_tokens][None]

time: 442 us -> 430 us (0.973)
  local copies, waits for them, and re-layouts: 24 us -> 15.2 us
    reshape x4 -> x0, local copies, waits for them, and re-layouts: 7.49 us -> none  [the longest x2 4.18 us: shards(): partner_swap(theirs.reshape(3 * span, half_cols), 5).reshape(theirs.shape)]
where the time goes in v11:
time: 430 us; the launch traced here: 429 us
  waiting for transfers between devices  179 us (42%)
  Pallas kernels  174 us (40%)
  other arithmetic  22.1 us (5%)
  matrix products  20.7 us (5%)
  between operations  18.6 us (4%)
  local copies, waits for them, and re-layouts  15.2 us (4%)
    all_gather x1, waiting for transfers between devices, shards(): gathered = lax.all_gather(both, 'row', axis=0, tiled=True)  94.7 us
    all_gather x1, waiting for transfers between devices, shards(): gathered_half = lax.all_gather(own_half, 'row', axis=1, tiled=True)  84.1 us
    pallas_call x1, Pallas kernels, ring_gather(): pl.pallas_call(functools.partial(ring_gather_kernel, zs, xs), out_shape=j...  66.6 us
    pallas_call x1, Pallas kernels, ring_scatter_sum(): pl.pallas_call(functools.partial(ring_scatter_kernel, zs, xs), out_shape=...  65.4 us
    pallas_call x1, Pallas kernels, halo_extend(): pl.pallas_call(halo_kernel, out_shape=jax.ShapeDtypeStruct((3, 3) + tile....  12.2 us
    pallas_call x1, Pallas kernels, attention(): pl.pallas_call(functools.partial(attention_kernel, scale), out_shape=jax....  11.2 us
    pallas_call x1, Pallas kernels, scatter_sum(): pl.pallas_call(functools.partial(scatter_sum_kernel, axis, count, rows),...  11 us
    dot_general x1, matrix products, shards(): jnp.dot(hidden_units, w_down, preferred_element_type=jnp.float32)  10.4 us
  transfers between devices with their start and end apart: 2, of which 2 were waited for; matrix products, arithmetic and copies ran while one was open for 4% of the time, Pallas kernels for 1%

profile of v11, /device:TPU:2, one launch (start us, length us, event | category | flops | bytes accessed | tf_op | source)
XLA Modules:
  0.0 429.4 jit_solution(17620926763521283594)
XLA Ops:
  7.3 1.8 constant_dynamic-slice_fusion
  9.2 0.9 convert_reduce_fusion.3
  10.1 0.9 fusion.52
  11.0 1.2 convert_reduce_fusion
  12.3 0.3 multiply_reduce_fusion
  12.6 0.7 slice_add_fusion
  13.4 0.3 add_convert_fusion
  13.7 0.3 copy-done.9
  14.0 0.9 pad_maximum_fusion.src_ref
  14.9 4.0 shard_map.166
  19.0 0.6 mul.308
  19.6 0.8 mul.309
  20.3 84.1 %all-gather.4.cloned.1.call-done = bf16[3,3072,384]{2,1,0:T(8,128)(2,1)} async-done(((bf16[3,96,384]{2,1,0:T(8,128)(2,1)}), bf16[3,3072,384]{2,1,0:T(8,128)(2,1)}) %all-gather.4.cloned.1.call-update) | async-done | bytes 7077904 | tf_op jit(solution)/shard_map/all_gather | solution.py:574
  104.4 4.8 %convolution_bitcast_fusion = f32[3,200,384]{2,1,0:T(8,128)S(1)} fusion(bf16[3,3072,384]{2,1,0:T(8,128)(2,1)} %all-gather.4.cloned.1.call-done, bf16[100,3072]{1,0:T(8,128)(2,1)} %shard_map.166, bf16[4,3072]{1,0:T(4,128)(2,1)} %copy-done.9, bf16[96,3072]{1,0:T(8,128)(2,1)S(1)} %add_convert_fusion), kind=kOutput, calls=%fused_computation.3 | convolution fusion | flops 1419264000 | bytes 9228288 | tf_op jit(solution)/shard_map/ld,cde->cle/dot_general | solution.py:578
  109.3 0.9 copy-done.4
  110.2 0.8 slice.238.src_ref
  111.0 3.7 shard_map.167
  114.7 1.2 slice_select_fusion
  116.0 0.9 fusion.31
  116.9 1.1 copy.29
  118.2 0.8 mul.305
  118.9 1.9 copy.31
  120.8 0.8 sub.126
  121.6 1.9 copy.30
  123.5 1.1 multiply_convert_fusion
  124.6 0.8 fusion.30
  125.4 1.1 convert_element_type.87
  126.7 0.3 reduce-window.9
  127.0 0.6 select_reduce_fusion.4
  128.5 1.3 select_reduce_fusion
  132.4 0.2 slice_reduce_fusion.2
  132.6 0.6 select_reduce_fusion.2
  133.9 0.7 and_convert_fusion
  134.6 0.6 select_reduce_fusion.5
  135.2 0.6 fusion.89
  135.8 2.7 select_convert_fusion.live_ref
  138.5 0.2 copy.27
  139.0 0.8 copy.32.q_ref
  139.8 94.7 %all-gather.6.cloned.1.call-done = bf16[64,112,768]{2,1,0:T(8,128)(2,1)} async-done(((bf16[2,112,768]{2,1,0:T(8,128)(2,1)}), bf16[64,112,768]{2,1,0:T(8,128)(2,1)}) %all-gather.6.cloned.1.call-update) | async-done | bytes 11010064 | tf_op jit(solution)/shard_map/all_gather | solution.py:595
  234.5 11.2 %shard_map.168 = bf16[96,768]{1,0:T(8,128)(2,1)} custom-call(bf16[96,768]{1,0:T(8,128)(2,1)} %copy.32.q_ref, bf16[32,2,112,768]{3,2,1,0:T(8,128)(2,1)} %bitcast.157, f32[1,3584]{1,0:T(1,128)} %select_convert_fusion.live_ref), custom_call_target="tpu_custom_call" | custom-call | tf_op jit(solution)/shard_map/pallas_call | solution.py:130
  245.7 1.8 convolution_convert_fusion.1.part_ref
  247.5 11.0 %shard_map.169 = f32[24,3072]{1,0:T(8,128)S(1)} custom-call(bf16[96,3072]{1,0:T(8,128)(2,1)S(1)} %convolution_convert_fusion.1.part_ref), custom_call_target="tpu_custom_call" | custom-call | tf_op jit(solution)/shard_map/pallas_call | solution.py:89
  258.5 1.0 fusion.43
  259.5 0.1 convert_reduce_fusion.1
  259.6 0.2 fusion.34
  259.9 0.8 fusion.37.block_ref
  260.7 66.6 %shard_map.170 = bf16[8,4,24,3072]{3,2,1,0:T(8,128)(2,1)} custom-call(bf16[24,3072]{1,0:T(8,128)(2,1)} %fusion.37.block_ref), custom_call_target="tpu_custom_call" | custom-call | tf_op jit(solution)/shard_map/pallas_call | solution.py:322
  327.3 10.4 %convolution_convert_fusion = bf16[768,3072]{1,0:T(8,128)(2,1)} fusion(bf16[384,3072]{1,0:T(8,128)(2,1)S(1)} %copy-done, bf16[768,3072]{1,0:T(8,128)(2,1)} %bitcast.161, bf16[3072,384]{1,0:T(8,128)(2,1)} %param.25), kind=kOutput, calls=%fused_computation | convolution fusion | flops 3628892160 | bytes 14155776 | tf_op jit(solution)/shard_map/dot_general | solution.py:620
  337.7 65.4 %shard_map.171 = f32[24,3072]{1,0:T(8,128)} custom-call(bf16[8,4,24,3072]{3,2,1,0:T(8,128)(2,1)} %bitcast.162), custom_call_target="tpu_custom_call" | custom-call | tf_op jit(solution)/shard_map/pallas_call | solution.py:231
  403.1 1.1 convert_reduce_fusion.2
  404.2 0.2 fusion.38
  404.5 0.9 multiply_convert_fusion.1
  405.6 0.9 copy.34
  406.5 12.2 %shard_map.172 = bf16[3,3,6,2,8,16]{5,4,3,2,1,0:T(8,128)(2,1)} custom-call(bf16[6,2,8,16]{3,2,1,0:T(8,128)(2,1)} %bitcast.176), custom_call_target="tpu_custom_call" | custom-call | tf_op jit(solution)/shard_map/pallas_call | solution.py:428
  418.7 0.9 slice_bitcast_fusion.2
  419.8 0.1 fusion.63
  419.9 0.2 convolution_add_fusion.7
  420.1 0.2 convolution_add_fusion.6
  420.3 0.2 convolution_add_fusion.5
  420.4 0.9 convolution_add_fusion.4
  421.3 0.2 convolution_add_fusion.3
  421.5 0.1 convolution_add_fusion.2
  421.6 0.2 convolution_add_fusion.1
  421.8 0.8 fusion.13
  (88 shorter events, 1.5 us)
Async XLA Ops:
  7.2 320.1 %copy-start = (bf16[384,3072]{1,0:T(8,128)(2,1)S(1)}, bf16[384,3072]{1,0:T(8,128)(2,1)}, u32[]{:S(2)}) copy-start(bf16[384,3072]{1,0:T(8,128)(2,1)} %param.26) | copy-start | bytes 7077892
  7.2 6.1 %copy-start.6 = (bf16[1,4,3072]{2,1,0:T(4,128)(2,1)S(1)}, bf16[1,4,3072]{2,1,0:T(4,128)(2,1)}, u32[]{:S(2)}) copy-start(bf16[1,4,3072]{2,1,0:T(4,128)(2,1)} %param.16) | copy-start | bytes 73732
  7.2 5.1 %copy-start.1 = (bf16[1,96,3072]{2,1,0:T(8,128)(2,1)S(1)}, bf16[1,96,3072]{2,1,0:T(8,128)(2,1)}, u32[]{:S(2)}) copy-start(bf16[1,96,3072]{2,1,0:T(8,128)(2,1)} %param.15) | copy-start | bytes 1769476
  7.2 5.4 %copy-start.8 = (f32[1,8,3072]{2,1,0:T(8,128)S(1)}, f32[1,8,3072]{2,1,0:T(8,128)}, u32[]{:S(2)}) copy-start(f32[1,8,3072]{2,1,0:T(8,128)} %param.20) | copy-start | bytes 294916
  7.2 97.2 %all-gather.4.cloned.1.call-start = ((), (), s32[]{:S(2)}) async-start(), calls=%async_computation | async-start | bytes 7299072 | tf_op jit(solution)/shard_map/all_gather | solution.py:574
  9.1 225.4 %all-gather.6.cloned.1.call-start = ((), (), s32[]{:S(2)}) async-start(), calls=%async_computation.1 | async-start | bytes 11354112 | tf_op jit(solution)/shard_map/all_gather | solution.py:595
  13.4 0.6 copy-start.9
  14.0 4.9 %copy-start.16 = (f32[64]{0:T(128)S(1)}, f32[64]{0:T(128)}, u32[]{:S(2)}) copy-start(f32[64]{0:T(128)} %param.22) | copy-start | bytes 772
  109.3 0.9 copy-start.4
  118.1 5.4 %copy-start.2 = (f32[1,100,768]{2,1,0:T(8,128)S(1)}, f32[1,100,768]{2,1,0:T(8,128)}, u32[]{:S(2)}) copy-start(f32[1,100,768]{2,1,0:T(8,128)} %get-tuple-element.11) | copy-start | bytes 921604
  125.4 1.6 copy-start.20
  125.4 7.0 %copy-start.15 = (s32[2,2]{1,0:T(2,128)S(1)}, s32[2,2]{1,0:T(2,128)}, u32[]{:S(2)}) copy-start(s32[2,2]{1,0:T(2,128)} %param.18) | copy-start | bytes 52
  125.4 9.1 %copy-start.21 = (s32[2]{0:T(128)S(1)}, s32[2]{0:T(128)}, u32[]{:S(2)}) copy-start(s32[2]{0:T(128)} %param.17) | copy-start | bytes 28
  125.4 13.1 %copy-start.3 = (f32[1,100,768]{2,1,0:T(8,128)S(1)}, f32[1,100,768]{2,1,0:T(8,128)}, u32[]{:S(2)}) copy-start(f32[1,100,768]{2,1,0:T(8,128)} %get-tuple-element.12) | copy-start | bytes 921604
  126.6 12.3 %copy-start.17 = (f32[64]{0:T(128)S(1)}, f32[64]{0:T(128)}, u32[]{:S(2)}) copy-start(f32[64]{0:T(128)} %param.21) | copy-start | bytes 772
  138.9 106.8 %slice-start = ((s8[4718592]{0:T(1024)(128)(4,1)}), s8[524288]{0:T(1024)(128)(4,1)S(1)}, s32[]{:S(2)}) async-start(s8[4718592]{0:T(1024)(128)(4,1)} %bitcast.163), calls=%async_computation.2 | async-start | bytes 1048576
  234.5 11.2 %slice-start.1 = ((s8[4718592]{0:T(1024)(128)(4,1)}), s8[4194304]{0:T(1024)(128)(4,1)S(1)}, s32[]{:S(2)}) async-start(s8[4718592]{0:T(1024)(128)(4,1)} %bitcast.163), calls=%async_computation.3 | async-start | bytes 8388608
  245.7 12.8 %copy-start.12 = (f32[1,1,3072]{2,1,0:T(1,128)S(1)}, f32[1,1,3072]{2,1,0:T(1,128)}, u32[]{:S(2)}) copy-start(f32[1,1,3072]{2,1,0:T(1,128)} %get-tuple-element.28) | copy-start | bytes 36868
  247.5 12.4 %copy-start.10 = (f32[1,1,3072]{2,1,0:T(1,128)S(1)}, f32[1,1,3072]{2,1,0:T(1,128)}, u32[]{:S(2)}) copy-start(f32[1,1,3072]{2,1,0:T(1,128)} %get-tuple-element.24) | copy-start | bytes 36868
  337.7 65.4 %copy-start.11 = (f32[1,1,3072]{2,1,0:T(1,128)S(1)}, f32[1,1,3072]{2,1,0:T(1,128)}, u32[]{:S(2)}) copy-start(f32[1,1,3072]{2,1,0:T(1,128)} %get-tuple-element.25) | copy-start | bytes 36868
  337.7 66.8 %copy-start.13 = (f32[1,1,3072]{2,1,0:T(1,128)S(1)}, f32[1,1,3072]{2,1,0:T(1,128)}, u32[]{:S(2)}) copy-start(f32[1,1,3072]{2,1,0:T(1,128)} %get-tuple-element.22) | copy-start | bytes 36868
  337.7 66.8 %copy-start.14 = (f32[1,1,3072]{2,1,0:T(1,128)S(1)}, f32[1,1,3072]{2,1,0:T(1,128)}, u32[]{:S(2)}) copy-start(f32[1,1,3072]{2,1,0:T(1,128)} %get-tuple-element.29) | copy-start | bytes 36868
  337.7 66.8 %copy-start.18 = (bf16[3072,64]{0,1:T(8,128)(2,1)S(1)}, bf16[3072,64]{0,1:T(8,128)(2,1)}, u32[]{:S(2)}) copy-start(bf16[3072,64]{0,1:T(8,128)(2,1)} %param.27) | copy-start | bytes 1179652
  337.7 66.8 %copy-start.19 = (f32[1,24,64]{2,1,0:T(8,128)S(1)}, f32[1,24,64]{2,1,0:T(8,128)}, u32[]{:S(2)}) copy-start(f32[1,24,64]{2,1,0:T(8,128)} %param.28) | copy-start | bytes 18436
  404.2 15.8 %copy-start.5 = (bf16[24,3072]{1,0:T(8,128)(2,1)}, bf16[24,3072]{1,0:T(8,128)(2,1)S(1)}, u32[]{:S(2)}) copy-start(bf16[24,3072]{1,0:T(8,128)(2,1)S(1)} %get-tuple-element.8) | copy-start | bytes 442372
  404.2 15.6 %copy-start.7 = (bf16[3,3,16,512]{3,2,1,0:T(8,128)(2,1)S(1)}, bf16[3,3,16,512]{3,2,1,0:T(8,128)(2,1)}, u32[]{:S(2)}) copy-start(bf16[3,3,16,512]{3,2,1,0:T(8,128)(2,1)} %param.29) | copy-start | bytes 442372
Sparse Core Ops, SparseCore 0:
  10.6 93.7 all-gather.3
  125.6 108.8 all-gather.5

commit v12 on v11

--- a/solution.py
+++ b/solution.py
@@ -448,6 +448,44 @@
     return jnp.concatenate(bands, axis=1)
 
 
+def prep_kernel(eps, raw_ref, q_gain_ref, k_gain_ref, q_ref, kv_ref):
+    span = raw_ref.shape[1]
+    lane = lax.broadcasted_iota(jnp.int32, (1, 128), 1)
+    first = lane < 64
+    kv_ref[...] = jnp.zeros(kv_ref.shape, kv_ref.dtype)
+    for pair in range(raw_ref.shape[2] // 128):
+        cols = slice(pair * 128, (pair + 1) * 128)
+        for which, gain_ref in ((0, q_gain_ref), (1, k_gain_ref)):
+            piece = raw_ref[which, :, cols]
+            low = jnp.sum(jnp.where(first, piece, 0.0), axis=1, keepdims=True)
+            high = jnp.sum(jnp.where(first, 0.0, piece), axis=1, keepdims=True)
+            centered = piece - jnp.where(first, low, high) / 64.0
+            squared = centered * centered
+            low = jnp.sum(jnp.where(first, squared, 0.0), axis=1, keepdims=True)
+            high = jnp.sum(jnp.where(first, 0.0, squared), axis=1, keepdims=True)
+            spread = jnp.where(first, low, high) / 64.0
+            normed = (centered * lax.rsqrt(spread + eps) * gain_ref[:, cols]).astype(jnp.bfloat16)
+            if which == 0:
+                q_ref[:, cols] = normed
+            else:
+                kv_ref[0, :span, cols] = normed
+        kv_ref[1, :span, cols] = raw_ref[2, :, cols].astype(jnp.bfloat16)
+
+
+def prep_heads(raw, q_gain, k_gain, padded_span):
+    width = raw.shape[2]
+    tiles = width // q_gain.shape[0]
+    return pl.pallas_call(
+        functools.partial(prep_kernel, 1e-06),
+        out_shape=(
+            jax.ShapeDtypeStruct((raw.shape[1], width), jnp.bfloat16),
+            jax.ShapeDtypeStruct((2, padded_span, width), jnp.bfloat16),
+        ),
+        in_specs=[pl.BlockSpec(memory_space=pltpu.VMEM)] * 3,
+        out_specs=(pl.BlockSpec(memory_space=pltpu.VMEM), pl.BlockSpec(memory_space=pltpu.VMEM)),
+    )(raw, jnp.tile(q_gain, tiles)[None], jnp.tile(k_gain, tiles)[None])
+
+
 def layer_norm(tensor, epsilon):
     average = jnp.mean(tensor, axis=-1, keepdims=True)
     centered = tensor - average
@@ -580,28 +618,15 @@
     received_raw = partner_swap(projected_rows[:, span:], 5)
     raw = jnp.concatenate(
         [jnp.where(request_id == 0, own_raw, received_raw), jnp.where(request_id == 0, received_raw, own_raw)], axis=2
-    ).reshape(3, span, 2 * half_heads, head_dim)
-    full = jnp.stack([head_norm(raw[0], q_gain), head_norm(raw[1], k_gain), raw[2].astype(jnp.bfloat16)])
-    groups = 1
-    heads_here = full.shape[2]
-    queries = full[0, :block_tokens][None]
-    key_block = full[1][None]
-    value_block = full[2][None]
-    attend = attention_step(queries, owners, grid, text_len, span, block_tokens, tile, text_rows)
-    empty_state = (jnp.zeros(queries.shape, jnp.float32), jnp.zeros(queries.shape[:3], jnp.float32))
+    )
+    heads_here = raw.shape[2] // head_dim
     padded_span = 16 * pl.cdiv(span, 16)
-    both = jnp.stack([key_block[0], value_block[0]], axis=0).reshape(2, span, heads_here * head_dim)
-    both = jnp.pad(both, ((0, 0), (0, padded_span - span), (0, 0)))[None]
-    gathered = lax.all_gather(both, "row", axis=0, tiled=True)
+    all_queries, both = prep_heads(raw, q_gain, k_gain, padded_span)
+    gathered = lax.all_gather(both[None], "row", axis=0, tiled=True)
     live = key_mask(
         gathered.shape[0] * padded_span, owners, grid, text_len, padded_span, block_tokens, tile, text_rows
     )
-    attended = attention(
-        queries[0].reshape(block_tokens, heads_here * head_dim),
-        gathered,
-        live,
-        head_dim ** (-0.5),
-    )
+    attended = attention(all_queries[:block_tokens], gathered, live, head_dim ** (-0.5))
     partial_out = jnp.dot(attended, w_out, preferred_element_type=jnp.float32)
     projected = scatter_sum(partial_out.astype(jnp.bfloat16), "col", 1)
     own_rows = lax.dynamic_slice_in_dim(source, col_id * tile, tile, 0)

time: 430 us -> 426 us (level)
  transfers between devices with their start and end apart: 2 -> 2, of which waited for: 2 -> 2; matrix products, arithmetic and copies ran while one was open for 4% -> 5% of each run, Pallas kernels for 1% -> 1%
where the time goes in v12:
time: 426 us; the launch traced here: 425 us
  Pallas kernels  178 us (42%)
  waiting for transfers between devices  176 us (41%)
  matrix products  20.7 us (5%)
  other arithmetic  19.9 us (5%)
  between operations  18.4 us (4%)
  local copies, waits for them, and re-layouts  11.6 us (3%)
    all_gather x1, waiting for transfers between devices, shards(): gathered = lax.all_gather(both[None], 'row', axis=0, tiled=True)  95.3 us
    all_gather x1, waiting for transfers between devices, shards(): gathered_half = lax.all_gather(own_half, 'row', axis=1, tiled=True)  80.9 us
    pallas_call x1, Pallas kernels, ring_gather(): pl.pallas_call(functools.partial(ring_gather_kernel, zs, xs), out_shape=j...  66.6 us
    pallas_call x1, Pallas kernels, ring_scatter_sum(): pl.pallas_call(functools.partial(ring_scatter_kernel, zs, xs), out_shape=...  65.7 us
    pallas_call x1, Pallas kernels, halo_extend(): pl.pallas_call(halo_kernel, out_shape=jax.ShapeDtypeStruct((3, 3) + tile....  12.6 us
    pallas_call x1, Pallas kernels, attention(): pl.pallas_call(functools.partial(attention_kernel, scale), out_shape=jax....  11.2 us
    pallas_call x1, Pallas kernels, scatter_sum(): pl.pallas_call(functools.partial(scatter_sum_kernel, axis, count, rows),...  11 us
    dot_general x1, matrix products, shards(): jnp.dot(hidden_units, w_down, preferred_element_type=jnp.float32)  10.4 us
  transfers between devices with their start and end apart: 2, of which 2 were waited for; matrix products, arithmetic and copies ran while one was open for 5% of the time, Pallas kernels for 1%

profile of v12, /device:TPU:2, one launch (start us, length us, event | category | flops | bytes accessed | tf_op | source)
XLA Modules:
  0.0 425.0 jit_solution(9466916294225432623)
XLA Ops:
  7.3 1.8 constant_dynamic-slice_fusion
  9.2 0.9 convert_reduce_fusion.3
  10.1 0.9 fusion.43
  11.0 1.2 convert_reduce_fusion
  12.3 0.3 multiply_reduce_fusion
  12.6 0.7 slice_add_fusion
  13.3 0.1 fusion.46
  13.4 0.3 add_convert_fusion
  13.7 0.3 copy-done.8
  14.0 0.9 pad_maximum_fusion.1.src_ref
  14.9 4.0 shard_map.166
  19.0 0.6 tile.4
  19.6 1.4 broadcast_in_dim_tile.6.q_gain_ref
  20.9 1.3 tile.5
  22.2 1.4 broadcast_in_dim_tile.7.k_gain_ref
  23.5 80.9 %all-gather.4.cloned.1.call-done = bf16[3,3072,384]{2,1,0:T(8,128)(2,1)} async-done(((bf16[3,96,384]{2,1,0:T(8,128)(2,1)}), bf16[3,3072,384]{2,1,0:T(8,128)(2,1)}) %all-gather.4.cloned.1.call-update) | async-done | bytes 7077904 | tf_op jit(solution)/shard_map/all_gather | solution.py:612
  104.4 4.8 %convolution_bitcast_fusion = f32[3,200,384]{2,1,0:T(8,128)S(1)} fusion(bf16[3,3072,384]{2,1,0:T(8,128)(2,1)} %all-gather.4.cloned.1.call-done, bf16[100,3072]{1,0:T(8,128)(2,1)} %shard_map.166, bf16[4,3072]{1,0:T(4,128)(2,1)} %copy-done.8, bf16[96,3072]{1,0:T(8,128)(2,1)S(1)} %add_convert_fusion), kind=kOutput, calls=%fused_computation.3 | convolution fusion | flops 1419264000 | bytes 9228288 | tf_op jit(solution)/shard_map/ld,cde->cle/dot_general | solution.py:616
  109.3 0.9 copy-done.2
  110.2 0.8 slice.222.src_ref
  111.0 3.7 shard_map.167
  114.7 1.2 slice_select_fusion.1
  116.0 1.0 pad_maximum_fusion.raw_ref
  117.0 3.3 shard_map.168
  120.3 1.1 convert_element_type.67
  121.5 0.3 reduce-window.9
  121.9 0.6 select_reduce_fusion.4
  123.2 0.1 slice_reduce_fusion
  123.4 1.3 select_reduce_fusion
  127.2 0.2 slice_reduce_fusion.2
  127.4 0.6 select_reduce_fusion.2
  128.7 0.7 and_convert_fusion
  129.4 0.6 select_reduce_fusion.5
  130.0 0.6 fusion.80
  130.7 2.7 select_convert_fusion.live_ref
  133.4 0.7 slice.176.q_ref
  134.0 95.3 %all-gather.6.cloned.1.call-done = bf16[64,112,768]{2,1,0:T(8,128)(2,1)} async-done(((bf16[2,112,768]{2,1,0:T(8,128)(2,1)}), bf16[64,112,768]{2,1,0:T(8,128)(2,1)}) %all-gather.6.cloned.1.call-update) | async-done | bytes 11010064 | tf_op jit(solution)/shard_map/all_gather | solution.py:625
  229.3 11.2 %shard_map.169 = bf16[96,768]{1,0:T(8,128)(2,1)} custom-call(bf16[96,768]{1,0:T(8,128)(2,1)} %slice.176.q_ref, bf16[32,2,112,768]{3,2,1,0:T(8,128)(2,1)} %bitcast.149, f32[1,3584]{1,0:T(1,128)} %select_convert_fusion.live_ref), custom_call_target="tpu_custom_call" | custom-call | tf_op jit(solution)/shard_map/pallas_call | solution.py:130
  240.5 1.8 convolution_convert_fusion.1.part_ref
  242.3 11.0 %shard_map.170 = f32[24,3072]{1,0:T(8,128)S(1)} custom-call(bf16[96,3072]{1,0:T(8,128)(2,1)S(1)} %convolution_convert_fusion.1.part_ref), custom_call_target="tpu_custom_call" | custom-call | tf_op jit(solution)/shard_map/pallas_call | solution.py:89
  253.4 1.0 fusion.34
  254.4 0.1 convert_reduce_fusion.1
  254.5 0.2 fusion.25
  254.7 0.8 fusion.28.block_ref
  255.5 66.6 %shard_map.171 = bf16[8,4,24,3072]{3,2,1,0:T(8,128)(2,1)} custom-call(bf16[24,3072]{1,0:T(8,128)(2,1)} %fusion.28.block_ref), custom_call_target="tpu_custom_call" | custom-call | tf_op jit(solution)/shard_map/pallas_call | solution.py:322
  322.1 10.4 %convolution_convert_fusion = bf16[768,3072]{1,0:T(8,128)(2,1)} fusion(bf16[384,3072]{1,0:T(8,128)(2,1)S(1)} %copy-done, bf16[768,3072]{1,0:T(8,128)(2,1)} %bitcast.150, bf16[3072,384]{1,0:T(8,128)(2,1)} %param.25), kind=kOutput, calls=%fused_computation | convolution fusion | flops 3628892160 | bytes 14155776 | tf_op jit(solution)/shard_map/dot_general | solution.py:645
  332.5 65.7 %shard_map.172 = f32[24,3072]{1,0:T(8,128)} custom-call(bf16[8,4,24,3072]{3,2,1,0:T(8,128)(2,1)} %bitcast.151), custom_call_target="tpu_custom_call" | custom-call | tf_op jit(solution)/shard_map/pallas_call | solution.py:231
  398.2 1.1 convert_reduce_fusion.2
  399.4 0.2 fusion.29
  399.6 0.9 multiply_convert_fusion
  400.5 0.1 copy.21
  400.6 0.1 convert_element_type.85
  400.8 0.9 copy.22
  401.6 12.6 %shard_map.173 = bf16[3,3,6,2,8,16]{5,4,3,2,1,0:T(8,128)(2,1)} custom-call(bf16[6,2,8,16]{3,2,1,0:T(8,128)(2,1)} %bitcast.160), custom_call_target="tpu_custom_call" | custom-call | tf_op jit(solution)/shard_map/pallas_call | solution.py:428
  414.2 0.9 slice_bitcast_fusion.2
  415.2 0.1 maximum_maximum_fusion.1
  415.3 0.1 fusion.54
  415.5 0.2 convolution_add_fusion.7
  415.6 0.1 convolution_add_fusion.6
  415.8 0.2 convolution_add_fusion.5
  416.0 0.9 convolution_add_fusion.4
  416.8 0.2 convolution_add_fusion.3
  417.0 0.1 convolution_add_fusion.2
  417.2 0.2 convolution_add_fusion.1
  417.3 0.8 fusion.13
  (69 shorter events, 0.6 us)
Async XLA Ops:
  7.2 314.9 %copy-start = (bf16[384,3072]{1,0:T(8,128)(2,1)S(1)}, bf16[384,3072]{1,0:T(8,128)(2,1)}, u32[]{:S(2)}) copy-start(bf16[384,3072]{1,0:T(8,128)(2,1)} %param.26) | copy-start | bytes 7077892
  7.2 6.1 %copy-start.4 = (bf16[1,4,3072]{2,1,0:T(4,128)(2,1)S(1)}, bf16[1,4,3072]{2,1,0:T(4,128)(2,1)}, u32[]{:S(2)}) copy-start(bf16[1,4,3072]{2,1,0:T(4,128)(2,1)} %param.16) | copy-start | bytes 73732
  7.2 5.1 %copy-start.1 = (bf16[1,96,3072]{2,1,0:T(8,128)(2,1)S(1)}, bf16[1,96,3072]{2,1,0:T(8,128)(2,1)}, u32[]{:S(2)}) copy-start(bf16[1,96,3072]{2,1,0:T(8,128)(2,1)} %param.15) | copy-start | bytes 1769476
  7.2 5.4 %copy-start.7 = (f32[1,8,3072]{2,1,0:T(8,128)S(1)}, f32[1,8,3072]{2,1,0:T(8,128)}, u32[]{:S(2)}) copy-start(f32[1,8,3072]{2,1,0:T(8,128)} %param.20) | copy-start | bytes 294916
  7.2 97.2 %all-gather.4.cloned.1.call-start = ((), (), s32[]{:S(2)}) async-start(), calls=%async_computation | async-start | bytes 7299072 | tf_op jit(solution)/shard_map/all_gather | solution.py:612
  9.1 220.2 %all-gather.6.cloned.1.call-start = ((), (), s32[]{:S(2)}) async-start(), calls=%async_computation.1 | async-start | bytes 11354112 | tf_op jit(solution)/shard_map/all_gather | solution.py:625
  13.4 0.6 copy-start.8
  14.0 4.9 %copy-start.15 = (f32[64]{0:T(128)S(1)}, f32[64]{0:T(128)}, u32[]{:S(2)}) copy-start(f32[64]{0:T(128)} %param.21) | copy-start | bytes 772
  109.2 0.9 copy-start.2
  120.3 1.6 copy-start.18
  120.3 7.0 %copy-start.14 = (s32[2,2]{1,0:T(2,128)S(1)}, s32[2,2]{1,0:T(2,128)}, u32[]{:S(2)}) copy-start(s32[2,2]{1,0:T(2,128)} %param.18) | copy-start | bytes 52
  120.3 9.1 %copy-start.19 = (s32[2]{0:T(128)S(1)}, s32[2]{0:T(128)}, u32[]{:S(2)}) copy-start(s32[2]{0:T(128)} %param.17) | copy-start | bytes 28
  120.3 13.1 %copy-start.6 = (bf16[100,768]{1,0:T(8,128)(2,1)S(1)}, bf16[100,768]{1,0:T(8,128)(2,1)}, u32[]{:S(2)}) copy-start(bf16[100,768]{1,0:T(8,128)(2,1)} %get-tuple-element.5) | copy-start | bytes 460804
  123.3 117.2 %slice-start = ((s8[4718592]{0:T(1024)(128)(4,1)}), s8[524288]{0:T(1024)(128)(4,1)S(1)}, s32[]{:S(2)}) async-start(s8[4718592]{0:T(1024)(128)(4,1)} %bitcast.152), calls=%async_computation.2 | async-start | bytes 1048576
  229.3 11.2 %slice-start.1 = ((s8[4718592]{0:T(1024)(128)(4,1)}), s8[4194304]{0:T(1024)(128)(4,1)S(1)}, s32[]{:S(2)}) async-start(s8[4718592]{0:T(1024)(128)(4,1)} %bitcast.152), calls=%async_computation.3 | async-start | bytes 8388608
  240.5 12.8 %copy-start.11 = (f32[1,1,3072]{2,1,0:T(1,128)S(1)}, f32[1,1,3072]{2,1,0:T(1,128)}, u32[]{:S(2)}) copy-start(f32[1,1,3072]{2,1,0:T(1,128)} %get-tuple-element.30) | copy-start | bytes 36868
  242.3 12.4 %copy-start.9 = (f32[1,1,3072]{2,1,0:T(1,128)S(1)}, f32[1,1,3072]{2,1,0:T(1,128)}, u32[]{:S(2)}) copy-start(f32[1,1,3072]{2,1,0:T(1,128)} %get-tuple-element.26) | copy-start | bytes 36868
  332.5 65.7 %copy-start.10 = (f32[1,1,3072]{2,1,0:T(1,128)S(1)}, f32[1,1,3072]{2,1,0:T(1,128)}, u32[]{:S(2)}) copy-start(f32[1,1,3072]{2,1,0:T(1,128)} %get-tuple-element.27) | copy-start | bytes 36868
  332.5 67.1 %copy-start.12 = (f32[1,1,3072]{2,1,0:T(1,128)S(1)}, f32[1,1,3072]{2,1,0:T(1,128)}, u32[]{:S(2)}) copy-start(f32[1,1,3072]{2,1,0:T(1,128)} %get-tuple-element.24) | copy-start | bytes 36868
  332.5 67.1 %copy-start.13 = (f32[1,1,3072]{2,1,0:T(1,128)S(1)}, f32[1,1,3072]{2,1,0:T(1,128)}, u32[]{:S(2)}) copy-start(f32[1,1,3072]{2,1,0:T(1,128)} %get-tuple-element.31) | copy-start | bytes 36868
  332.5 67.1 %copy-start.16 = (bf16[3072,64]{0,1:T(8,128)(2,1)S(1)}, bf16[3072,64]{0,1:T(8,128)(2,1)}, u32[]{:S(2)}) copy-start(bf16[3072,64]{0,1:T(8,128)(2,1)} %param.27) | copy-start | bytes 1179652
  332.5 67.1 %copy-start.17 = (f32[1,24,64]{2,1,0:T(8,128)S(1)}, f32[1,24,64]{2,1,0:T(8,128)}, u32[]{:S(2)}) copy-start(f32[1,24,64]{2,1,0:T(8,128)} %param.28) | copy-start | bytes 18436
  399.3 16.1 %copy-start.3 = (bf16[24,3072]{1,0:T(8,128)(2,1)}, bf16[24,3072]{1,0:T(8,128)(2,1)S(1)}, u32[]{:S(2)}) copy-start(bf16[24,3072]{1,0:T(8,128)(2,1)S(1)} %get-tuple-element.12) | copy-start | bytes 442372
  399.3 16.0 %copy-start.5 = (bf16[3,3,16,512]{3,2,1,0:T(8,128)(2,1)S(1)}, bf16[3,3,16,512]{3,2,1,0:T(8,128)(2,1)}, u32[]{:S(2)}) copy-start(bf16[3,3,16,512]{3,2,1,0:T(8,128)(2,1)} %param.29) | copy-start | bytes 442372
Sparse Core Ops, SparseCore 0:
  10.6 93.7 all-gather.3
  120.4 108.8 all-gather.5

commit v13 on v12

--- a/solution.py
+++ b/solution.py
@@ -103,16 +103,19 @@
     )(part)
 
 
-def attention_kernel(scale, q_ref, kv_ref, live_ref, out_ref):
-    sources, _, block, width = kv_ref.shape
+def attention_kernel(scale, q_ref, first_kv, second_kv, first_live, second_live, out_ref):
     lane = lax.broadcasted_iota(jnp.int32, (1, 128), 1)
     first = lane < 64
-    live = live_ref[...]
-    for pair in range(width // 128):
+    per_half = first_kv.shape[3] // 128
+    for pair in range(2 * per_half):
+        kv_ref, live_ref = (first_kv, first_live) if pair < per_half else (second_kv, second_live)
+        sources, _, block, width = kv_ref.shape
+        live = live_ref[...]
         cols = slice(pair * 128, (pair + 1) * 128)
+        local = slice((pair % per_half) * 128, (pair % per_half + 1) * 128)
         query = q_ref[:, cols]
-        keys = kv_ref[:, 0, :, cols].reshape(sources * block, 128)
-        values = kv_ref[:, 1, :, cols].reshape(sources * block, 128)
+        keys = kv_ref[:, 0, :, local].reshape(sources * block, 128)
+        values = kv_ref[:, 1, :, local].reshape(sources * block, 128)
         results = []
         for half in (first, jnp.logical_not(first)):
             picked = jnp.where(half, query, jnp.zeros_like(query))
@@ -126,14 +129,14 @@
         out_ref[:, cols] = jnp.where(first, results[0], results[1]).astype(out_ref.dtype)
 
 
-def attention(queries, gathered, live, scale):
+def attention(queries, first_kv, second_kv, first_live, second_live, scale):
     return pl.pallas_call(
         functools.partial(attention_kernel, scale),
         out_shape=jax.ShapeDtypeStruct(queries.shape, jnp.bfloat16),
-        in_specs=[pl.BlockSpec(memory_space=pltpu.VMEM)] * 3,
+        in_specs=[pl.BlockSpec(memory_space=pltpu.VMEM)] * 5,
         out_specs=pl.BlockSpec(memory_space=pltpu.VMEM),
         compiler_params=pltpu.CompilerParams(vmem_limit_bytes=56 * 1024 * 1024),
-    )(queries, gathered, live)
+    )(queries, first_kv, second_kv, first_live, second_live)
 
 
 def ring_scatter_kernel(zs, xs, part_ref, out_ref, landed, outgoing, own_sum, crossed, ring_send, ring_recv, cross_send, cross_recv):
@@ -622,11 +625,14 @@
     heads_here = raw.shape[2] // head_dim
     padded_span = 16 * pl.cdiv(span, 16)
     all_queries, both = prep_heads(raw, q_gain, k_gain, padded_span)
-    gathered = lax.all_gather(both[None], "row", axis=0, tiled=True)
-    live = key_mask(
-        gathered.shape[0] * padded_span, owners, grid, text_len, padded_span, block_tokens, tile, text_rows
-    )
-    attended = attention(all_queries[:block_tokens], gathered, live, head_dim ** (-0.5))
+    split_cols = both.shape[2] // 2
+    first_kv = lax.all_gather(both[None, :, :, :split_cols], "row", axis=0, tiled=True)
+    second_kv = ring_gather(both[:, :, split_cols:], 4, 8, 7)
+    second_kv = second_kv.reshape((-1,) + second_kv.shape[2:])
+    sources = first_kv.shape[0]
+    live = key_mask(sources * padded_span, owners, grid, text_len, padded_span, block_tokens, tile, text_rows)
+    second_live = live.reshape(4, sources // 4, padded_span).transpose(1, 0, 2).reshape(1, -1)
+    attended = attention(all_queries[:block_tokens], first_kv, second_kv, live, second_live, head_dim ** (-0.5))
     partial_out = jnp.dot(attended, w_out, preferred_element_type=jnp.float32)
     projected = scatter_sum(partial_out.astype(jnp.bfloat16), "col", 1)
     own_rows = lax.dynamic_slice_in_dim(source, col_id * tile, tile, 0)

time: 426 us -> 435 us (1.021); the launches traced: 425 us -> 429 us
  waiting for transfers between devices: 176 us -> 80.9 us
  Pallas kernels: 178 us -> 272 us
    pallas_call x1 -> x2, Pallas kernels: 66.6 us -> 167 us  [ring_gather(): pl.pallas_call(functools.partial(ring_gather_kernel, zs, xs), out_shape=j...]
    all_gather x1, waiting for transfers between devices: 95.3 us -> 0.02 us  [shards(): lax.all_gather(both[None, :, :, :split_cols], 'row', axis=0, tiled=True)]
  transfers between devices with their start and end apart: 2 -> 2, of which waited for: 2 -> 1; matrix products, arithmetic and copies ran while one was open for 5% -> 5% of each run, Pallas kernels for 1% -> 24%
where the time goes in v13:
time: 435 us; the launch traced here: 429 us
  Pallas kernels  272 us (63%)
  waiting for transfers between devices  80.9 us (19%)
  other arithmetic  23 us (5%)
  matrix products  20.7 us (5%)
  between operations  18.7 us (4%)
  local copies, waits for them, and re-layouts  13.7 us (3%)
    pallas_call x2, Pallas kernels, ring_gather(): pl.pallas_call(functools.partial(ring_gather_kernel, zs, xs), out_shape=j...  167 us
    all_gather x1, waiting for transfers between devices, shards(): gathered_half = lax.all_gather(own_half, 'row', axis=1, tiled=True)  80.9 us
    pallas_call x1, Pallas kernels, ring_scatter_sum(): pl.pallas_call(functools.partial(ring_scatter_kernel, zs, xs), out_shape=...  63.7 us
    pallas_call x1, Pallas kernels, attention(): pl.pallas_call(functools.partial(attention_kernel, scale), out_shape=jax....  11.3 us
    dot_general x1, matrix products, shards(): jnp.dot(hidden_units, w_down, preferred_element_type=jnp.float32)  10.4 us
    pallas_call x1, Pallas kernels, halo_extend(): pl.pallas_call(halo_kernel, out_shape=jax.ShapeDtypeStruct((3, 3) + tile....  9.55 us
    pallas_call x1, Pallas kernels, scatter_sum(): pl.pallas_call(functools.partial(scatter_sum_kernel, axis, count, rows),...  9.33 us
  transfers between devices with their start and end apart: 2, of which 1 were waited for; matrix products, arithmetic and copies ran while one was open for 5% of the time, Pallas kernels for 24%

profile of v13, /device:TPU:2, one launch (start us, length us, event | category | flops | bytes accessed | tf_op | source)
XLA Modules:
  0.0 429.4 jit_solution(14674223510641908148)
XLA Ops:
  7.3 1.8 constant_dynamic-slice_fusion
  9.2 0.9 convert_reduce_fusion.3
  10.1 0.9 fusion.43
  11.0 1.2 convert_reduce_fusion
  12.3 0.3 multiply_reduce_fusion
  12.6 0.7 slice_add_fusion
  13.4 0.3 add_convert_fusion
  13.7 0.3 copy-done.8
  14.0 0.9 pad_maximum_fusion.1.src_ref
  14.9 4.0 shard_map.166
  19.0 0.6 tile.4
  19.6 1.4 broadcast_in_dim_tile.6.q_gain_ref
  20.9 1.3 tile.5
  22.2 1.4 broadcast_in_dim_tile.7.k_gain_ref
  23.5 80.9 %all-gather.4.cloned.1.call-done = bf16[3,3072,384]{2,1,0:T(8,128)(2,1)} async-done(((bf16[3,96,384]{2,1,0:T(8,128)(2,1)}), bf16[3,3072,384]{2,1,0:T(8,128)(2,1)}) %all-gather.4.cloned.1.call-update) | async-done | bytes 7077904 | tf_op jit(solution)/shard_map/all_gather | solution.py:615
  104.4 4.8 %convolution_bitcast_fusion = f32[3,200,384]{2,1,0:T(8,128)S(1)} fusion(bf16[3,3072,384]{2,1,0:T(8,128)(2,1)} %all-gather.4.cloned.1.call-done, bf16[100,3072]{1,0:T(8,128)(2,1)} %shard_map.166, bf16[4,3072]{1,0:T(4,128)(2,1)} %copy-done.8, bf16[96,3072]{1,0:T(8,128)(2,1)S(1)} %add_convert_fusion), kind=kOutput, calls=%fused_computation.3 | convolution fusion | flops 1419264000 | bytes 9228288 | tf_op jit(solution)/shard_map/ld,cde->cle/dot_general | solution.py:619
  109.3 0.9 copy-done.2
  110.2 0.8 slice.230.src_ref
  111.0 3.7 shard_map.167
  114.7 1.2 slice_select_fusion.1
  116.0 1.0 pad_maximum_fusion.raw_ref
  117.0 3.4 shard_map.168
  120.3 1.8 fusion.95
  122.1 1.1 convert_element_type.69
  123.3 0.3 reduce-window.9
  123.7 0.6 select_reduce_fusion.4
  125.0 0.1 slice_reduce_fusion
  125.2 1.3 select_reduce_fusion
  129.4 0.1 div.102
  129.8 0.2 slice_reduce_fusion.2
  129.9 0.6 select_reduce_fusion.2
  131.3 0.7 and_convert_fusion
  131.9 0.6 select_reduce_fusion.5
  132.6 0.7 fusion.84
  133.3 2.8 select_convert_fusion.1.first_live
  136.0 2.8 select_convert_fusion.second_live
  138.8 0.7 slice.182.q_ref
  139.5 99.8 %shard_map.169 = bf16[8,4,2,112,384]{4,3,2,1,0:T(8,128)(2,1)} custom-call(bf16[2,112,384]{2,1,0:T(8,128)(2,1)} %get-tuple-element.15.block_ref), custom_call_target="tpu_custom_call" | custom-call | tf_op jit(solution)/shard_map/pallas_call | solution.py:325
  239.4 11.3 %shard_map.170 = bf16[96,768]{1,0:T(8,128)(2,1)} custom-call(bf16[96,768]{1,0:T(8,128)(2,1)} %slice.182.q_ref, bf16[32,2,112,384]{3,2,1,0:T(8,128)(2,1)} %bitcast.151, bf16[32,2,112,384]{3,2,1,0:T(8,128)(2,1)} %bitcast.150, f32[1,3584]{1,0:T(1,128)} %select_convert_fusion.1.first_live, f32[1,3584]{1,0:T(1,128)} %select_convert_fusion.second_live), custom_call_target="tpu_custom_call" | custom-call | tf_op jit(solution)/shard_map/pallas_call | solution.py:133
  250.6 1.8 convolution_convert_fusion.1.part_ref
  252.5 9.3 %shard_map.171 = f32[24,3072]{1,0:T(8,128)S(1)} custom-call(bf16[96,3072]{1,0:T(8,128)(2,1)S(1)} %convolution_convert_fusion.1.part_ref), custom_call_target="tpu_custom_call" | custom-call | tf_op jit(solution)/shard_map/pallas_call | solution.py:89
  261.8 1.0 fusion.34
  262.8 0.1 convert_reduce_fusion.1
  263.0 0.2 fusion.25
  263.2 0.8 fusion.28.block_ref
  264.0 67.6 %shard_map.172 = bf16[8,4,24,3072]{3,2,1,0:T(8,128)(2,1)} custom-call(bf16[24,3072]{1,0:T(8,128)(2,1)} %fusion.28.block_ref), custom_call_target="tpu_custom_call" | custom-call | tf_op jit(solution)/shard_map/pallas_call | solution.py:325
  331.6 10.4 %convolution_convert_fusion = bf16[768,3072]{1,0:T(8,128)(2,1)} fusion(bf16[384,3072]{1,0:T(8,128)(2,1)S(1)} %copy-done, bf16[768,3072]{1,0:T(8,128)(2,1)} %bitcast.152, bf16[3072,384]{1,0:T(8,128)(2,1)} %param.25), kind=kOutput, calls=%fused_computation | convolution fusion | flops 3628892160 | bytes 14155776 | tf_op jit(solution)/shard_map/dot_general | solution.py:651
  342.0 63.7 %shard_map.173 = f32[24,3072]{1,0:T(8,128)} custom-call(bf16[8,4,24,3072]{3,2,1,0:T(8,128)(2,1)} %bitcast.153), custom_call_target="tpu_custom_call" | custom-call | tf_op jit(solution)/shard_map/pallas_call | solution.py:234
  405.7 1.1 convert_reduce_fusion.2
  406.9 0.2 fusion.29
  407.1 0.9 multiply_convert_fusion
  408.1 0.1 convert_element_type.88
  408.3 0.9 copy.22
  409.1 9.5 %shard_map.174 = bf16[3,3,6,2,8,16]{5,4,3,2,1,0:T(8,128)(2,1)} custom-call(bf16[6,2,8,16]{3,2,1,0:T(8,128)(2,1)} %bitcast.162), custom_call_target="tpu_custom_call" | custom-call | tf_op jit(solution)/shard_map/pallas_call | solution.py:431
  418.7 0.9 slice_bitcast_fusion.2
  419.8 0.1 fusion.54
  420.0 0.2 convolution_add_fusion.7
  420.1 0.2 convolution_add_fusion.6
  420.3 0.2 convolution_add_fusion.5
  420.4 0.9 convolution_add_fusion.4
  421.3 0.2 convolution_add_fusion.3
  421.5 0.1 convolution_add_fusion.2
  421.7 0.2 convolution_add_fusion.1
  421.8 0.8 fusion.13
  (78 shorter events, 1.1 us)
Async XLA Ops:
  7.2 324.4 %copy-start = (bf16[384,3072]{1,0:T(8,128)(2,1)S(1)}, bf16[384,3072]{1,0:T(8,128)(2,1)}, u32[]{:S(2)}) copy-start(bf16[384,3072]{1,0:T(8,128)(2,1)} %param.26) | copy-start | bytes 7077892
  7.2 6.1 %copy-start.4 = (bf16[1,4,3072]{2,1,0:T(4,128)(2,1)S(1)}, bf16[1,4,3072]{2,1,0:T(4,128)(2,1)}, u32[]{:S(2)}) copy-start(bf16[1,4,3072]{2,1,0:T(4,128)(2,1)} %param.16) | copy-start | bytes 73732
  7.2 5.1 %copy-start.1 = (bf16[1,96,3072]{2,1,0:T(8,128)(2,1)S(1)}, bf16[1,96,3072]{2,1,0:T(8,128)(2,1)}, u32[]{:S(2)}) copy-start(bf16[1,96,3072]{2,1,0:T(8,128)(2,1)} %param.15) | copy-start | bytes 1769476
  7.2 5.4 %copy-start.7 = (f32[1,8,3072]{2,1,0:T(8,128)S(1)}, f32[1,8,3072]{2,1,0:T(8,128)}, u32[]{:S(2)}) copy-start(f32[1,8,3072]{2,1,0:T(8,128)} %param.20) | copy-start | bytes 294916
  7.2 97.2 %all-gather.4.cloned.1.call-start = ((), (), s32[]{:S(2)}) async-start(), calls=%async_computation | async-start | bytes 7299072 | tf_op jit(solution)/shard_map/all_gather | solution.py:615
  9.1 230.2 %all-gather.6.cloned.1.call-start = ((), (), s32[]{:S(2)}) async-start(), calls=%async_computation.1 | async-start | bytes 5677056 | tf_op jit(solution)/shard_map/all_gather | solution.py:629
  13.4 0.6 copy-start.8
  14.0 4.9 %copy-start.15 = (f32[64]{0:T(128)S(1)}, f32[64]{0:T(128)}, u32[]{:S(2)}) copy-start(f32[64]{0:T(128)} %param.21) | copy-start | bytes 772
  109.2 0.9 copy-start.2
  120.3 3.4 copy-start.18
  122.1 7.7 %copy-start.14 = (s32[2,2]{1,0:T(2,128)S(1)}, s32[2,2]{1,0:T(2,128)}, u32[]{:S(2)}) copy-start(s32[2,2]{1,0:T(2,128)} %param.18) | copy-start | bytes 52
  122.1 9.8 %copy-start.19 = (s32[2]{0:T(128)S(1)}, s32[2]{0:T(128)}, u32[]{:S(2)}) copy-start(s32[2]{0:T(128)} %param.17) | copy-start | bytes 28
  122.1 16.7 %copy-start.6 = (bf16[100,768]{1,0:T(8,128)(2,1)S(1)}, bf16[100,768]{1,0:T(8,128)(2,1)}, u32[]{:S(2)}) copy-start(bf16[100,768]{1,0:T(8,128)(2,1)} %get-tuple-element.5) | copy-start | bytes 460804
  139.5 111.1 %slice-start = ((s8[4718592]{0:T(1024)(128)(4,1)}), s8[524288]{0:T(1024)(128)(4,1)S(1)}, s32[]{:S(2)}) async-start(s8[4718592]{0:T(1024)(128)(4,1)} %bitcast.154), calls=%async_computation.2 | async-start | bytes 1048576
  239.4 11.3 %slice-start.1 = ((s8[4718592]{0:T(1024)(128)(4,1)}), s8[4194304]{0:T(1024)(128)(4,1)S(1)}, s32[]{:S(2)}) async-start(s8[4718592]{0:T(1024)(128)(4,1)} %bitcast.154), calls=%async_computation.3 | async-start | bytes 8388608
  250.6 11.2 %copy-start.11 = (f32[1,1,3072]{2,1,0:T(1,128)S(1)}, f32[1,1,3072]{2,1,0:T(1,128)}, u32[]{:S(2)}) copy-start(f32[1,1,3072]{2,1,0:T(1,128)} %get-tuple-element.32) | copy-start | bytes 36868
  252.4 10.7 %copy-start.9 = (f32[1,1,3072]{2,1,0:T(1,128)S(1)}, f32[1,1,3072]{2,1,0:T(1,128)}, u32[]{:S(2)}) copy-start(f32[1,1,3072]{2,1,0:T(1,128)} %get-tuple-element.28) | copy-start | bytes 36868
  342.0 63.7 %copy-start.10 = (f32[1,1,3072]{2,1,0:T(1,128)S(1)}, f32[1,1,3072]{2,1,0:T(1,128)}, u32[]{:S(2)}) copy-start(f32[1,1,3072]{2,1,0:T(1,128)} %get-tuple-element.29) | copy-start | bytes 36868
  342.0 65.1 %copy-start.12 = (f32[1,1,3072]{2,1,0:T(1,128)S(1)}, f32[1,1,3072]{2,1,0:T(1,128)}, u32[]{:S(2)}) copy-start(f32[1,1,3072]{2,1,0:T(1,128)} %get-tuple-element.26) | copy-start | bytes 36868
  342.0 65.1 %copy-start.13 = (f32[1,1,3072]{2,1,0:T(1,128)S(1)}, f32[1,1,3072]{2,1,0:T(1,128)}, u32[]{:S(2)}) copy-start(f32[1,1,3072]{2,1,0:T(1,128)} %get-tuple-element.33) | copy-start | bytes 36868
  342.0 65.1 %copy-start.16 = (bf16[3072,64]{0,1:T(8,128)(2,1)S(1)}, bf16[3072,64]{0,1:T(8,128)(2,1)}, u32[]{:S(2)}) copy-start(bf16[3072,64]{0,1:T(8,128)(2,1)} %param.27) | copy-start | bytes 1179652
  342.0 65.1 %copy-start.17 = (f32[1,24,64]{2,1,0:T(8,128)S(1)}, f32[1,24,64]{2,1,0:T(8,128)}, u32[]{:S(2)}) copy-start(f32[1,24,64]{2,1,0:T(8,128)} %param.28) | copy-start | bytes 18436
  406.8 13.1 %copy-start.3 = (bf16[24,3072]{1,0:T(8,128)(2,1)}, bf16[24,3072]{1,0:T(8,128)(2,1)S(1)}, u32[]{:S(2)}) copy-start(bf16[24,3072]{1,0:T(8,128)(2,1)S(1)} %get-tuple-element.12) | copy-start | bytes 442372
  406.8 13.0 %copy-start.5 = (bf16[3,3,16,512]{3,2,1,0:T(8,128)(2,1)S(1)}, bf16[3,3,16,512]{3,2,1,0:T(8,128)(2,1)}, u32[]{:S(2)}) copy-start(bf16[3,3,16,512]{3,2,1,0:T(8,128)(2,1)} %param.29) | copy-start | bytes 442372
Sparse Core Ops, SparseCore 0:
  10.6 93.7 all-gather.3
  122.2 100.6 all-gather.5

commit v14 on v12

--- a/solution.py
+++ b/solution.py
@@ -113,17 +113,16 @@
         query = q_ref[:, cols]
         keys = kv_ref[:, 0, :, cols].reshape(sources * block, 128)
         values = kv_ref[:, 1, :, cols].reshape(sources * block, 128)
-        results = []
-        for half in (first, jnp.logical_not(first)):
-            picked = jnp.where(half, query, jnp.zeros_like(query))
-            scores = lax.dot_general(
-                picked, keys, (((1,), (1,)), ((), ())), preferred_element_type=jnp.float32
-            ) * scale
-            weights = jnp.exp(scores) * live
-            totals = jnp.sum(weights, axis=1, keepdims=True)
-            summed = jnp.dot(weights.astype(jnp.bfloat16), values, preferred_element_type=jnp.float32)
-            results.append(summed / totals)
-        out_ref[:, cols] = jnp.where(first, results[0], results[1]).astype(out_ref.dtype)
+        rows = query.shape[0]
+        zeros = jnp.zeros_like(query)
+        picked = jnp.concatenate([jnp.where(first, query, zeros), jnp.where(first, zeros, query)], axis=0)
+        scores = lax.dot_general(
+            picked, keys, (((1,), (1,)), ((), ())), preferred_element_type=jnp.float32
+        ) * scale
+        weights = jnp.exp(scores) * live
+        totals = jnp.sum(weights, axis=1, keepdims=True)
+        summed = jnp.dot(weights.astype(jnp.bfloat16), values, preferred_element_type=jnp.float32) / totals
+        out_ref[:, cols] = jnp.where(first, summed[:rows], summed[rows:]).astype(out_ref.dtype)
 
 
 def attention(queries, gathered, live, scale):

time: 426 us -> 424 us (level)
  no operation moved by 1% of the time
where the time goes in v14:
time: 424 us; the launch traced here: 423 us
  Pallas kernels  177 us (42%)
  waiting for transfers between devices  176 us (42%)
  matrix products  20.7 us (5%)
  other arithmetic  19.9 us (5%)
  between operations  18.4 us (4%)
  local copies, waits for them, and re-layouts  11.6 us (3%)
    all_gather x1, waiting for transfers between devices, shards(): gathered = lax.all_gather(both[None], 'row', axis=0, tiled=True)  95.3 us
    all_gather x1, waiting for transfers between devices, shards(): gathered_half = lax.all_gather(own_half, 'row', axis=1, tiled=True)  80.9 us
    pallas_call x1, Pallas kernels, ring_gather(): pl.pallas_call(functools.partial(ring_gather_kernel, zs, xs), out_shape=j...  66.6 us
    pallas_call x1, Pallas kernels, ring_scatter_sum(): pl.pallas_call(functools.partial(ring_scatter_kernel, zs, xs), out_shape=...  65.3 us
    pallas_call x1, Pallas kernels, halo_extend(): pl.pallas_call(halo_kernel, out_shape=jax.ShapeDtypeStruct((3, 3) + tile....  12 us
    pallas_call x1, Pallas kernels, scatter_sum(): pl.pallas_call(functools.partial(scatter_sum_kernel, axis, count, rows),...  11 us
    pallas_call x1, Pallas kernels, attention(): pl.pallas_call(functools.partial(attention_kernel, scale), out_shape=jax....  10.5 us
    dot_general x1, matrix products, shards(): jnp.dot(hidden_units, w_down, preferred_element_type=jnp.float32)  10.4 us
  transfers between devices with their start and end apart: 2, of which 2 were waited for; matrix products, arithmetic and copies ran while one was open for 5% of the time, Pallas kernels for 1%

profile of v14, /device:TPU:2, one launch (start us, length us, event | category | flops | bytes accessed | tf_op | source)
XLA Modules:
  0.0 423.5 jit_solution(15884749188765805265)
XLA Ops:
  7.3 1.8 constant_dynamic-slice_fusion
  9.2 0.9 convert_reduce_fusion.3
  10.1 0.9 fusion.43
  11.0 1.2 convert_reduce_fusion
  12.3 0.3 multiply_reduce_fusion
  12.6 0.7 slice_add_fusion
  13.3 0.1 fusion.46
  13.4 0.3 add_convert_fusion
  13.7 0.3 copy-done.8
  14.0 0.9 pad_maximum_fusion.1.src_ref
  14.9 4.0 shard_map.166
  19.0 0.6 tile.4
  19.6 1.4 broadcast_in_dim_tile.6.q_gain_ref
  20.9 1.3 tile.5
  22.2 1.4 broadcast_in_dim_tile.7.k_gain_ref
  23.5 80.9 %all-gather.4.cloned.1.call-done = bf16[3,3072,384]{2,1,0:T(8,128)(2,1)} async-done(((bf16[3,96,384]{2,1,0:T(8,128)(2,1)}), bf16[3,3072,384]{2,1,0:T(8,128)(2,1)}) %all-gather.4.cloned.1.call-update) | async-done | bytes 7077904 | tf_op jit(solution)/shard_map/all_gather | solution.py:611
  104.4 4.8 %convolution_bitcast_fusion = f32[3,200,384]{2,1,0:T(8,128)S(1)} fusion(bf16[3,3072,384]{2,1,0:T(8,128)(2,1)} %all-gather.4.cloned.1.call-done, bf16[100,3072]{1,0:T(8,128)(2,1)} %shard_map.166, bf16[4,3072]{1,0:T(4,128)(2,1)} %copy-done.8, bf16[96,3072]{1,0:T(8,128)(2,1)S(1)} %add_convert_fusion), kind=kOutput, calls=%fused_computation.3 | convolution fusion | flops 1419264000 | bytes 9228288 | tf_op jit(solution)/shard_map/ld,cde->cle/dot_general | solution.py:615
  109.3 0.9 copy-done.2
  110.2 0.8 slice.222.src_ref
  111.0 3.7 shard_map.167
  114.7 1.2 slice_select_fusion.1
  116.0 1.0 pad_maximum_fusion.raw_ref
  117.0 3.3 shard_map.168
  120.3 1.1 convert_element_type.67
  121.5 0.3 reduce-window.9
  121.9 0.6 select_reduce_fusion.4
  123.2 0.1 slice_reduce_fusion
  123.4 1.3 select_reduce_fusion
  127.2 0.2 slice_reduce_fusion.2
  127.4 0.6 select_reduce_fusion.2
  128.7 0.7 and_convert_fusion
  129.4 0.6 select_reduce_fusion.5
  130.0 0.6 fusion.80
  130.7 2.7 select_convert_fusion.live_ref
  133.4 0.7 slice.176.q_ref
  134.0 95.3 %all-gather.6.cloned.1.call-done = bf16[64,112,768]{2,1,0:T(8,128)(2,1)} async-done(((bf16[2,112,768]{2,1,0:T(8,128)(2,1)}), bf16[64,112,768]{2,1,0:T(8,128)(2,1)}) %all-gather.6.cloned.1.call-update) | async-done | bytes 11010064 | tf_op jit(solution)/shard_map/all_gather | solution.py:624
  229.3 10.5 %shard_map.169 = bf16[96,768]{1,0:T(8,128)(2,1)} custom-call(bf16[96,768]{1,0:T(8,128)(2,1)} %slice.176.q_ref, bf16[32,2,112,768]{3,2,1,0:T(8,128)(2,1)} %bitcast.149, f32[1,3584]{1,0:T(1,128)} %select_convert_fusion.live_ref), custom_call_target="tpu_custom_call" | custom-call | tf_op jit(solution)/shard_map/pallas_call | solution.py:129
  239.9 1.8 convolution_convert_fusion.1.part_ref
  241.7 11.0 %shard_map.170 = f32[24,3072]{1,0:T(8,128)S(1)} custom-call(bf16[96,3072]{1,0:T(8,128)(2,1)S(1)} %convolution_convert_fusion.1.part_ref), custom_call_target="tpu_custom_call" | custom-call | tf_op jit(solution)/shard_map/pallas_call | solution.py:89
  252.7 1.0 fusion.34
  253.7 0.1 convert_reduce_fusion.1
  253.9 0.2 fusion.25
  254.1 0.8 fusion.28.block_ref
  254.9 66.6 %shard_map.171 = bf16[8,4,24,3072]{3,2,1,0:T(8,128)(2,1)} custom-call(bf16[24,3072]{1,0:T(8,128)(2,1)} %fusion.28.block_ref), custom_call_target="tpu_custom_call" | custom-call | tf_op jit(solution)/shard_map/pallas_call | solution.py:321
  321.5 10.4 %convolution_convert_fusion = bf16[768,3072]{1,0:T(8,128)(2,1)} fusion(bf16[384,3072]{1,0:T(8,128)(2,1)S(1)} %copy-done, bf16[768,3072]{1,0:T(8,128)(2,1)} %bitcast.150, bf16[3072,384]{1,0:T(8,128)(2,1)} %param.25), kind=kOutput, calls=%fused_computation | convolution fusion | flops 3628892160 | bytes 14155776 | tf_op jit(solution)/shard_map/dot_general | solution.py:644
  331.9 65.3 %shard_map.172 = f32[24,3072]{1,0:T(8,128)} custom-call(bf16[8,4,24,3072]{3,2,1,0:T(8,128)(2,1)} %bitcast.151), custom_call_target="tpu_custom_call" | custom-call | tf_op jit(solution)/shard_map/pallas_call | solution.py:230
  397.3 1.1 convert_reduce_fusion.2
  398.4 0.2 fusion.29
  398.7 0.9 multiply_convert_fusion
  399.6 0.1 copy.21
  399.7 0.1 convert_element_type.85
  399.8 0.9 copy.22
  400.7 12.0 %shard_map.173 = bf16[3,3,6,2,8,16]{5,4,3,2,1,0:T(8,128)(2,1)} custom-call(bf16[6,2,8,16]{3,2,1,0:T(8,128)(2,1)} %bitcast.160), custom_call_target="tpu_custom_call" | custom-call | tf_op jit(solution)/shard_map/pallas_call | solution.py:427
  412.7 0.9 slice_bitcast_fusion.2
  413.7 0.1 maximum_maximum_fusion.1
  413.8 0.1 fusion.54
  414.0 0.2 convolution_add_fusion.7
  414.2 0.2 convolution_add_fusion.6
  414.3 0.2 convolution_add_fusion.5
  414.5 0.9 convolution_add_fusion.4
  415.4 0.2 convolution_add_fusion.3
  415.5 0.1 convolution_add_fusion.2
  415.7 0.2 convolution_add_fusion.1
  415.9 0.8 fusion.13
  (69 shorter events, 0.6 us)
Async XLA Ops:
  7.2 314.3 %copy-start = (bf16[384,3072]{1,0:T(8,128)(2,1)S(1)}, bf16[384,3072]{1,0:T(8,128)(2,1)}, u32[]{:S(2)}) copy-start(bf16[384,3072]{1,0:T(8,128)(2,1)} %param.26) | copy-start | bytes 7077892
  7.2 6.1 %copy-start.4 = (bf16[1,4,3072]{2,1,0:T(4,128)(2,1)S(1)}, bf16[1,4,3072]{2,1,0:T(4,128)(2,1)}, u32[]{:S(2)}) copy-start(bf16[1,4,3072]{2,1,0:T(4,128)(2,1)} %param.16) | copy-start | bytes 73732
  7.2 5.1 %copy-start.1 = (bf16[1,96,3072]{2,1,0:T(8,128)(2,1)S(1)}, bf16[1,96,3072]{2,1,0:T(8,128)(2,1)}, u32[]{:S(2)}) copy-start(bf16[1,96,3072]{2,1,0:T(8,128)(2,1)} %param.15) | copy-start | bytes 1769476
  7.2 5.4 %copy-start.7 = (f32[1,8,3072]{2,1,0:T(8,128)S(1)}, f32[1,8,3072]{2,1,0:T(8,128)}, u32[]{:S(2)}) copy-start(f32[1,8,3072]{2,1,0:T(8,128)} %param.20) | copy-start | bytes 294916
  7.2 97.2 %all-gather.4.cloned.1.call-start = ((), (), s32[]{:S(2)}) async-start(), calls=%async_computation | async-start | bytes 7299072 | tf_op jit(solution)/shard_map/all_gather | solution.py:611
  9.1 220.2 %all-gather.6.cloned.1.call-start = ((), (), s32[]{:S(2)}) async-start(), calls=%async_computation.1 | async-start | bytes 11354112 | tf_op jit(solution)/shard_map/all_gather | solution.py:624
  13.4 0.6 copy-start.8
  14.0 4.9 %copy-start.15 = (f32[64]{0:T(128)S(1)}, f32[64]{0:T(128)}, u32[]{:S(2)}) copy-start(f32[64]{0:T(128)} %param.21) | copy-start | bytes 772
  109.2 0.9 copy-start.2
  120.3 1.6 copy-start.18
  120.3 7.0 %copy-start.14 = (s32[2,2]{1,0:T(2,128)S(1)}, s32[2,2]{1,0:T(2,128)}, u32[]{:S(2)}) copy-start(s32[2,2]{1,0:T(2,128)} %param.18) | copy-start | bytes 52
  120.3 9.1 %copy-start.19 = (s32[2]{0:T(128)S(1)}, s32[2]{0:T(128)}, u32[]{:S(2)}) copy-start(s32[2]{0:T(128)} %param.17) | copy-start | bytes 28
  120.3 13.1 %copy-start.6 = (bf16[100,768]{1,0:T(8,128)(2,1)S(1)}, bf16[100,768]{1,0:T(8,128)(2,1)}, u32[]{:S(2)}) copy-start(bf16[100,768]{1,0:T(8,128)(2,1)} %get-tuple-element.5) | copy-start | bytes 460804
  123.3 116.6 %slice-start = ((s8[4718592]{0:T(1024)(128)(4,1)}), s8[524288]{0:T(1024)(128)(4,1)S(1)}, s32[]{:S(2)}) async-start(s8[4718592]{0:T(1024)(128)(4,1)} %bitcast.152), calls=%async_computation.2 | async-start | bytes 1048576
  229.3 10.5 %slice-start.1 = ((s8[4718592]{0:T(1024)(128)(4,1)}), s8[4194304]{0:T(1024)(128)(4,1)S(1)}, s32[]{:S(2)}) async-start(s8[4718592]{0:T(1024)(128)(4,1)} %bitcast.152), calls=%async_computation.3 | async-start | bytes 8388608
  239.9 12.8 %copy-start.11 = (f32[1,1,3072]{2,1,0:T(1,128)S(1)}, f32[1,1,3072]{2,1,0:T(1,128)}, u32[]{:S(2)}) copy-start(f32[1,1,3072]{2,1,0:T(1,128)} %get-tuple-element.30) | copy-start | bytes 36868
  241.7 12.4 %copy-start.9 = (f32[1,1,3072]{2,1,0:T(1,128)S(1)}, f32[1,1,3072]{2,1,0:T(1,128)}, u32[]{:S(2)}) copy-start(f32[1,1,3072]{2,1,0:T(1,128)} %get-tuple-element.26) | copy-start | bytes 36868
  331.9 65.4 %copy-start.10 = (f32[1,1,3072]{2,1,0:T(1,128)S(1)}, f32[1,1,3072]{2,1,0:T(1,128)}, u32[]{:S(2)}) copy-start(f32[1,1,3072]{2,1,0:T(1,128)} %get-tuple-element.27) | copy-start | bytes 36868
  331.9 66.8 %copy-start.12 = (f32[1,1,3072]{2,1,0:T(1,128)S(1)}, f32[1,1,3072]{2,1,0:T(1,128)}, u32[]{:S(2)}) copy-start(f32[1,1,3072]{2,1,0:T(1,128)} %get-tuple-element.24) | copy-start | bytes 36868
  331.9 66.8 %copy-start.13 = (f32[1,1,3072]{2,1,0:T(1,128)S(1)}, f32[1,1,3072]{2,1,0:T(1,128)}, u32[]{:S(2)}) copy-start(f32[1,1,3072]{2,1,0:T(1,128)} %get-tuple-element.31) | copy-start | bytes 36868
  331.9 66.8 %copy-start.16 = (bf16[3072,64]{0,1:T(8,128)(2,1)S(1)}, bf16[3072,64]{0,1:T(8,128)(2,1)}, u32[]{:S(2)}) copy-start(bf16[3072,64]{0,1:T(8,128)(2,1)} %param.27) | copy-start | bytes 1179652
  331.9 66.8 %copy-start.17 = (f32[1,24,64]{2,1,0:T(8,128)S(1)}, f32[1,24,64]{2,1,0:T(8,128)}, u32[]{:S(2)}) copy-start(f32[1,24,64]{2,1,0:T(8,128)} %param.28) | copy-start | bytes 18436
  398.4 15.6 %copy-start.3 = (bf16[24,3072]{1,0:T(8,128)(2,1)}, bf16[24,3072]{1,0:T(8,128)(2,1)S(1)}, u32[]{:S(2)}) copy-start(bf16[24,3072]{1,0:T(8,128)(2,1)S(1)} %get-tuple-element.12) | copy-start | bytes 442372
  398.4 15.4 %copy-start.5 = (bf16[3,3,16,512]{3,2,1,0:T(8,128)(2,1)S(1)}, bf16[3,3,16,512]{3,2,1,0:T(8,128)(2,1)}, u32[]{:S(2)}) copy-start(bf16[3,3,16,512]{3,2,1,0:T(8,128)(2,1)} %param.29) | copy-start | bytes 442372
Sparse Core Ops, SparseCore 0:
  10.6 93.7 all-gather.3
  120.4 108.8 all-gather.5

commit v15 on v14

--- a/solution.py
+++ b/solution.py
@@ -89,7 +89,7 @@
     return pl.pallas_call(
         functools.partial(scatter_sum_kernel, axis, count, rows),
         out_shape=jax.ShapeDtypeStruct((rows, width), jnp.float32),
-        in_specs=[pl.BlockSpec(memory_space=pl.ANY)],
+        in_specs=[pl.BlockSpec(memory_space=pltpu.VMEM)],
         out_specs=pl.BlockSpec(memory_space=pltpu.VMEM),
         scratch_shapes=[
             pltpu.VMEM((count, rows, width), part.dtype),

time: 424 us -> 424 us (level)
  no operation moved by 1% of the time
where the time goes in v15:
time: 424 us; the launch traced here: 423 us
  Pallas kernels  177 us (42%)
  waiting for transfers between devices  176 us (42%)
  matrix products  20.7 us (5%)
  other arithmetic  19.9 us (5%)
  between operations  18.4 us (4%)
  local copies, waits for them, and re-layouts  11.6 us (3%)
    all_gather x1, waiting for transfers between devices, shards(): gathered = lax.all_gather(both[None], 'row', axis=0, tiled=True)  95.3 us
    all_gather x1, waiting for transfers between devices, shards(): gathered_half = lax.all_gather(own_half, 'row', axis=1, tiled=True)  80.9 us
    pallas_call x1, Pallas kernels, ring_gather(): pl.pallas_call(functools.partial(ring_gather_kernel, zs, xs), out_shape=j...  66.6 us
    pallas_call x1, Pallas kernels, ring_scatter_sum(): pl.pallas_call(functools.partial(ring_scatter_kernel, zs, xs), out_shape=...  65.3 us
    pallas_call x1, Pallas kernels, halo_extend(): pl.pallas_call(halo_kernel, out_shape=jax.ShapeDtypeStruct((3, 3) + tile....  12 us
    pallas_call x1, Pallas kernels, scatter_sum(): pl.pallas_call(functools.partial(scatter_sum_kernel, axis, count, rows),...  11 us
    pallas_call x1, Pallas kernels, attention(): pl.pallas_call(functools.partial(attention_kernel, scale), out_shape=jax....  10.5 us
    dot_general x1, matrix products, shards(): jnp.dot(hidden_units, w_down, preferred_element_type=jnp.float32)  10.4 us
  transfers between devices with their start and end apart: 2, of which 2 were waited for; matrix products, arithmetic and copies ran while one was open for 5% of the time, Pallas kernels for 1%

profile of v15, /device:TPU:2, one launch (start us, length us, event | category | flops | bytes accessed | tf_op | source)
XLA Modules:
  0.0 423.5 jit_solution(15884749188765805265)
XLA Ops:
  7.3 1.8 constant_dynamic-slice_fusion
  9.2 0.9 convert_reduce_fusion.3
  10.1 0.9 fusion.43
  11.0 1.2 convert_reduce_fusion
  12.3 0.3 multiply_reduce_fusion
  12.6 0.7 slice_add_fusion
  13.3 0.1 fusion.46
  13.4 0.3 add_convert_fusion
  13.7 0.3 copy-done.8
  14.0 0.9 pad_maximum_fusion.1.src_ref
  14.9 4.0 shard_map.166
  19.0 0.6 tile.4
  19.6 1.4 broadcast_in_dim_tile.6.q_gain_ref
  20.9 1.3 tile.5
  22.2 1.4 broadcast_in_dim_tile.7.k_gain_ref
  23.5 80.9 %all-gather.4.cloned.1.call-done = bf16[3,3072,384]{2,1,0:T(8,128)(2,1)} async-done(((bf16[3,96,384]{2,1,0:T(8,128)(2,1)}), bf16[3,3072,384]{2,1,0:T(8,128)(2,1)}) %all-gather.4.cloned.1.call-update) | async-done | bytes 7077904 | tf_op jit(solution)/shard_map/all_gather | solution.py:611
  104.4 4.8 %convolution_bitcast_fusion = f32[3,200,384]{2,1,0:T(8,128)S(1)} fusion(bf16[3,3072,384]{2,1,0:T(8,128)(2,1)} %all-gather.4.cloned.1.call-done, bf16[100,3072]{1,0:T(8,128)(2,1)} %shard_map.166, bf16[4,3072]{1,0:T(4,128)(2,1)} %copy-done.8, bf16[96,3072]{1,0:T(8,128)(2,1)S(1)} %add_convert_fusion), kind=kOutput, calls=%fused_computation.3 | convolution fusion | flops 1419264000 | bytes 9228288 | tf_op jit(solution)/shard_map/ld,cde->cle/dot_general | solution.py:615
  109.3 0.9 copy-done.2
  110.2 0.8 slice.222.src_ref
  111.0 3.7 shard_map.167
  114.7 1.2 slice_select_fusion.1
  116.0 1.0 pad_maximum_fusion.raw_ref
  117.0 3.3 shard_map.168
  120.3 1.1 convert_element_type.67
  121.5 0.3 reduce-window.9
  121.9 0.6 select_reduce_fusion.4
  123.2 0.1 slice_reduce_fusion
  123.4 1.3 select_reduce_fusion
  127.2 0.2 slice_reduce_fusion.2
  127.4 0.6 select_reduce_fusion.2
  128.7 0.7 and_convert_fusion
  129.4 0.6 select_reduce_fusion.5
  130.0 0.6 fusion.80
  130.7 2.7 select_convert_fusion.live_ref
  133.4 0.7 slice.176.q_ref
  134.0 95.3 %all-gather.6.cloned.1.call-done = bf16[64,112,768]{2,1,0:T(8,128)(2,1)} async-done(((bf16[2,112,768]{2,1,0:T(8,128)(2,1)}), bf16[64,112,768]{2,1,0:T(8,128)(2,1)}) %all-gather.6.cloned.1.call-update) | async-done | bytes 11010064 | tf_op jit(solution)/shard_map/all_gather | solution.py:624
  229.3 10.5 %shard_map.169 = bf16[96,768]{1,0:T(8,128)(2,1)} custom-call(bf16[96,768]{1,0:T(8,128)(2,1)} %slice.176.q_ref, bf16[32,2,112,768]{3,2,1,0:T(8,128)(2,1)} %bitcast.149, f32[1,3584]{1,0:T(1,128)} %select_convert_fusion.live_ref), custom_call_target="tpu_custom_call" | custom-call | tf_op jit(solution)/shard_map/pallas_call | solution.py:129
  239.9 1.8 convolution_convert_fusion.1.part_ref
  241.7 11.0 %shard_map.170 = f32[24,3072]{1,0:T(8,128)S(1)} custom-call(bf16[96,3072]{1,0:T(8,128)(2,1)S(1)} %convolution_convert_fusion.1.part_ref), custom_call_target="tpu_custom_call" | custom-call | tf_op jit(solution)/shard_map/pallas_call | solution.py:89
  252.7 1.0 fusion.34
  253.7 0.1 convert_reduce_fusion.1
  253.9 0.2 fusion.25
  254.1 0.8 fusion.28.block_ref
  254.9 66.6 %shard_map.171 = bf16[8,4,24,3072]{3,2,1,0:T(8,128)(2,1)} custom-call(bf16[24,3072]{1,0:T(8,128)(2,1)} %fusion.28.block_ref), custom_call_target="tpu_custom_call" | custom-call | tf_op jit(solution)/shard_map/pallas_call | solution.py:321
  321.5 10.4 %convolution_convert_fusion = bf16[768,3072]{1,0:T(8,128)(2,1)} fusion(bf16[384,3072]{1,0:T(8,128)(2,1)S(1)} %copy-done, bf16[768,3072]{1,0:T(8,128)(2,1)} %bitcast.150, bf16[3072,384]{1,0:T(8,128)(2,1)} %param.25), kind=kOutput, calls=%fused_computation | convolution fusion | flops 3628892160 | bytes 14155776 | tf_op jit(solution)/shard_map/dot_general | solution.py:644
  331.9 65.3 %shard_map.172 = f32[24,3072]{1,0:T(8,128)} custom-call(bf16[8,4,24,3072]{3,2,1,0:T(8,128)(2,1)} %bitcast.151), custom_call_target="tpu_custom_call" | custom-call | tf_op jit(solution)/shard_map/pallas_call | solution.py:230
  397.3 1.1 convert_reduce_fusion.2
  398.4 0.2 fusion.29
  398.7 0.9 multiply_convert_fusion
  399.6 0.1 copy.21
  399.7 0.1 convert_element_type.85
  399.8 0.9 copy.22
  400.7 12.0 %shard_map.173 = bf16[3,3,6,2,8,16]{5,4,3,2,1,0:T(8,128)(2,1)} custom-call(bf16[6,2,8,16]{3,2,1,0:T(8,128)(2,1)} %bitcast.160), custom_call_target="tpu_custom_call" | custom-call | tf_op jit(solution)/shard_map/pallas_call | solution.py:427
  412.7 0.9 slice_bitcast_fusion.2
  413.7 0.1 maximum_maximum_fusion.1
  413.8 0.1 fusion.54
  414.0 0.2 convolution_add_fusion.7
  414.2 0.2 convolution_add_fusion.6
  414.3 0.2 convolution_add_fusion.5
  414.5 0.9 convolution_add_fusion.4
  415.4 0.2 convolution_add_fusion.3
  415.5 0.1 convolution_add_fusion.2
  415.7 0.2 convolution_add_fusion.1
  415.9 0.8 fusion.13
  (69 shorter events, 0.6 us)
Async XLA Ops:
  7.2 314.3 %copy-start = (bf16[384,3072]{1,0:T(8,128)(2,1)S(1)}, bf16[384,3072]{1,0:T(8,128)(2,1)}, u32[]{:S(2)}) copy-start(bf16[384,3072]{1,0:T(8,128)(2,1)} %param.26) | copy-start | bytes 7077892
  7.2 6.1 %copy-start.4 = (bf16[1,4,3072]{2,1,0:T(4,128)(2,1)S(1)}, bf16[1,4,3072]{2,1,0:T(4,128)(2,1)}, u32[]{:S(2)}) copy-start(bf16[1,4,3072]{2,1,0:T(4,128)(2,1)} %param.16) | copy-start | bytes 73732
  7.2 5.1 %copy-start.1 = (bf16[1,96,3072]{2,1,0:T(8,128)(2,1)S(1)}, bf16[1,96,3072]{2,1,0:T(8,128)(2,1)}, u32[]{:S(2)}) copy-start(bf16[1,96,3072]{2,1,0:T(8,128)(2,1)} %param.15) | copy-start | bytes 1769476
  7.2 5.4 %copy-start.7 = (f32[1,8,3072]{2,1,0:T(8,128)S(1)}, f32[1,8,3072]{2,1,0:T(8,128)}, u32[]{:S(2)}) copy-start(f32[1,8,3072]{2,1,0:T(8,128)} %param.20) | copy-start | bytes 294916
  7.2 97.2 %all-gather.4.cloned.1.call-start = ((), (), s32[]{:S(2)}) async-start(), calls=%async_computation | async-start | bytes 7299072 | tf_op jit(solution)/shard_map/all_gather | solution.py:611
  9.1 220.2 %all-gather.6.cloned.1.call-start = ((), (), s32[]{:S(2)}) async-start(), calls=%async_computation.1 | async-start | bytes 11354112 | tf_op jit(solution)/shard_map/all_gather | solution.py:624
  13.4 0.6 copy-start.8
  14.0 4.9 %copy-start.15 = (f32[64]{0:T(128)S(1)}, f32[64]{0:T(128)}, u32[]{:S(2)}) copy-start(f32[64]{0:T(128)} %param.21) | copy-start | bytes 772
  109.2 0.9 copy-start.2
  120.3 1.6 copy-start.18
  120.3 7.0 %copy-start.14 = (s32[2,2]{1,0:T(2,128)S(1)}, s32[2,2]{1,0:T(2,128)}, u32[]{:S(2)}) copy-start(s32[2,2]{1,0:T(2,128)} %param.18) | copy-start | bytes 52
  120.3 9.1 %copy-start.19 = (s32[2]{0:T(128)S(1)}, s32[2]{0:T(128)}, u32[]{:S(2)}) copy-start(s32[2]{0:T(128)} %param.17) | copy-start | bytes 28
  120.3 13.1 %copy-start.6 = (bf16[100,768]{1,0:T(8,128)(2,1)S(1)}, bf16[100,768]{1,0:T(8,128)(2,1)}, u32[]{:S(2)}) copy-start(bf16[100,768]{1,0:T(8,128)(2,1)} %get-tuple-element.5) | copy-start | bytes 460804
  123.3 116.6 %slice-start = ((s8[4718592]{0:T(1024)(128)(4,1)}), s8[524288]{0:T(1024)(128)(4,1)S(1)}, s32[]{:S(2)}) async-start(s8[4718592]{0:T(1024)(128)(4,1)} %bitcast.152), calls=%async_computation.2 | async-start | bytes 1048576
  229.3 10.5 %slice-start.1 = ((s8[4718592]{0:T(1024)(128)(4,1)}), s8[4194304]{0:T(1024)(128)(4,1)S(1)}, s32[]{:S(2)}) async-start(s8[4718592]{0:T(1024)(128)(4,1)} %bitcast.152), calls=%async_computation.3 | async-start | bytes 8388608
  239.9 12.8 %copy-start.11 = (f32[1,1,3072]{2,1,0:T(1,128)S(1)}, f32[1,1,3072]{2,1,0:T(1,128)}, u32[]{:S(2)}) copy-start(f32[1,1,3072]{2,1,0:T(1,128)} %get-tuple-element.30) | copy-start | bytes 36868
  241.7 12.4 %copy-start.9 = (f32[1,1,3072]{2,1,0:T(1,128)S(1)}, f32[1,1,3072]{2,1,0:T(1,128)}, u32[]{:S(2)}) copy-start(f32[1,1,3072]{2,1,0:T(1,128)} %get-tuple-element.26) | copy-start | bytes 36868
  331.9 65.4 %copy-start.10 = (f32[1,1,3072]{2,1,0:T(1,128)S(1)}, f32[1,1,3072]{2,1,0:T(1,128)}, u32[]{:S(2)}) copy-start(f32[1,1,3072]{2,1,0:T(1,128)} %get-tuple-element.27) | copy-start | bytes 36868
  331.9 66.8 %copy-start.12 = (f32[1,1,3072]{2,1,0:T(1,128)S(1)}, f32[1,1,3072]{2,1,0:T(1,128)}, u32[]{:S(2)}) copy-start(f32[1,1,3072]{2,1,0:T(1,128)} %get-tuple-element.24) | copy-start | bytes 36868
  331.9 66.8 %copy-start.13 = (f32[1,1,3072]{2,1,0:T(1,128)S(1)}, f32[1,1,3072]{2,1,0:T(1,128)}, u32[]{:S(2)}) copy-start(f32[1,1,3072]{2,1,0:T(1,128)} %get-tuple-element.31) | copy-start | bytes 36868
  331.9 66.8 %copy-start.16 = (bf16[3072,64]{0,1:T(8,128)(2,1)S(1)}, bf16[3072,64]{0,1:T(8,128)(2,1)}, u32[]{:S(2)}) copy-start(bf16[3072,64]{0,1:T(8,128)(2,1)} %param.27) | copy-start | bytes 1179652
  331.9 66.8 %copy-start.17 = (f32[1,24,64]{2,1,0:T(8,128)S(1)}, f32[1,24,64]{2,1,0:T(8,128)}, u32[]{:S(2)}) copy-start(f32[1,24,64]{2,1,0:T(8,128)} %param.28) | copy-start | bytes 18436
  398.4 15.6 %copy-start.3 = (bf16[24,3072]{1,0:T(8,128)(2,1)}, bf16[24,3072]{1,0:T(8,128)(2,1)S(1)}, u32[]{:S(2)}) copy-start(bf16[24,3072]{1,0:T(8,128)(2,1)S(1)} %get-tuple-element.12) | copy-start | bytes 442372
  398.4 15.4 %copy-start.5 = (bf16[3,3,16,512]{3,2,1,0:T(8,128)(2,1)S(1)}, bf16[3,3,16,512]{3,2,1,0:T(8,128)(2,1)}, u32[]{:S(2)}) copy-start(bf16[3,3,16,512]{3,2,1,0:T(8,128)(2,1)} %param.29) | copy-start | bytes 442372
Sparse Core Ops, SparseCore 0:
  10.6 93.7 all-gather.3
  120.4 108.8 all-gather.5
